TPU v7x, 32 devices: a whole 2x2x4 slice. The times are simulated.
32 devices in a mesh: wide: 16 (over z, x, core), ctr: 2 (over y).
Axes of the slice: x: 2, y: 2, z: 4, core: 2. Of those that a mesh axis runs over, the one named last changes fastest.
Arguments:
- tens: bfloat16 [2048, 256, 128], P(('wide', 'ctr')), may hold values from -0.29882812 to 0.29882812
- coef: bfloat16 [120, 2048], P(None, 'wide'), may hold values from -0.5 to 0.5
- aux_of: int32 [2048, 1], P(('wide', 'ctr')), may hold values from 0 to 15; in each aligned block of 64 rows (0 to 63, 64 to 127, ...) at most 8 rows name the same one
- slot_of: int32 [2048], P(('wide', 'ctr')), may hold values from 0 to 7
- metric: bfloat16 [16, 256, 256], P('wide'), as said below
Outputs:
- exchange: float32 [120, 2048], P(None, ('wide', 'ctr'))
Inputs may be any that keep to these rules, and one draw needn't show every extreme that they name: `aux_of`: among the blocks of one device at most 8 name the same auxiliary block, and in every draw some device has exactly 8 that do. `metric`: each block is symmetric.
All inputs are finite; a program needn't handle non-finite values.
Results may differ from a plain program's by a relative error of at most 0.0011.
Values may be sent and summed in bfloat16 or wider, within the bound.
No kernel may reach another device: no remote copies, remote signals or barrier semaphores. Data moves between devices by JAX's collectives and lax.ppermute only.
A program may use at most 64 MiB of HBM per device.

v0:
```python
import jax
import jax.numpy as jnp
from jax import lax
from jax.sharding import PartitionSpec as P

OCC_DEV = 8


def body(tens, coef, aux_of, slot_of, metric):
    owners = lax.axis_size("wide")
    block_count = tens.shape[0]
    capacity = max(2, 2 * block_count // owners)
    total_slots = owners * capacity
    half_form = jnp.einsum("jm,bpm->bjp", coef, tens, preferred_element_type=jnp.float32).astype(
        jnp.bfloat16
    )
    target = aux_of[:, 0]
    series = jnp.arange(block_count)
    matches = target[:, None] == target[None, :]
    earlier = series[None, :] < series[:, None]
    ranking = jnp.sum(jnp.where(matches & earlier, 1, 0), axis=1)
    position = target * capacity + ranking
    selector = position[None, :] == jnp.arange(total_slots)[:, None]
    selector_bf = jnp.where(selector, 1.0, 0.0).astype(jnp.bfloat16)
    outgoing = jnp.einsum(
        "kb,bjp->kjp", selector_bf, half_form, preferred_element_type=jnp.float32
    ).astype(jnp.bfloat16)
    slot_tags = jnp.sum(jnp.where(selector, slot_of[None, :] + 1, 0), axis=1)
    received, tags_in = (
        lax.all_to_all(outgoing, "wide", split_axis=0, concat_axis=0, tiled=True),
        lax.all_to_all(slot_tags, "wide", split_axis=0, concat_axis=0, tiled=True),
    )
    slot_onehot = jnp.where(
        tags_in[None, :] == (jnp.arange(OCC_DEV) + 1)[:, None], 1.0, 0.0
    ).astype(jnp.bfloat16)
    fitted = jnp.einsum(
        "sk,kjp->sjp", slot_onehot, received, preferred_element_type=jnp.float32
    ).astype(jnp.bfloat16)
    weighted = jnp.einsum(
        "sjp,pq->sjq", fitted, metric[0], preferred_element_type=jnp.float32
    ).astype(jnp.bfloat16)
    answers = jnp.einsum(
        "sk,sjq->kjq", slot_onehot, weighted, preferred_element_type=jnp.float32
    ).astype(jnp.bfloat16)
    returned = lax.all_to_all(answers, "wide", split_axis=0, concat_axis=0, tiled=True)
    per_block = jnp.einsum(
        "kb,kjq->bjq", selector_bf, returned, preferred_element_type=jnp.float32
    ).astype(jnp.bfloat16)
    partial_value = jnp.einsum("bjq,bqm->jm", per_block, tens, preferred_element_type=jnp.float32)
    return lax.psum_scatter(partial_value, "ctr", scatter_dimension=1, tiled=True)


def solution(mesh):
    placed = (
        P(("wide", "ctr"), None, None),
        P(None, "wide"),
        P(("wide", "ctr"), None),
        P(("wide", "ctr")),
        P("wide", None, None),
    )
    return jax.shard_map(
        body, mesh=mesh, in_specs=placed, out_specs=P(None, ("wide", "ctr")), check_vma=False
    )
```

profile of v0, /device:TPU:0, one launch (start us, length us, event | category | flops | bytes accessed | tf_op | source)
XLA Modules:
  0.0 424.8 jit_solution(14362370959812156064)
XLA Ops:
  6.5 0.0 copy-start
  6.5 0.9 select_reduce_fusion.1
  7.4 0.7 multiply_add_fusion
  8.1 0.1 select_reduce_fusion
  8.2 0.7 all_to_all.12
  8.9 7.4 %all-to-all-start = ((s32[16,8,1]{1,2,0:T(1,128)}), s32[16,8,1]{1,2,0:T(1,128)S(1)}, u32[]{:S(2)}, u32[]{:S(2)}) async-start(s32[16,8,1]{1,2,0:T(1,128)} %bitcast.2), calls=%async_computation | async-start | bytes 16384 | tf_op jit(solution)/shard_map/all_to_all | solution.py:31
  16.3 4.9 %convert_bitcast_fusion = bf16[64,120,256]{2,1,0:T(8,128)(2,1)S(1)} fusion(bf16[64,256,128]{2,1,0:T(8,128)(2,1)} %param.5, bf16[120,128]{1,0:T(8,128)(2,1)} %param.6), kind=kOutput, calls=%fused_computation.9 | convolution fusion | flops 505282560 | bytes 8157184 | tf_op jit(solution)/shard_map/jm,bpm->bjp/dot_general | solution.py:14
  21.2 2.3 convolution_convert_fusion.1
  23.5 7.8 %copy.26 = bf16[128,120,256]{2,1,0:T(8,128)(2,1)} copy(bf16[128,120,256]{2,0,1:T(8,128)(2,1)S(1)} %convolution_convert_fusion.1) | data formatting | bytes 15728640 | tf_op jit(solution)/shard_map/convert_element_type | solution.py:27
  31.3 0.0 all-to-all-done
  31.3 6.1 %all-to-all-start.1 = ((bf16[128,120,256]{2,1,0:T(8,128)(2,1)}), bf16[128,120,256]{2,1,0:T(8,128)(2,1)}, u32[]{:S(2)}, u32[]{:S(2)}) async-start(bf16[128,120,256]{2,1,0:T(8,128)(2,1)} %copy.26), calls=%async_computation.1 | async-start | bytes 15728640 | tf_op jit(solution)/shard_map/all_to_all | solution.py:30
  37.4 0.2 reduce-scatter.2.cloned.1.call-start
  37.6 0.5 broadcast.18
  38.1 0.7 reduce.3
  38.8 0.1 eq.47
  38.9 140.1 %all-to-all-done.1 = bf16[128,120,256]{2,1,0:T(8,128)(2,1)} async-done(((bf16[128,120,256]{2,1,0:T(8,128)(2,1)}), bf16[128,120,256]{2,1,0:T(8,128)(2,1)}, u32[]{:S(2)}, u32[]{:S(2)}) %all-to-all-start.1) | async-done | bytes 7864352 | tf_op jit(solution)/shard_map/all_to_all | solution.py:30
  178.9 4.6 %fusion.10 = bf16[8,120,256]{2,0,1:T(8,128)(2,1)S(1)} fusion(bf16[128,120,256]{2,1,0:T(8,128)(2,1)} %all-to-all-done.1, s32[128]{0:T(128)S(1)} %eq.47, s32[8]{0:T(128)S(1)} %iota_add_fusion), kind=kOutput, calls=%fused_computation.12 | convolution fusion | flops 63163392 | bytes 8356384 | tf_op jit(solution)/shard_map/sk,kjp->sjp/dot_general | solution.py:36
  183.5 0.0 copy-done
  183.5 0.3 convolution_convert_fusion.2
  183.8 2.3 convolution_convert_fusion
  186.1 7.7 %copy.30 = bf16[128,120,256]{2,1,0:T(8,128)(2,1)} copy(bf16[128,120,256]{2,0,1:T(8,128)(2,1)S(1)} %convolution_convert_fusion) | data formatting | bytes 15728640 | tf_op jit(solution)/shard_map/convert_element_type | solution.py:44
  193.8 205.3 %all_to_all.19 = bf16[128,120,256]{2,1,0:T(8,128)(2,1)S(1)} all-to-all(bf16[128,120,256]{2,1,0:T(8,128)(2,1)} %copy.30), channel_id=1, replica_groups=mesh['wide'=16,'ctr'=2] {'wide'}, dimensions={0} | all-to-all | bytes 15728640 | tf_op jit(solution)/shard_map/all_to_all | solution.py:45
  399.1 0.0 copy-start.1
  399.1 1.5 fusion.7
  400.7 0.6 copy-done.1
  401.3 5.5 %fusion.13 = f32[120,128]{0,1:T(8,128)} fusion(bf16[64,256,128]{2,1,0:T(8,128)(2,1)S(1)} %copy-done.1, bf16[64,120,256]{2,0,1:T(8,128)(2,1)S(1)} %fusion.7), kind=kOutput, calls=%fused_computation.13 | convolution fusion | flops 503316480 | bytes 8187904 | tf_op jit(solution)/shard_map/bjq,bqm->jm/dot_general | solution.py:49
  406.9 0.0 reduce-scatter.2.cloned.1.call-update
  406.9 11.0 %reduce-scatter.2.cloned.1.call-done = f32[120,64]{0,1:T(8,128)} async-done(((f32[120,128]{0,1:T(8,128)}), f32[120,64]{0,1:T(8,128)}) %reduce-scatter.2.cloned.1.call-update) | async-done | bytes 30736 | tf_op jit(solution)/shard_map/reduce_scatter | solution.py:50
  (1 shorter events, 0.0 us)
Async XLA Ops:
  6.5 177.0 %copy-start = (bf16[1,256,256]{2,1,0:T(8,128)(2,1)S(1)}, bf16[1,256,256]{2,1,0:T(8,128)(2,1)}, u32[]{:S(2)}) copy-start(bf16[1,256,256]{2,1,0:T(8,128)(2,1)} %param.9) | copy-start | bytes 393220
  8.9 22.4 %all-to-all-start = ((s32[16,8,1]{1,2,0:T(1,128)}), s32[16,8,1]{1,2,0:T(1,128)S(1)}, u32[]{:S(2)}, u32[]{:S(2)}) async-start(s32[16,8,1]{1,2,0:T(1,128)} %bitcast.2), calls=%async_computation | async-start | bytes 16384 | tf_op jit(solution)/shard_map/all_to_all | solution.py:31
  31.3 147.6 %all-to-all-start.1 = ((bf16[128,120,256]{2,1,0:T(8,128)(2,1)}), bf16[128,120,256]{2,1,0:T(8,128)(2,1)}, u32[]{:S(2)}, u32[]{:S(2)}) async-start(bf16[128,120,256]{2,1,0:T(8,128)(2,1)} %copy.26), calls=%async_computation.1 | async-start | bytes 15728640 | tf_op jit(solution)/shard_map/all_to_all | solution.py:30
  37.4 380.6 %reduce-scatter.2.cloned.1.call-start = ((), (), s32[]{:S(2)}) async-start(), calls=%async_computation.4 | async-start | bytes 98304 | tf_op jit(solution)/shard_map/reduce_scatter | solution.py:50
  399.1 2.2 copy-start.1
Sparse Core Ops, SparseCore 0:
  407.0 10.8 reduce-scatter.1
where the time goes:
time: 425 us
  blocking collectives  205 us (48%)
  waiting for transfers between devices  151 us (36%)
  matrix products  21.5 us (5%)
  local copies, waits for them, and re-layouts  17.4 us (4%)
  starting transfers between devices  13.6 us (3%)
  between operations  13.5 us (3%)
    all_to_all x1, blocking collectives, body(): lax.all_to_all(answers, 'wide', split_axis=0, concat_axis=0, tiled=True)  205 us
    all_to_all x1, waiting for transfers between devices, body(): lax.all_to_all(outgoing, 'wide', split_axis=0, concat_axis=0, tiled=True)  140 us
    reduce_scatter x1, waiting for transfers between devices, body(): lax.psum_scatter(partial_value, 'ctr', scatter_dimension=1, tiled=True)  11 us
  transfers between devices with their start and end apart: 3, of which 2 were waited for; matrix products, arithmetic and copies ran while one was open for 4% of the time, Pallas kernels for 0%

commit v1 on v0

--- a/solution.py
+++ b/solution.py
@@ -1,12 +1,201 @@
+import functools
+
 import jax
 import jax.numpy as jnp
 from jax import lax
+from jax.experimental import pallas as pl
+from jax.experimental.pallas import tpu as pltpu
 from jax.sharding import PartitionSpec as P
 
 OCC_DEV = 8
-
-
-def body(tens, coef, aux_of, slot_of, metric):
+GROUP = 4
+MIB = 1 << 20
+
+
+def ring_place(chip, chips):
+    return jnp.where(chip % 2 == 0, chip // 2, chips - 1 - chip // 2)
+
+
+def ring_pairs(chips, step):
+    order = list(range(0, chips, 2)) + list(range(1, chips, 2))[::-1]
+    return [
+        (2 * order[k] + core, 2 * order[(k + step) % chips] + core)
+        for k in range(chips)
+        for core in range(2)
+    ]
+
+
+def sum_cells_kernel(order, cell, tens, coef, out, total):
+    out[...] = jnp.zeros_like(out)
+    block_count = tens.shape[0]
+
+    def group(g, carry):
+        halves, cells, firsts = [], [], []
+        for u in range(GROUP):
+            k = g * GROUP + u
+            b = order[k]
+            here = cell[b]
+            before = cell[order[jnp.maximum(k - 1, 0)]]
+            half = lax.dot_general(
+                coef[...], tens[b], (((1,), (1,)), ((), ())), preferred_element_type=jnp.float32
+            )
+            halves.append(half.astype(jnp.bfloat16).astype(jnp.float32))
+            cells.append(here)
+            firsts.append(jnp.logical_or(k == 0, before != here))
+        for half, here, first in zip(halves, cells, firsts):
+            keep = jnp.where(first, 0.0, 1.0)
+            value = total[...] * keep + half
+            total[...] = value
+            out[here] = value.astype(jnp.bfloat16)
+        return carry
+
+    total[...] = jnp.zeros_like(total)
+    lax.fori_loop(0, block_count // GROUP, group, 0)
+
+
+def sum_cells(order, cell, tens, coef, cells):
+    rows, width = coef.shape[0], tens.shape[1]
+    return pl.pallas_call(
+        sum_cells_kernel,
+        out_shape=jax.ShapeDtypeStruct((cells, rows, width), jnp.bfloat16),
+        grid_spec=pltpu.PrefetchScalarGridSpec(
+            num_scalar_prefetch=2,
+            grid=(1,),
+            in_specs=[
+                pl.BlockSpec(tens.shape, lambda i, *_: (0, 0, 0), pipeline_mode=pl.Buffered(1)),
+                pl.BlockSpec(coef.shape, lambda i, *_: (0, 0), pipeline_mode=pl.Buffered(1)),
+            ],
+            out_specs=pl.BlockSpec(
+                (cells, rows, width), lambda i, *_: (0, 0, 0), pipeline_mode=pl.Buffered(1)
+            ),
+            scratch_shapes=[pltpu.VMEM((rows, width), jnp.float32)],
+        ),
+        compiler_params=pltpu.CompilerParams(vmem_limit_bytes=24 * MIB),
+        name="sum_cells",
+    )(order, cell, tens, coef)
+
+
+def apply_cells_kernel(cell, weighted, tens, out):
+    block_count = tens.shape[0]
+
+    def group(g, total):
+        for u in range(GROUP):
+            b = g * GROUP + u
+            total = total + jnp.dot(
+                weighted[cell[b]], tens[b], preferred_element_type=jnp.float32
+            )
+        return total
+
+    out[...] = lax.fori_loop(0, block_count // GROUP, group, jnp.zeros(out.shape, jnp.float32))
+
+
+def apply_cells(cell, weighted, tens):
+    rows, width = weighted.shape[1], tens.shape[2]
+    return pl.pallas_call(
+        apply_cells_kernel,
+        out_shape=jax.ShapeDtypeStruct((rows, width), jnp.float32),
+        grid_spec=pltpu.PrefetchScalarGridSpec(
+            num_scalar_prefetch=1,
+            grid=(1,),
+            in_specs=[
+                pl.BlockSpec(weighted.shape, lambda i, *_: (0, 0, 0), pipeline_mode=pl.Buffered(1)),
+                pl.BlockSpec(tens.shape, lambda i, *_: (0, 0, 0), pipeline_mode=pl.Buffered(1)),
+            ],
+            out_specs=pl.BlockSpec((rows, width), lambda i, *_: (0, 0)),
+        ),
+        compiler_params=pltpu.CompilerParams(vmem_limit_bytes=24 * MIB),
+        name="apply_cells",
+    )(cell, weighted, tens)
+
+
+def sum_over_ctr(partial_value):
+    if lax.axis_size("ctr") != 2:
+        return lax.psum_scatter(partial_value, "ctr", scatter_dimension=1, tiled=True)
+    width = partial_value.shape[1] // 2
+    low, high = partial_value[:, :width], partial_value[:, width:]
+    first = lax.axis_index("ctr") == 0
+    mine, other = jnp.where(first, low, high), jnp.where(first, high, low)
+    return mine + lax.ppermute(other, "ctr", [(0, 1), (1, 0)])
+
+
+def cells_body(tens, coef, aux_of, slot_of, metric):
+    owners = lax.axis_size("wide")
+    chips = owners // 2
+    far = chips // 2
+    slots = OCC_DEV
+    block_count = tens.shape[0]
+    me = lax.axis_index("wide")
+    core, place = me % 2, ring_place(me // 2, chips)
+    forward = functools.partial(lax.ppermute, axis_name="wide", perm=ring_pairs(chips, 1))
+    backward = functools.partial(lax.ppermute, axis_name="wide", perm=ring_pairs(chips, -1))
+    across = functools.partial(
+        lax.ppermute, axis_name="wide", perm=[(k, k ^ 1) for k in range(owners)]
+    )
+
+    target = aux_of[:, 0]
+    ahead = (ring_place(target // 2, chips) - place) % chips
+    other_core = jnp.where(target % 2 == core, 0, 1)
+    cell = (other_core * chips + ahead) * slots + slot_of
+    series = jnp.arange(block_count)
+    key = cell * block_count + series
+    rank = jnp.sum(jnp.where(key[None, :] < key[:, None], 1, 0), axis=1)
+    order = jnp.sum(jnp.where(rank[None, :] == series[:, None], series[None, :], 0), axis=1)
+
+    sums = sum_cells(order, cell, tens, coef, 2 * chips * slots)
+    halves = [slice(0, slots // 2), slice(slots // 2, slots)]
+
+    def at(kind, ahead):
+        start = (kind * chips + ahead) * slots
+        return sums[start : start + slots]
+
+    local = {}
+    for step in range(far, -1, -1):
+        for r in sorted({step, (chips - step) % chips}):
+            got = across(at(1, r))
+            local[r] = [
+                at(0, r)[h].astype(jnp.float32) + got[h].astype(jnp.float32) for h in halves
+            ]
+
+    def add(value, held):
+        return held if value is None else value.astype(jnp.float32) + held
+
+    up, down = [None, None], [None, None]
+    for step in range(far, 0, -1):
+        for h in range(2):
+            if step < far or h == 0:
+                up[h] = forward(add(up[h], local[step][h]).astype(jnp.bfloat16))
+            if step < far or h == 1:
+                down[h] = backward(add(down[h], local[chips - step][h]).astype(jnp.bfloat16))
+
+    own = []
+    for h in range(2):
+        fitted = add(down[h], add(up[h], local[0][h])).astype(jnp.bfloat16)
+        own.append(
+            jnp.einsum(
+                "sjp,pq->sjq", fitted, metric[0], preferred_element_type=jnp.float32
+            ).astype(jnp.bfloat16)
+        )
+
+    held = {0: list(own)}
+    up, down = list(own), list(own)
+    for step in range(1, far + 1):
+        for r in (chips - step, step):
+            held.setdefault(r, [None, None])
+        for h in range(2):
+            if step < far or h == 0:
+                up[h] = forward(up[h])
+                held[chips - step][h] = up[h]
+            if step < far or h == 1:
+                down[h] = backward(down[h])
+                held[step][h] = down[h]
+
+    pieces = [jnp.concatenate(held[r]) for r in range(chips)]
+    others = [across(piece) for piece in pieces]
+    partial_value = apply_cells(cell, jnp.concatenate(pieces + others), tens)
+    return sum_over_ctr(partial_value)
+
+
+def slots_body(tens, coef, aux_of, slot_of, metric):
     owners = lax.axis_size("wide")
     block_count = tens.shape[0]
     capacity = max(2, 2 * block_count // owners)
@@ -47,7 +236,13 @@
         "kb,kjq->bjq", selector_bf, returned, preferred_element_type=jnp.float32
     ).astype(jnp.bfloat16)
     partial_value = jnp.einsum("bjq,bqm->jm", per_block, tens, preferred_element_type=jnp.float32)
-    return lax.psum_scatter(partial_value, "ctr", scatter_dimension=1, tiled=True)
+    return sum_over_ctr(partial_value)
+
+
+def body(tens, coef, aux_of, slot_of, metric):
+    owners, block_count = lax.axis_size("wide"), tens.shape[0]
+    dense = owners * OCC_DEV <= 2 * block_count and owners % 4 == 0
+    return (cells_body if dense else slots_body)(tens, coef, aux_of, slot_of, metric)
 
 
 def solution(mesh):

time: 425 us -> 129 us (0.30)
  blocking collectives: 205 us -> 0 us
  waiting for transfers between devices: 151 us -> 55.8 us
  starting transfers between devices: 13.6 us -> 35.4 us
  matrix products: 21.5 us -> 1.95 us
  between operations: 13.5 us -> 0.18 us
  Pallas kernels: 0 us -> 8.92 us
  local copies, waits for them, and re-layouts: 17.4 us -> 23.8 us
    all_to_all x1 -> x0, blocking collectives: 205 us -> none  [body(): lax.all_to_all(answers, 'wide', split_axis=0, concat_axis=0, tiled=True)]
    all_to_all x2 -> x0, waiting for transfers between devices: 140 us -> none  [the longest x1 140 us: body(): lax.all_to_all(outgoing, 'wide', split_axis=0, concat_axis=0, tiled=True)]
    ppermute x0 -> x45, waiting for transfers between devices: none -> 55.8 us  [the longest x7 23.3 us: cells_body(): backward(add(down[h], local[chips - step][h]).astype(jnp.bfloat16))]
    ppermute x0 -> x45, starting transfers between devices: none -> 35.4 us  [the longest x7 11.7 us: cells_body(): up[h] = forward(up[h])]
    unnamed x4 -> x31, local copies, waits for them, and re-layouts: 0.65 us -> 22 us
    dot_general x7 -> x2, matrix products: 21.5 us -> 1.95 us  [cells_body(): jnp.einsum('sjp,pq->sjq', fitted, metric[0], preferred_element_type=jnp.f...]
    convert_element_type x2 -> x0, local copies, waits for them, and re-layouts: 15.5 us -> none  [the longest x1 7.78 us: body(): outgoing = jnp.einsum('kb,bjp->kjp', selector_bf, half_form, preferred_el...]
    all_to_all x2 -> x0, starting transfers between devices: 13.4 us -> none  [the longest x1 7.36 us: body(): lax.all_to_all(slot_tags, 'wide', split_axis=0, concat_axis=0, tiled=True)]
  transfers between devices with their start and end apart: 3 -> 45, of which waited for: 2 -> 23; matrix products, arithmetic and copies ran while one was open for 4% -> 14% of each run, Pallas kernels for 0% -> 0%
where the time goes in v1:
time: 129 us
  waiting for transfers between devices  55.8 us (43%)
  starting transfers between devices  35.4 us (27%)
  local copies, waits for them, and re-layouts  23.8 us (18%)
  Pallas kernels  8.92 us (7%)
  other arithmetic  2.81 us (2%)
  matrix products  1.95 us (2%)
    ppermute x7, waiting for transfers between devices, cells_body(): backward(add(down[h], local[chips - step][h]).astype(jnp.bfloat16))  23.3 us
    unnamed x31, local copies, waits for them, and re-layouts  22 us
    ppermute x7, waiting for transfers between devices, cells_body(): down[h] = backward(down[h])  13.3 us
    ppermute x7, starting transfers between devices, cells_body(): up[h] = forward(up[h])  11.7 us
    ppermute x7, starting transfers between devices, cells_body(): backward(add(down[h], local[chips - step][h]).astype(jnp.bfloat16))  9.96 us
    ppermute x7, waiting for transfers between devices, cells_body(): up[h] = forward(add(up[h], local[step][h]).astype(jnp.bfloat16))  9.17 us
    ppermute x7, waiting for transfers between devices, cells_body(): up[h] = forward(up[h])  6.11 us
    ppermute x7, starting transfers between devices, cells_body(): up[h] = forward(add(up[h], local[step][h]).astype(jnp.bfloat16))  5.41 us
  transfers between devices with their start and end apart: 45, of which 23 were waited for; matrix products, arithmetic and copies ran while one was open for 14% of the time, Pallas kernels for 0%

profile of v1, /device:TPU:0, one launch (start us, length us, event | category | flops | bytes accessed | tf_op | source)
XLA Modules:
  0.0 128.8 jit_solution(14660892286677711451)
XLA Ops:
  1.1 2.2 %copy-done.1 = bf16[64,256,128]{2,1,0:T(8,128)(2,1)S(1)} copy-done((bf16[64,256,128]{2,1,0:T(8,128)(2,1)S(1)}, bf16[64,256,128]{2,1,0:T(8,128)(2,1)}, u32[]{:S(2)}) %copy-start.1) | copy-done | bytes 4194328
  4.0 4.9 %sum_cells.1 = bf16[128,120,256]{2,1,0:T(8,128)(2,1)S(1)} custom-call(s32[64]{0:T(128)S(1)} %select_reduce_fusion.order, s32[64]{0:T(128)S(1)} %get-tuple-element.6.cell, bf16[64,256,128]{2,1,0:T(8,128)(2,1)S(1)} %copy-done.1, bf16[120,128]{1,0:T(8,128)(2,1)S(1)} %copy-done.4), custom_call_target="tpu_custom_call" | custom-call | tf_op jit(solution)/shard_map/sum_cells/pallas_call | solution.py:58
  10.2 1.0 collective-permute-done.6
  11.3 2.9 %collective-permute-start.15 = (bf16[4,120,256]{2,1,0:T(8,128)(2,1)S(1)}, bf16[4,120,256]{2,1,0:T(8,128)(2,1)S(1)}, u32[]{:S(2)}, u32[]{:S(2)}) collective-permute-start(bf16[4,120,256]{2,1,0:T(8,128)(2,1)S(1)} %get-tuple-element.13), channel_id=1, source_target_pairs={{0,4},{2,6},{8,0},{10,2},{16,8},{18,10},{24,16},{26,18},{28,24},{3... | collective-permute-start | bytes 737288 | tf_op jit(solution)/shard_map/ppermute | solution.py:168
  14.9 5.7 %collective-permute-done.15 = bf16[4,120,256]{2,1,0:T(8,128)(2,1)S(1)} collective-permute-done((bf16[4,120,256]{2,1,0:T(8,128)(2,1)S(1)}, bf16[4,120,256]{2,1,0:T(8,128)(2,1)S(1)}, u32[]{:S(2)}, u32[]{:S(2)}) %collective-permute-start.15) | collective-permute-done | bytes 245792 | tf_op jit(solution)/shard_map/ppermute | solution.py:168
  20.6 1.4 %collective-permute-done.7 = bf16[4,120,256]{2,1,0:T(8,128)(2,1)S(1)} collective-permute-done((bf16[4,120,256]{2,1,0:T(8,128)(2,1)S(1)}, bf16[4,120,256]{2,1,0:T(8,128)(2,1)S(1)}, u32[]{:S(2)}, u32[]{:S(2)}) %collective-permute-start.7) | collective-permute-done | bytes 245792 | tf_op jit(solution)/shard_map/ppermute | solution.py:166
  22.3 1.6 %collective-permute-start.16 = (bf16[4,120,256]{2,1,0:T(8,128)(2,1)S(1)}, bf16[4,120,256]{2,1,0:T(8,128)(2,1)S(1)}, u32[]{:S(2)}, u32[]{:S(2)}) collective-permute-start(bf16[4,120,256]{2,1,0:T(8,128)(2,1)S(1)} %get-tuple-element.11), channel_id=1, source_target_pairs={{0,4},{2,6},{8,0},{10,2},{16,8},{18,10},{24,16},{26,18},{28,24},{3... | collective-permute-start | bytes 737288 | tf_op jit(solution)/shard_map/ppermute | solution.py:168
  23.9 1.6 %collective-permute-start.1 = (bf16[4,120,256]{2,1,0:T(8,128)(2,1)S(1)}, bf16[4,120,256]{2,1,0:T(8,128)(2,1)S(1)}, u32[]{:S(2)}, u32[]{:S(2)}) collective-permute-start(bf16[4,120,256]{2,1,0:T(8,128)(2,1)S(1)} %get-tuple-element.12), channel_id=1, source_target_pairs={{0,4},{2,6},{8,0},{10,2},{16,8},{18,10},{24,16},{26,18},{28,24},{3... | collective-permute-start | bytes 737288 | tf_op jit(solution)/shard_map/ppermute | solution.py:168
  26.4 4.8 %collective-permute-done.16 = bf16[4,120,256]{2,1,0:T(8,128)(2,1)S(1)} collective-permute-done((bf16[4,120,256]{2,1,0:T(8,128)(2,1)S(1)}, bf16[4,120,256]{2,1,0:T(8,128)(2,1)S(1)}, u32[]{:S(2)}, u32[]{:S(2)}) %collective-permute-start.16) | collective-permute-done | bytes 245792 | tf_op jit(solution)/shard_map/ppermute | solution.py:168
  31.3 3.2 %collective-permute-done.1 = bf16[4,120,256]{2,1,0:T(8,128)(2,1)S(1)} collective-permute-done((bf16[4,120,256]{2,1,0:T(8,128)(2,1)S(1)}, bf16[4,120,256]{2,1,0:T(8,128)(2,1)S(1)}, u32[]{:S(2)}, u32[]{:S(2)}) %collective-permute-start.1) | collective-permute-done | bytes 245792 | tf_op jit(solution)/shard_map/ppermute | solution.py:168
  34.5 2.6 %collective-permute-done.19 = bf16[4,120,256]{2,1,0:T(8,128)(2,1)S(1)} collective-permute-done((bf16[4,120,256]{2,1,0:T(8,128)(2,1)S(1)}, bf16[4,120,256]{2,1,0:T(8,128)(2,1)S(1)}, u32[]{:S(2)}, u32[]{:S(2)}) %collective-permute-start.19) | collective-permute-done | bytes 245792 | tf_op jit(solution)/shard_map/ppermute | solution.py:166
  37.5 1.6 %collective-permute-start.17 = (bf16[4,120,256]{2,1,0:T(8,128)(2,1)S(1)}, bf16[4,120,256]{2,1,0:T(8,128)(2,1)S(1)}, u32[]{:S(2)}, u32[]{:S(2)}) collective-permute-start(bf16[4,120,256]{2,1,0:T(8,128)(2,1)S(1)} %get-tuple-element.9), channel_id=1, source_target_pairs={{0,4},{2,6},{8,0},{10,2},{16,8},{18,10},{24,16},{26,18},{28,24},{3... | collective-permute-start | bytes 737288 | tf_op jit(solution)/shard_map/ppermute | solution.py:168
  39.7 1.4 %collective-permute-start.11 = (bf16[4,120,256]{2,1,0:T(8,128)(2,1)S(1)}, bf16[4,120,256]{2,1,0:T(8,128)(2,1)S(1)}, u32[]{:S(2)}, u32[]{:S(2)}) collective-permute-start(bf16[4,120,256]{2,1,0:T(8,128)(2,1)S(1)} %get-tuple-element.23), channel_id=1, source_target_pairs={{0,8},{2,10},{8,16},{10,18},{16,24},{18,26},{24,28},{26,30},{28,20... | collective-permute-start | bytes 737288 | tf_op jit(solution)/shard_map/ppermute | solution.py:166
  41.6 3.9 %collective-permute-done.17 = bf16[4,120,256]{2,1,0:T(8,128)(2,1)S(1)} collective-permute-done((bf16[4,120,256]{2,1,0:T(8,128)(2,1)S(1)}, bf16[4,120,256]{2,1,0:T(8,128)(2,1)S(1)}, u32[]{:S(2)}, u32[]{:S(2)}) %collective-permute-start.17) | collective-permute-done | bytes 245792 | tf_op jit(solution)/shard_map/ppermute | solution.py:168
  45.5 2.6 %collective-permute-done.3 = bf16[4,120,256]{2,1,0:T(8,128)(2,1)S(1)} collective-permute-done((bf16[4,120,256]{2,1,0:T(8,128)(2,1)S(1)}, bf16[4,120,256]{2,1,0:T(8,128)(2,1)S(1)}, u32[]{:S(2)}, u32[]{:S(2)}) %collective-permute-start.3) | collective-permute-done | bytes 245792 | tf_op jit(solution)/shard_map/ppermute | solution.py:168
  48.2 2.0 %collective-permute-done.20 = bf16[4,120,256]{2,1,0:T(8,128)(2,1)S(1)} collective-permute-done((bf16[4,120,256]{2,1,0:T(8,128)(2,1)S(1)}, bf16[4,120,256]{2,1,0:T(8,128)(2,1)S(1)}, u32[]{:S(2)}, u32[]{:S(2)}) %collective-permute-start.20) | collective-permute-done | bytes 245792 | tf_op jit(solution)/shard_map/ppermute | solution.py:166
  50.6 0.8 collective-permute-start.5
  51.4 1.2 collective-permute-start.13
  53.4 1.2 collective-permute-start.21
  54.7 2.2 %collective-permute-done.5 = bf16[4,120,256]{2,1,0:T(8,128)(2,1)S(1)} collective-permute-done((bf16[4,120,256]{2,1,0:T(8,128)(2,1)S(1)}, bf16[4,120,256]{2,1,0:T(8,128)(2,1)S(1)}, u32[]{:S(2)}, u32[]{:S(2)}) %collective-permute-start.5) | collective-permute-done | bytes 245792 | tf_op jit(solution)/shard_map/ppermute | solution.py:168
  56.9 0.9 collective-permute-done.13
  57.7 1.0 constant_dynamic-update-slice_fusion.23
  59.5 2.3 %collective-permute-done.21 = bf16[4,120,256]{2,1,0:T(8,128)(2,1)S(1)} collective-permute-done((bf16[4,120,256]{2,1,0:T(8,128)(2,1)S(1)}, bf16[4,120,256]{2,1,0:T(8,128)(2,1)S(1)}, u32[]{:S(2)}, u32[]{:S(2)}) %collective-permute-start.21) | collective-permute-done | bytes 245792 | tf_op jit(solution)/shard_map/ppermute | solution.py:166
  61.8 1.0 constant_dynamic-update-slice_fusion.22
  62.8 1.2 collective-permute-start.33
  65.0 1.9 %collective-permute-start.28 = (bf16[4,120,256]{2,1,0:T(8,128)(2,1)S(1)}, bf16[4,120,256]{2,1,0:T(8,128)(2,1)S(1)}, u32[]{:S(2)}, u32[]{:S(2)}) collective-permute-start(bf16[4,120,256]{2,1,0:T(8,128)(2,1)S(1)} %get-tuple-element.36), channel_id=1, source_target_pairs={{0,8},{2,10},{8,16},{10,18},{16,24},{18,26},{24,28},{26,30},{28,20... | collective-permute-start | bytes 737288 | tf_op jit(solution)/shard_map/ppermute | solution.py:186
  67.0 2.0 %collective-permute-done.33 = bf16[4,120,256]{2,1,0:T(8,128)(2,1)S(1)} collective-permute-done((bf16[4,120,256]{2,1,0:T(8,128)(2,1)S(1)}, bf16[4,120,256]{2,1,0:T(8,128)(2,1)S(1)}, u32[]{:S(2)}, u32[]{:S(2)}) %collective-permute-start.33) | collective-permute-done | bytes 245792 | tf_op jit(solution)/shard_map/ppermute | solution.py:186
  69.0 1.2 collective-permute-start.34
  71.0 3.6 %collective-permute-done.22 = bf16[4,120,256]{2,1,0:T(8,128)(2,1)S(1)} collective-permute-done((bf16[4,120,256]{2,1,0:T(8,128)(2,1)S(1)}, bf16[4,120,256]{2,1,0:T(8,128)(2,1)S(1)}, u32[]{:S(2)}, u32[]{:S(2)}) %collective-permute-start.22) | collective-permute-done | bytes 245792 | tf_op jit(solution)/shard_map/ppermute | solution.py:189
  75.5 1.3 %collective-permute-start.29 = (bf16[4,120,256]{2,1,0:T(8,128)(2,1)S(1)}, bf16[4,120,256]{2,1,0:T(8,128)(2,1)S(1)}, u32[]{:S(2)}, u32[]{:S(2)}) collective-permute-start(bf16[4,120,256]{2,1,0:T(8,128)(2,1)S(1)} %collective-permute-done.28), channel_id=1, source_target_pairs={{0,8},{2,10},{8,16},{10,18},{16,24},{18,26},{24,28},{26,30},{28,20... | collective-permute-start | bytes 737288 | tf_op jit(solution)/shard_map/ppermute | solution.py:186
  78.3 1.6 %collective-permute-done.25 = bf16[4,120,256]{2,1,0:T(8,128)(2,1)S(1)} collective-permute-done((bf16[4,120,256]{2,1,0:T(8,128)(2,1)S(1)}, bf16[4,120,256]{2,1,0:T(8,128)(2,1)S(1)}, u32[]{:S(2)}, u32[]{:S(2)}) %collective-permute-start.25) | collective-permute-done | bytes 245792 | tf_op jit(solution)/shard_map/ppermute | solution.py:189
  80.7 4.5 %collective-permute-done.24 = bf16[4,120,256]{2,1,0:T(8,128)(2,1)S(1)} collective-permute-done((bf16[4,120,256]{2,1,0:T(8,128)(2,1)S(1)}, bf16[4,120,256]{2,1,0:T(8,128)(2,1)S(1)}, u32[]{:S(2)}, u32[]{:S(2)}) %collective-permute-start.24) | collective-permute-done | bytes 245792 | tf_op jit(solution)/shard_map/ppermute | solution.py:189
  85.2 0.8 collective-permute-start.26
  86.0 1.2 collective-permute-start.30
  88.8 1.6 %collective-permute-done.27 = bf16[4,120,256]{2,1,0:T(8,128)(2,1)S(1)} collective-permute-done((bf16[4,120,256]{2,1,0:T(8,128)(2,1)S(1)}, bf16[4,120,256]{2,1,0:T(8,128)(2,1)S(1)}, u32[]{:S(2)}, u32[]{:S(2)}) %collective-permute-start.27) | collective-permute-done | bytes 245792 | tf_op jit(solution)/shard_map/ppermute | solution.py:189
  90.4 1.7 %collective-permute-start.35 = (bf16[4,120,256]{2,1,0:T(8,128)(2,1)S(1)}, bf16[4,120,256]{2,1,0:T(8,128)(2,1)S(1)}, u32[]{:S(2)}, u32[]{:S(2)}) collective-permute-start(bf16[4,120,256]{2,1,0:T(8,128)(2,1)S(1)} %collective-permute-done.34), channel_id=1, source_target_pairs={{0,8},{2,10},{8,16},{10,18},{16,24},{18,26},{24,28},{26,30},{28,20... | collective-permute-start | bytes 737288 | tf_op jit(solution)/shard_map/ppermute | solution.py:186
  92.5 1.9 %collective-permute-done.26 = bf16[4,120,256]{2,1,0:T(8,128)(2,1)S(1)} collective-permute-done((bf16[4,120,256]{2,1,0:T(8,128)(2,1)S(1)}, bf16[4,120,256]{2,1,0:T(8,128)(2,1)S(1)}, u32[]{:S(2)}, u32[]{:S(2)}) %collective-permute-start.26) | collective-permute-done | bytes 245792 | tf_op jit(solution)/shard_map/ppermute | solution.py:189
  94.4 3.1 %collective-permute-start.31 = (bf16[4,120,256]{2,1,0:T(8,128)(2,1)S(1)}, bf16[4,120,256]{2,1,0:T(8,128)(2,1)S(1)}, u32[]{:S(2)}, u32[]{:S(2)}) collective-permute-start(bf16[4,120,256]{2,1,0:T(8,128)(2,1)S(1)} %collective-permute-done.30), channel_id=1, source_target_pairs={{0,8},{2,10},{8,16},{10,18},{16,24},{18,26},{24,28},{26,30},{28,20... | collective-permute-start | bytes 737288 | tf_op jit(solution)/shard_map/ppermute | solution.py:186
  99.4 3.4 %collective-permute-done.31 = bf16[4,120,256]{2,1,0:T(8,128)(2,1)S(1)} collective-permute-done((bf16[4,120,256]{2,1,0:T(8,128)(2,1)S(1)}, bf16[4,120,256]{2,1,0:T(8,128)(2,1)S(1)}, u32[]{:S(2)}, u32[]{:S(2)}) %collective-permute-start.31) | collective-permute-done | bytes 245792 | tf_op jit(solution)/shard_map/ppermute | solution.py:186
  109.1 0.8 constant_dynamic-update-slice_fusion.7
  110.4 0.8 constant_dynamic-update-slice_fusion.6
  111.3 0.8 constant_dynamic-update-slice_fusion.5
  112.1 0.8 constant_dynamic-update-slice_fusion.4
  115.4 0.9 constant_dynamic-update-slice_fusion.weighted
  116.2 3.2 %copy-done.3 = bf16[128,120,256]{2,1,0:T(8,128)(2,1)S(1)} copy-done((bf16[128,120,256]{2,1,0:T(8,128)(2,1)S(1)}, bf16[128,120,256]{2,1,0:T(8,128)(2,1)}, u32[]{:S(2)}) %copy-start.3) | copy-done | bytes 7864344
  119.5 4.0 %apply_cells.1 = f32[120,128]{1,0:T(8,128)S(1)} custom-call(s32[64]{0:T(128)S(1)} %get-tuple-element.6.cell, bf16[128,120,256]{2,1,0:T(8,128)(2,1)S(1)} %copy-done.3, bf16[64,256,128]{2,1,0:T(8,128)(2,1)S(1)} %copy-done.2), custom_call_target="tpu_custom_call" | custom-call | tf_op jit(solution)/shard_map/apply_cells/pallas_call | solution.py:94
  123.6 1.5 %collective-permute-start.44 = (f32[120,64]{1,0:T(8,128)S(1)}, f32[120,64]{1,0:T(8,128)S(1)}, u32[]{:S(2)}, u32[]{:S(2)}) collective-permute-start(f32[120,64]{1,0:T(8,128)S(1)} %slice_select_fusion), channel_id=1, source_target_pairs={{0,1},{1,0},{2,3},{3,2},{4,5},{5,4},{6,7},{7,6},{8,9},{9,8},{10,11... | collective-permute-start | bytes 92168 | tf_op jit(solution)/shard_map/ppermute | solution.py:118
  125.1 2.9 %collective-permute-done.44 = f32[120,64]{1,0:T(8,128)S(1)} collective-permute-done((f32[120,64]{1,0:T(8,128)S(1)}, f32[120,64]{1,0:T(8,128)S(1)}, u32[]{:S(2)}, u32[]{:S(2)}) %collective-permute-start.44) | collective-permute-done | bytes 30752 | tf_op jit(solution)/shard_map/ppermute | solution.py:118
  (97 shorter events, 27.4 us)
Async XLA Ops:
  0.0 57.7 %copy-start = (bf16[1,256,256]{2,1,0:T(8,128)(2,1)S(1)}, bf16[1,256,256]{2,1,0:T(8,128)(2,1)}, u32[]{:S(2)}) copy-start(bf16[1,256,256]{2,1,0:T(8,128)(2,1)} %param.9) | copy-start | bytes 393220
  9.2 2.0 %collective-permute-start.6 = (bf16[8,120,256]{2,1,0:T(8,128)(2,1)S(1)}, bf16[8,120,256]{2,1,0:T(8,128)(2,1)S(1)}, u32[]{:S(2)}, u32[]{:S(2)}) collective-permute-start(bf16[8,120,256]{2,1,0:T(8,128)(2,1)S(1)} %get-tuple-element.31), channel_id=1, source_target_pairs={{0,2},{2,0},{4,6},{6,4},{8,10},{10,8},{12,14},{14,12},{16,18},{18,... | collective-permute-start | bytes 1474568 | tf_op jit(solution)/shard_map/ppermute | solution.py:154
  9.7 4.7 %collective-permute-start.8 = (bf16[8,120,256]{2,1,0:T(8,128)(2,1)S(1)}, bf16[8,120,256]{2,1,0:T(8,128)(2,1)S(1)}, u32[]{:S(2)}, u32[]{:S(2)}) collective-permute-start(bf16[8,120,256]{2,1,0:T(8,128)(2,1)S(1)} %get-tuple-element.30), channel_id=1, source_target_pairs={{0,2},{2,0},{4,6},{6,4},{8,10},{10,8},{12,14},{14,12},{16,18},{18,... | collective-permute-start | bytes 1474568 | tf_op jit(solution)/shard_map/ppermute | solution.py:154
  9.8 5.1 %collective-permute-start = (bf16[8,120,256]{2,1,0:T(8,128)(2,1)S(1)}, bf16[8,120,256]{2,1,0:T(8,128)(2,1)S(1)}, u32[]{:S(2)}, u32[]{:S(2)}) collective-permute-start(bf16[8,120,256]{2,1,0:T(8,128)(2,1)S(1)} %get-tuple-element.34), channel_id=1, source_target_pairs={{0,2},{2,0},{4,6},{6,4},{8,10},{10,8},{12,14},{14,12},{16,18},{18,... | collective-permute-start | bytes 1474568 | tf_op jit(solution)/shard_map/ppermute | solution.py:154
  11.3 9.2 %collective-permute-start.15 = (bf16[4,120,256]{2,1,0:T(8,128)(2,1)S(1)}, bf16[4,120,256]{2,1,0:T(8,128)(2,1)S(1)}, u32[]{:S(2)}, u32[]{:S(2)}) collective-permute-start(bf16[4,120,256]{2,1,0:T(8,128)(2,1)S(1)} %get-tuple-element.13), channel_id=1, source_target_pairs={{0,4},{2,6},{8,0},{10,2},{16,8},{18,10},{24,16},{26,18},{28,24},{3... | collective-permute-start | bytes 737288 | tf_op jit(solution)/shard_map/ppermute | solution.py:168
  14.3 7.7 %collective-permute-start.7 = (bf16[4,120,256]{2,1,0:T(8,128)(2,1)S(1)}, bf16[4,120,256]{2,1,0:T(8,128)(2,1)S(1)}, u32[]{:S(2)}, u32[]{:S(2)}) collective-permute-start(bf16[4,120,256]{2,1,0:T(8,128)(2,1)S(1)} %get-tuple-element.14), channel_id=1, source_target_pairs={{0,8},{2,10},{8,16},{10,18},{16,24},{18,26},{24,28},{26,30},{28,20... | collective-permute-start | bytes 737288 | tf_op jit(solution)/shard_map/ppermute | solution.py:166
  14.4 11.6 %collective-permute-start.10 = (bf16[8,120,256]{2,1,0:T(8,128)(2,1)S(1)}, bf16[8,120,256]{2,1,0:T(8,128)(2,1)S(1)}, u32[]{:S(2)}, u32[]{:S(2)}) collective-permute-start(bf16[8,120,256]{2,1,0:T(8,128)(2,1)S(1)} %get-tuple-element.29), channel_id=1, source_target_pairs={{0,2},{2,0},{4,6},{6,4},{8,10},{10,8},{12,14},{14,12},{16,18},{18,... | collective-permute-start | bytes 1474568 | tf_op jit(solution)/shard_map/ppermute | solution.py:154
  14.4 12.0 %collective-permute-start.2 = (bf16[8,120,256]{2,1,0:T(8,128)(2,1)S(1)}, bf16[8,120,256]{2,1,0:T(8,128)(2,1)S(1)}, u32[]{:S(2)}, u32[]{:S(2)}) collective-permute-start(bf16[8,120,256]{2,1,0:T(8,128)(2,1)S(1)} %get-tuple-element.33), channel_id=1, source_target_pairs={{0,2},{2,0},{4,6},{6,4},{8,10},{10,8},{12,14},{14,12},{16,18},{18,... | collective-permute-start | bytes 1474568 | tf_op jit(solution)/shard_map/ppermute | solution.py:154
  22.3 8.9 %collective-permute-start.16 = (bf16[4,120,256]{2,1,0:T(8,128)(2,1)S(1)}, bf16[4,120,256]{2,1,0:T(8,128)(2,1)S(1)}, u32[]{:S(2)}, u32[]{:S(2)}) collective-permute-start(bf16[4,120,256]{2,1,0:T(8,128)(2,1)S(1)} %get-tuple-element.11), channel_id=1, source_target_pairs={{0,4},{2,6},{8,0},{10,2},{16,8},{18,10},{24,16},{26,18},{28,24},{3... | collective-permute-start | bytes 737288 | tf_op jit(solution)/shard_map/ppermute | solution.py:168
  23.9 10.5 %collective-permute-start.1 = (bf16[4,120,256]{2,1,0:T(8,128)(2,1)S(1)}, bf16[4,120,256]{2,1,0:T(8,128)(2,1)S(1)}, u32[]{:S(2)}, u32[]{:S(2)}) collective-permute-start(bf16[4,120,256]{2,1,0:T(8,128)(2,1)S(1)} %get-tuple-element.12), channel_id=1, source_target_pairs={{0,4},{2,6},{8,0},{10,2},{16,8},{18,10},{24,16},{26,18},{28,24},{3... | collective-permute-start | bytes 737288 | tf_op jit(solution)/shard_map/ppermute | solution.py:168
  25.5 9.0 %collective-permute-start.9 = (bf16[4,120,256]{2,1,0:T(8,128)(2,1)S(1)}, bf16[4,120,256]{2,1,0:T(8,128)(2,1)S(1)}, u32[]{:S(2)}, u32[]{:S(2)}) collective-permute-start(bf16[4,120,256]{2,1,0:T(8,128)(2,1)S(1)} %get-tuple-element.25), channel_id=1, source_target_pairs={{0,8},{2,10},{8,16},{10,18},{16,24},{18,26},{24,28},{26,30},{28,20... | collective-permute-start | bytes 737288 | tf_op jit(solution)/shard_map/ppermute | solution.py:166
  26.0 11.1 %collective-permute-start.19 = (bf16[4,120,256]{2,1,0:T(8,128)(2,1)S(1)}, bf16[4,120,256]{2,1,0:T(8,128)(2,1)S(1)}, u32[]{:S(2)}, u32[]{:S(2)}) collective-permute-start(bf16[4,120,256]{2,1,0:T(8,128)(2,1)S(1)} %get-tuple-element.26), channel_id=1, source_target_pairs={{0,8},{2,10},{8,16},{10,18},{16,24},{18,26},{24,28},{26,30},{28,20... | collective-permute-start | bytes 737288 | tf_op jit(solution)/shard_map/ppermute | solution.py:166
  26.4 14.7 %collective-permute-start.12 = (bf16[8,120,256]{2,1,0:T(8,128)(2,1)S(1)}, bf16[8,120,256]{2,1,0:T(8,128)(2,1)S(1)}, u32[]{:S(2)}, u32[]{:S(2)}) collective-permute-start(bf16[8,120,256]{2,1,0:T(8,128)(2,1)S(1)} %get-tuple-element.28), channel_id=1, source_target_pairs={{0,2},{2,0},{4,6},{6,4},{8,10},{10,8},{12,14},{14,12},{16,18},{18,... | collective-permute-start | bytes 1474568 | tf_op jit(solution)/shard_map/ppermute | solution.py:154
  31.3 10.3 %collective-permute-start.4 = (bf16[8,120,256]{2,1,0:T(8,128)(2,1)S(1)}, bf16[8,120,256]{2,1,0:T(8,128)(2,1)S(1)}, u32[]{:S(2)}, u32[]{:S(2)}) collective-permute-start(bf16[8,120,256]{2,1,0:T(8,128)(2,1)S(1)} %get-tuple-element.32), channel_id=1, source_target_pairs={{0,2},{2,0},{4,6},{6,4},{8,10},{10,8},{12,14},{14,12},{16,18},{18,... | collective-permute-start | bytes 1474568 | tf_op jit(solution)/shard_map/ppermute | solution.py:154
  37.5 8.0 %collective-permute-start.17 = (bf16[4,120,256]{2,1,0:T(8,128)(2,1)S(1)}, bf16[4,120,256]{2,1,0:T(8,128)(2,1)S(1)}, u32[]{:S(2)}, u32[]{:S(2)}) collective-permute-start(bf16[4,120,256]{2,1,0:T(8,128)(2,1)S(1)} %get-tuple-element.9), channel_id=1, source_target_pairs={{0,4},{2,6},{8,0},{10,2},{16,8},{18,10},{24,16},{26,18},{28,24},{3... | collective-permute-start | bytes 737288 | tf_op jit(solution)/shard_map/ppermute | solution.py:168
  39.1 9.1 %collective-permute-start.3 = (bf16[4,120,256]{2,1,0:T(8,128)(2,1)S(1)}, bf16[4,120,256]{2,1,0:T(8,128)(2,1)S(1)}, u32[]{:S(2)}, u32[]{:S(2)}) collective-permute-start(bf16[4,120,256]{2,1,0:T(8,128)(2,1)S(1)} %get-tuple-element.10), channel_id=1, source_target_pairs={{0,4},{2,6},{8,0},{10,2},{16,8},{18,10},{24,16},{26,18},{28,24},{3... | collective-permute-start | bytes 737288 | tf_op jit(solution)/shard_map/ppermute | solution.py:168
  39.7 8.5 %collective-permute-start.11 = (bf16[4,120,256]{2,1,0:T(8,128)(2,1)S(1)}, bf16[4,120,256]{2,1,0:T(8,128)(2,1)S(1)}, u32[]{:S(2)}, u32[]{:S(2)}) collective-permute-start(bf16[4,120,256]{2,1,0:T(8,128)(2,1)S(1)} %get-tuple-element.23), channel_id=1, source_target_pairs={{0,8},{2,10},{8,16},{10,18},{16,24},{18,26},{24,28},{26,30},{28,20... | collective-permute-start | bytes 737288 | tf_op jit(solution)/shard_map/ppermute | solution.py:166
  41.1 9.0 %collective-permute-start.20 = (bf16[4,120,256]{2,1,0:T(8,128)(2,1)S(1)}, bf16[4,120,256]{2,1,0:T(8,128)(2,1)S(1)}, u32[]{:S(2)}, u32[]{:S(2)}) collective-permute-start(bf16[4,120,256]{2,1,0:T(8,128)(2,1)S(1)} %get-tuple-element.24), channel_id=1, source_target_pairs={{0,8},{2,10},{8,16},{10,18},{16,24},{18,26},{24,28},{26,30},{28,20... | collective-permute-start | bytes 737288 | tf_op jit(solution)/shard_map/ppermute | solution.py:166
  41.6 13.1 %collective-permute-start.14 = (bf16[8,120,256]{2,1,0:T(8,128)(2,1)S(1)}, bf16[8,120,256]{2,1,0:T(8,128)(2,1)S(1)}, u32[]{:S(2)}, u32[]{:S(2)}) collective-permute-start(bf16[8,120,256]{2,1,0:T(8,128)(2,1)S(1)} %get-tuple-element.27), channel_id=1, source_target_pairs={{0,2},{2,0},{4,6},{6,4},{8,10},{10,8},{12,14},{14,12},{16,18},{18,... | collective-permute-start | bytes 1474568 | tf_op jit(solution)/shard_map/ppermute | solution.py:154
  50.6 6.3 %collective-permute-start.5 = (bf16[4,120,256]{2,1,0:T(8,128)(2,1)S(1)}, bf16[4,120,256]{2,1,0:T(8,128)(2,1)S(1)}, u32[]{:S(2)}, u32[]{:S(2)}) collective-permute-start(bf16[4,120,256]{2,1,0:T(8,128)(2,1)S(1)} %get-tuple-element.8), channel_id=1, source_target_pairs={{0,4},{2,6},{8,0},{10,2},{16,8},{18,10},{24,16},{26,18},{28,24},{3... | collective-permute-start | bytes 737288 | tf_op jit(solution)/shard_map/ppermute | solution.py:168
  51.4 6.3 %collective-permute-start.13 = (bf16[4,120,256]{2,1,0:T(8,128)(2,1)S(1)}, bf16[4,120,256]{2,1,0:T(8,128)(2,1)S(1)}, u32[]{:S(2)}, u32[]{:S(2)}) collective-permute-start(bf16[4,120,256]{2,1,0:T(8,128)(2,1)S(1)} %get-tuple-element.21), channel_id=1, source_target_pairs={{0,8},{2,10},{8,16},{10,18},{16,24},{18,26},{24,28},{26,30},{28,20... | collective-permute-start | bytes 737288 | tf_op jit(solution)/shard_map/ppermute | solution.py:166
  52.7 6.8 %collective-permute-start.18 = (bf16[4,120,256]{2,1,0:T(8,128)(2,1)S(1)}, bf16[4,120,256]{2,1,0:T(8,128)(2,1)S(1)}, u32[]{:S(2)}, u32[]{:S(2)}) collective-permute-start(bf16[4,120,256]{2,1,0:T(8,128)(2,1)S(1)} %get-tuple-element.7), channel_id=1, source_target_pairs={{0,4},{2,6},{8,0},{10,2},{16,8},{18,10},{24,16},{26,18},{28,24},{3... | collective-permute-start | bytes 737288 | tf_op jit(solution)/shard_map/ppermute | solution.py:168
  53.4 8.4 %collective-permute-start.21 = (bf16[4,120,256]{2,1,0:T(8,128)(2,1)S(1)}, bf16[4,120,256]{2,1,0:T(8,128)(2,1)S(1)}, u32[]{:S(2)}, u32[]{:S(2)}) collective-permute-start(bf16[4,120,256]{2,1,0:T(8,128)(2,1)S(1)} %get-tuple-element.22), channel_id=1, source_target_pairs={{0,8},{2,10},{8,16},{10,18},{16,24},{18,26},{24,28},{26,30},{28,20... | collective-permute-start | bytes 737288 | tf_op jit(solution)/shard_map/ppermute | solution.py:166
  62.8 6.2 %collective-permute-start.33 = (bf16[4,120,256]{2,1,0:T(8,128)(2,1)S(1)}, bf16[4,120,256]{2,1,0:T(8,128)(2,1)S(1)}, u32[]{:S(2)}, u32[]{:S(2)}) collective-permute-start(bf16[4,120,256]{2,1,0:T(8,128)(2,1)S(1)} %get-tuple-element.38), channel_id=1, source_target_pairs={{0,8},{2,10},{8,16},{10,18},{16,24},{18,26},{24,28},{26,30},{28,20... | collective-permute-start | bytes 737288 | tf_op jit(solution)/shard_map/ppermute | solution.py:186
  64.0 6.2 %collective-permute-start.23 = (bf16[4,120,256]{2,1,0:T(8,128)(2,1)S(1)}, bf16[4,120,256]{2,1,0:T(8,128)(2,1)S(1)}, u32[]{:S(2)}, u32[]{:S(2)}) collective-permute-start(bf16[4,120,256]{2,1,0:T(8,128)(2,1)S(1)} %get-tuple-element.38), channel_id=1, source_target_pairs={{0,4},{2,6},{8,0},{10,2},{16,8},{18,10},{24,16},{26,18},{28,24},{3... | collective-permute-start | bytes 737288 | tf_op jit(solution)/shard_map/ppermute | solution.py:189
  64.8 9.8 %collective-permute-start.22 = (bf16[4,120,256]{2,1,0:T(8,128)(2,1)S(1)}, bf16[4,120,256]{2,1,0:T(8,128)(2,1)S(1)}, u32[]{:S(2)}, u32[]{:S(2)}) collective-permute-start(bf16[4,120,256]{2,1,0:T(8,128)(2,1)S(1)} %get-tuple-element.36), channel_id=1, source_target_pairs={{0,4},{2,6},{8,0},{10,2},{16,8},{18,10},{24,16},{26,18},{28,24},{3... | collective-permute-start | bytes 737288 | tf_op jit(solution)/shard_map/ppermute | solution.py:189
  65.0 10.5 %collective-permute-start.28 = (bf16[4,120,256]{2,1,0:T(8,128)(2,1)S(1)}, bf16[4,120,256]{2,1,0:T(8,128)(2,1)S(1)}, u32[]{:S(2)}, u32[]{:S(2)}) collective-permute-start(bf16[4,120,256]{2,1,0:T(8,128)(2,1)S(1)} %get-tuple-element.36), channel_id=1, source_target_pairs={{0,8},{2,10},{8,16},{10,18},{16,24},{18,26},{24,28},{26,30},{28,20... | collective-permute-start | bytes 737288 | tf_op jit(solution)/shard_map/ppermute | solution.py:186
  66.9 42.2 %collective-permute-start.36 = (bf16[8,120,256]{2,1,0:T(8,128)(2,1)S(1)}, bf16[8,120,256]{2,1,0:T(8,128)(2,1)S(1)}, u32[]{:S(2)}, u32[]{:S(2)}) collective-permute-start(bf16[8,120,256]{2,1,0:T(8,128)(2,1)S(1)} %pad_maximum_fusion), channel_id=1, source_target_pairs={{0,2},{2,0},{4,6},{6,4},{8,10},{10,8},{12,14},{14,12},{16,18},{18,... | collective-permute-start | bytes 1474568 | tf_op jit(solution)/shard_map/ppermute | solution.py:193
  69.0 19.8 %collective-permute-start.34 = (bf16[4,120,256]{2,1,0:T(8,128)(2,1)S(1)}, bf16[4,120,256]{2,1,0:T(8,128)(2,1)S(1)}, u32[]{:S(2)}, u32[]{:S(2)}) collective-permute-start(bf16[4,120,256]{2,1,0:T(8,128)(2,1)S(1)} %collective-permute-done.33), channel_id=1, source_target_pairs={{0,8},{2,10},{8,16},{10,18},{16,24},{18,26},{24,28},{26,30},{28,20... | collective-permute-start | bytes 737288 | tf_op jit(solution)/shard_map/ppermute | solution.py:186
  70.2 9.7 %collective-permute-start.25 = (bf16[4,120,256]{2,1,0:T(8,128)(2,1)S(1)}, bf16[4,120,256]{2,1,0:T(8,128)(2,1)S(1)}, u32[]{:S(2)}, u32[]{:S(2)}) collective-permute-start(bf16[4,120,256]{2,1,0:T(8,128)(2,1)S(1)} %collective-permute-done.23), channel_id=1, source_target_pairs={{0,4},{2,6},{8,0},{10,2},{16,8},{18,10},{24,16},{26,18},{28,24},{3... | collective-permute-start | bytes 737288 | tf_op jit(solution)/shard_map/ppermute | solution.py:189
  74.6 10.5 %collective-permute-start.24 = (bf16[4,120,256]{2,1,0:T(8,128)(2,1)S(1)}, bf16[4,120,256]{2,1,0:T(8,128)(2,1)S(1)}, u32[]{:S(2)}, u32[]{:S(2)}) collective-permute-start(bf16[4,120,256]{2,1,0:T(8,128)(2,1)S(1)} %collective-permute-done.22), channel_id=1, source_target_pairs={{0,4},{2,6},{8,0},{10,2},{16,8},{18,10},{24,16},{26,18},{28,24},{3... | collective-permute-start | bytes 737288 | tf_op jit(solution)/shard_map/ppermute | solution.py:189
  75.5 10.6 %collective-permute-start.29 = (bf16[4,120,256]{2,1,0:T(8,128)(2,1)S(1)}, bf16[4,120,256]{2,1,0:T(8,128)(2,1)S(1)}, u32[]{:S(2)}, u32[]{:S(2)}) collective-permute-start(bf16[4,120,256]{2,1,0:T(8,128)(2,1)S(1)} %collective-permute-done.28), channel_id=1, source_target_pairs={{0,8},{2,10},{8,16},{10,18},{16,24},{18,26},{24,28},{26,30},{28,20... | collective-permute-start | bytes 737288 | tf_op jit(solution)/shard_map/ppermute | solution.py:186
  79.9 10.5 %collective-permute-start.27 = (bf16[4,120,256]{2,1,0:T(8,128)(2,1)S(1)}, bf16[4,120,256]{2,1,0:T(8,128)(2,1)S(1)}, u32[]{:S(2)}, u32[]{:S(2)}) collective-permute-start(bf16[4,120,256]{2,1,0:T(8,128)(2,1)S(1)} %collective-permute-done.25), channel_id=1, source_target_pairs={{0,4},{2,6},{8,0},{10,2},{16,8},{18,10},{24,16},{26,18},{28,24},{3... | collective-permute-start | bytes 737288 | tf_op jit(solution)/shard_map/ppermute | solution.py:189
  85.2 9.1 %collective-permute-start.26 = (bf16[4,120,256]{2,1,0:T(8,128)(2,1)S(1)}, bf16[4,120,256]{2,1,0:T(8,128)(2,1)S(1)}, u32[]{:S(2)}, u32[]{:S(2)}) collective-permute-start(bf16[4,120,256]{2,1,0:T(8,128)(2,1)S(1)} %collective-permute-done.24), channel_id=1, source_target_pairs={{0,4},{2,6},{8,0},{10,2},{16,8},{18,10},{24,16},{26,18},{28,24},{3... | collective-permute-start | bytes 737288 | tf_op jit(solution)/shard_map/ppermute | solution.py:189
  86.0 6.4 %collective-permute-start.30 = (bf16[4,120,256]{2,1,0:T(8,128)(2,1)S(1)}, bf16[4,120,256]{2,1,0:T(8,128)(2,1)S(1)}, u32[]{:S(2)}, u32[]{:S(2)}) collective-permute-start(bf16[4,120,256]{2,1,0:T(8,128)(2,1)S(1)} %collective-permute-done.29), channel_id=1, source_target_pairs={{0,8},{2,10},{8,16},{10,18},{16,24},{18,26},{24,28},{26,30},{28,20... | collective-permute-start | bytes 737288 | tf_op jit(solution)/shard_map/ppermute | solution.py:186
  88.7 26.6 %collective-permute-start.43 = (bf16[8,120,256]{2,1,0:T(8,128)(2,1)S(1)}, bf16[8,120,256]{2,1,0:T(8,128)(2,1)S(1)}, u32[]{:S(2)}, u32[]{:S(2)}) collective-permute-start(bf16[8,120,256]{2,1,0:T(8,128)(2,1)S(1)} %pad_maximum_fusion.7), channel_id=1, source_target_pairs={{0,2},{2,0},{4,6},{6,4},{8,10},{10,8},{12,14},{14,12},{16,18},{18,... | collective-permute-start | bytes 1474568 | tf_op jit(solution)/shard_map/ppermute | solution.py:193
  88.8 27.4 %copy-start.2 = (bf16[64,256,128]{2,1,0:T(8,128)(2,1)S(1)}, bf16[64,256,128]{2,1,0:T(8,128)(2,1)}, u32[]{:S(2)}) copy-start(bf16[64,256,128]{2,1,0:T(8,128)(2,1)} %tens.3) | copy-start | bytes 12582916
  90.4 8.9 %collective-permute-start.35 = (bf16[4,120,256]{2,1,0:T(8,128)(2,1)S(1)}, bf16[4,120,256]{2,1,0:T(8,128)(2,1)S(1)}, u32[]{:S(2)}, u32[]{:S(2)}) collective-permute-start(bf16[4,120,256]{2,1,0:T(8,128)(2,1)S(1)} %collective-permute-done.34), channel_id=1, source_target_pairs={{0,8},{2,10},{8,16},{10,18},{16,24},{18,26},{24,28},{26,30},{28,20... | collective-permute-start | bytes 737288 | tf_op jit(solution)/shard_map/ppermute | solution.py:186
  92.4 11.1 %collective-permute-start.32 = (bf16[4,120,256]{2,1,0:T(8,128)(2,1)S(1)}, bf16[4,120,256]{2,1,0:T(8,128)(2,1)S(1)}, u32[]{:S(2)}, u32[]{:S(2)}) collective-permute-start(bf16[4,120,256]{2,1,0:T(8,128)(2,1)S(1)} %collective-permute-done.27), channel_id=1, source_target_pairs={{0,4},{2,6},{8,0},{10,2},{16,8},{18,10},{24,16},{26,18},{28,24},{3... | collective-permute-start | bytes 737288 | tf_op jit(solution)/shard_map/ppermute | solution.py:189
  94.4 8.4 %collective-permute-start.31 = (bf16[4,120,256]{2,1,0:T(8,128)(2,1)S(1)}, bf16[4,120,256]{2,1,0:T(8,128)(2,1)S(1)}, u32[]{:S(2)}, u32[]{:S(2)}) collective-permute-start(bf16[4,120,256]{2,1,0:T(8,128)(2,1)S(1)} %collective-permute-done.30), channel_id=1, source_target_pairs={{0,8},{2,10},{8,16},{10,18},{16,24},{18,26},{24,28},{26,30},{28,20... | collective-permute-start | bytes 737288 | tf_op jit(solution)/shard_map/ppermute | solution.py:186
  99.3 10.6 %collective-permute-start.37 = (bf16[8,120,256]{2,1,0:T(8,128)(2,1)S(1)}, bf16[8,120,256]{2,1,0:T(8,128)(2,1)S(1)}, u32[]{:S(2)}, u32[]{:S(2)}) collective-permute-start(bf16[8,120,256]{2,1,0:T(8,128)(2,1)S(1)} %pad_maximum_fusion.1), channel_id=1, source_target_pairs={{0,2},{2,0},{4,6},{6,4},{8,10},{10,8},{12,14},{14,12},{16,18},{18,... | collective-permute-start | bytes 1474568 | tf_op jit(solution)/shard_map/ppermute | solution.py:193
  102.8 8.5 %collective-permute-start.38 = (bf16[8,120,256]{2,1,0:T(8,128)(2,1)S(1)}, bf16[8,120,256]{2,1,0:T(8,128)(2,1)S(1)}, u32[]{:S(2)}, u32[]{:S(2)}) collective-permute-start(bf16[8,120,256]{2,1,0:T(8,128)(2,1)S(1)} %pad_maximum_fusion.2), channel_id=1, source_target_pairs={{0,2},{2,0},{4,6},{6,4},{8,10},{10,8},{12,14},{14,12},{16,18},{18,... | collective-permute-start | bytes 1474568 | tf_op jit(solution)/shard_map/ppermute | solution.py:193
  103.5 8.6 %collective-permute-start.39 = (bf16[8,120,256]{2,1,0:T(8,128)(2,1)S(1)}, bf16[8,120,256]{2,1,0:T(8,128)(2,1)S(1)}, u32[]{:S(2)}, u32[]{:S(2)}) collective-permute-start(bf16[8,120,256]{2,1,0:T(8,128)(2,1)S(1)} %pad_maximum_fusion.3), channel_id=1, source_target_pairs={{0,2},{2,0},{4,6},{6,4},{8,10},{10,8},{12,14},{14,12},{16,18},{18,... | collective-permute-start | bytes 1474568 | tf_op jit(solution)/shard_map/ppermute | solution.py:193
  109.1 3.8 %collective-permute-start.40 = (bf16[8,120,256]{2,1,0:T(8,128)(2,1)S(1)}, bf16[8,120,256]{2,1,0:T(8,128)(2,1)S(1)}, u32[]{:S(2)}, u32[]{:S(2)}) collective-permute-start(bf16[8,120,256]{2,1,0:T(8,128)(2,1)S(1)} %pad_maximum_fusion.4), channel_id=1, source_target_pairs={{0,2},{2,0},{4,6},{6,4},{8,10},{10,8},{12,14},{14,12},{16,18},{18,... | collective-permute-start | bytes 1474568 | tf_op jit(solution)/shard_map/ppermute | solution.py:193
  109.9 3.8 %collective-permute-start.41 = (bf16[8,120,256]{2,1,0:T(8,128)(2,1)S(1)}, bf16[8,120,256]{2,1,0:T(8,128)(2,1)S(1)}, u32[]{:S(2)}, u32[]{:S(2)}) collective-permute-start(bf16[8,120,256]{2,1,0:T(8,128)(2,1)S(1)} %pad_maximum_fusion.5), channel_id=1, source_target_pairs={{0,2},{2,0},{4,6},{6,4},{8,10},{10,8},{12,14},{14,12},{16,18},{18,... | collective-permute-start | bytes 1474568 | tf_op jit(solution)/shard_map/ppermute | solution.py:193
  111.2 3.3 %collective-permute-start.42 = (bf16[8,120,256]{2,1,0:T(8,128)(2,1)S(1)}, bf16[8,120,256]{2,1,0:T(8,128)(2,1)S(1)}, u32[]{:S(2)}, u32[]{:S(2)}) collective-permute-start(bf16[8,120,256]{2,1,0:T(8,128)(2,1)S(1)} %pad_maximum_fusion.6), channel_id=1, source_target_pairs={{0,2},{2,0},{4,6},{6,4},{8,10},{10,8},{12,14},{14,12},{16,18},{18,... | collective-permute-start | bytes 1474568 | tf_op jit(solution)/shard_map/ppermute | solution.py:193
  116.2 3.2 %copy-start.3 = (bf16[128,120,256]{2,1,0:T(8,128)(2,1)S(1)}, bf16[128,120,256]{2,1,0:T(8,128)(2,1)}, u32[]{:S(2)}) copy-start(bf16[128,120,256]{2,1,0:T(8,128)(2,1)} %constant_dynamic-update-slice_fusion.weighted) | copy-start | bytes 23592964
  123.6 4.5 %collective-permute-start.44 = (f32[120,64]{1,0:T(8,128)S(1)}, f32[120,64]{1,0:T(8,128)S(1)}, u32[]{:S(2)}, u32[]{:S(2)}) collective-permute-start(f32[120,64]{1,0:T(8,128)S(1)} %slice_select_fusion), channel_id=1, source_target_pairs={{0,1},{1,0},{2,3},{3,2},{4,5},{5,4},{6,7},{7,6},{8,9},{9,8},{10,11... | collective-permute-start | bytes 92168 | tf_op jit(solution)/shard_map/ppermute | solution.py:118
  (2 other events, 3.0 us)

commit v2 on v1

v2 whole, which is shorter than its diff:
```python
import functools

import jax
import jax.numpy as jnp
from jax import lax
from jax.experimental import pallas as pl
from jax.experimental.pallas import tpu as pltpu
from jax.sharding import PartitionSpec as P

OCC_DEV = 8
GROUP = 4
CHUNKS = 8
KERNEL_VMEM = 28 << 20


def ring_place(chip, chips):
    return jnp.where(chip % 2 == 0, chip // 2, chips - 1 - chip // 2)


def ring_pairs(chips, step):
    order = list(range(0, chips, 2)) + list(range(1, chips, 2))[::-1]
    return [
        (2 * order[k] + core, 2 * order[(k + (step, -step)[core]) % chips] + core)
        for k in range(chips)
        for core in range(2)
    ]


def whole(x):
    return pl.BlockSpec(x.shape, lambda i, *_: (0,) * len(x.shape), pipeline_mode=pl.Buffered(1))


def cost(blocks, tens, rows, more):
    width, depth = tens.shape[1:]
    return pl.CostEstimate(
        flops=2 * blocks * rows * width * depth,
        bytes_accessed=2 * blocks * width * depth + more,
        transcendentals=0,
    )


def sum_cells_kernel(sends, cell, again, tens, coef, *refs):
    out, copied, (blocks, rows_in, totals, arrived) = refs[0], refs[1:-4], refs[-4:]
    block_count = tens.shape[0]
    chunk = block_count // CHUNKS
    copies = [pltpu.make_async_copy(coef, rows_in, arrived.at[CHUNKS])]
    for c in range(CHUNKS):
        part = slice(c * chunk, (c + 1) * chunk)
        copies.append(pltpu.make_async_copy(tens.at[part], blocks.at[part], arrived.at[c]))
    for copy in copies:
        copy.start()
    out[...] = jnp.zeros_like(out)
    copies[0].wait()
    for c in range(CHUNKS):
        copies[1 + c].wait()
        for start in range(c * chunk, (c + 1) * chunk, GROUP):
            halves = [
                lax.dot_general(
                    rows_in[...],
                    blocks[b],
                    (((1,), (1,)), ((), ())),
                    preferred_element_type=jnp.float32,
                )
                for b in range(start, start + GROUP)
            ]
            for b, half in zip(range(start, start + GROUP), halves):
                here = cell[b]
                half = half.astype(jnp.bfloat16).astype(jnp.float32)
                total = jnp.where(again[b] != 0, totals[here] + half, half)
                totals[here] = total
                out[here] = total.astype(jnp.bfloat16)
    for send, copy in zip(sends, copied):
        for k, c in enumerate(send):
            copy[k] = out[c]


def sum_cells(cell, again, tens, coef, cells, sends):
    rows, width = coef.shape[0], tens.shape[1]
    outs = [jax.ShapeDtypeStruct((cells, rows, width), jnp.bfloat16)]
    outs += [jax.ShapeDtypeStruct((len(send), rows, width), jnp.bfloat16) for send in sends]
    hbm = pl.BlockSpec(memory_space=pltpu.HBM)
    return pl.pallas_call(
        functools.partial(sum_cells_kernel, sends),
        out_shape=tuple(outs),
        grid_spec=pltpu.PrefetchScalarGridSpec(
            num_scalar_prefetch=2,
            grid=(1,),
            in_specs=[hbm, hbm],
            out_specs=tuple(whole(out) for out in outs),
            scratch_shapes=[
                pltpu.VMEM(tens.shape, tens.dtype),
                pltpu.VMEM(coef.shape, coef.dtype),
                pltpu.VMEM((cells, rows, width), jnp.float32),
                pltpu.SemaphoreType.DMA((CHUNKS + 1,)),
            ],
        ),
        compiler_params=pltpu.CompilerParams(vmem_limit_bytes=KERNEL_VMEM),
        cost_estimate=cost(tens.shape[0], tens, rows, 2 * cells * rows * width),
        name="sum_cells",
    )(
        cell,
        again,
        pltpu.with_memory_space_constraint(tens, pltpu.HBM),
        pltpu.with_memory_space_constraint(coef, pltpu.HBM),
    )


def apply_cells_kernel(step, sorted_blocks, bounds, order, cell, before, tens, *refs):
    count, first, low, high = step
    pieces, outs, held = refs[:count], refs[count:-1], refs[-1]
    slots = pieces[0].shape[0]
    for p, piece in enumerate(pieces):
        held[p * slots : (p + 1) * slots] = piece[...]
    empty = count * slots
    held[empty] = jnp.zeros(held.shape[1:], held.dtype)
    start, stop, last = bounds[low], bounds[high], order.shape[0] - 1

    def group(g, total):
        for u in range(GROUP):
            k = start + g * GROUP + u
            b = order[jnp.minimum(k, last)]
            here = jnp.where(k < stop, cell[b] - first, empty)
            at = jnp.minimum(k, tens.shape[0] - 1) if sorted_blocks else b
            total = total + jnp.dot(held[here], tens[at], preferred_element_type=jnp.float32)
        return total

    outs[0][...] = lax.fori_loop(0, (stop - start + GROUP - 1) // GROUP, group, before[...])
    if len(outs) > 1:
        for k in range(outs[1].shape[0]):
            outs[1][k] = tens[order[k]]


def apply_cells(step, bounds, order, cell, before, tens, pieces, most, sorted_blocks=False, take=0):
    rows, width = pieces[0].shape[1:]
    cells = len(pieces) * pieces[0].shape[0]
    outs = [jax.ShapeDtypeStruct(before.shape, jnp.float32)]
    if take:
        outs.append(jax.ShapeDtypeStruct((take, *tens.shape[1:]), tens.dtype))
    return pl.pallas_call(
        functools.partial(apply_cells_kernel, (len(pieces), *step), sorted_blocks),
        out_shape=tuple(outs),
        grid_spec=pltpu.PrefetchScalarGridSpec(
            num_scalar_prefetch=3,
            grid=(1,),
            in_specs=[whole(before), whole(tens)] + [whole(piece) for piece in pieces],
            out_specs=tuple(whole(out) for out in outs),
            scratch_shapes=[pltpu.VMEM((cells + 1, rows, width), jnp.bfloat16)],
        ),
        compiler_params=pltpu.CompilerParams(vmem_limit_bytes=KERNEL_VMEM),
        cost_estimate=cost(min(most, tens.shape[0]), tens, rows, 2 * cells * rows * width),
        name="apply_cells",
    )(bounds, order, cell, before, tens, *pieces)


def sum_over_ctr(partial_value):
    if lax.axis_size("ctr") != 2:
        return lax.psum_scatter(partial_value, "ctr", scatter_dimension=1, tiled=True)
    width = partial_value.shape[1] // 2
    low, high = partial_value[:, :width], partial_value[:, width:]
    first = lax.axis_index("ctr") == 0
    mine, other = jnp.where(first, low, high), jnp.where(first, high, low)
    return mine + lax.ppermute(other, "ctr", [(0, 1), (1, 0)])


def cells_body(tens, coef, aux_of, slot_of, metric):
    owners = lax.axis_size("wide")
    chips = owners // 2
    far = chips // 2
    slots = OCC_DEV
    block_count = tens.shape[0]
    me = lax.axis_index("wide")
    core, place = me % 2, ring_place(me // 2, chips)
    forward = functools.partial(lax.ppermute, axis_name="wide", perm=ring_pairs(chips, 1))
    backward = functools.partial(lax.ppermute, axis_name="wide", perm=ring_pairs(chips, -1))
    across = functools.partial(
        lax.ppermute, axis_name="wide", perm=[(k, k ^ 1) for k in range(owners)]
    )

    half_slots = slots // 2
    pieces_of, group_starts = {}, []
    for step in range(far, -1, -1):
        for h in range(2):
            group_starts.append(len(pieces_of))
            for r in sorted({step, (chips - step) % chips}):
                for kind in range(2):
                    pieces_of[r, h, kind] = len(pieces_of)
    group_starts.append(len(pieces_of))
    cells = len(pieces_of) * half_slots

    target = aux_of[:, 0]
    ahead = ring_place(target // 2, chips) - place
    ahead = jnp.where(target % 2 == 0, ahead, -ahead) % chips
    step_of = jnp.minimum(ahead, chips - ahead)
    paired = jnp.where((step_of == 0) | (step_of == far), 0, 1)
    piece = jnp.where(step_of == far, 0, 4 + (far - 1 - step_of) * 8)
    piece += (slot_of // half_slots) * (2 + 2 * paired) + 2 * paired * jnp.where(ahead > far, 1, 0)
    piece += jnp.where(target % 2 == core, 0, 1)
    cell = piece * half_slots + slot_of % half_slots
    series = jnp.arange(block_count)
    key = cell * block_count + series
    rank = jnp.sum(jnp.where(key[None, :] < key[:, None], 1, 0), axis=1)
    order = jnp.sum(jnp.where(rank[None, :] == series[:, None], series[None, :], 0), axis=1)
    limits = jnp.array([start * half_slots for start in group_starts], jnp.int32)
    bounds = jnp.sum(jnp.where(cell[None, :] < limits[:, None], 1, 0), axis=1)

    apart = lax.optimization_barrier
    capacity = 2 * block_count // owners
    same = (cell[None, :] == cell[:, None]) & (series[None, :] < series[:, None])
    again = jnp.sum(jnp.where(same, 1, 0), axis=1)
    sent = [(r, h) for r, h, kind in pieces_of if kind == 1]
    sends = [[], []]
    for r, h in sent:
        start = pieces_of[r, h, 1] * half_slots
        sends[r != far] += range(start, start + half_slots)
    sums, *others = sum_cells(cell, again, tens, coef, cells, sends)
    got = [across(others[0])]
    got[0], others[1] = apart((got[0], others[1]))
    got.append(across(others[1]))
    local = {}
    for k, (r, h) in enumerate(sent):
        start = pieces_of[r, h, 0] * half_slots
        mine = apart(sums[start : start + half_slots])
        start = (k if r == far else k - 2) * half_slots
        other = apart(got[r != far][start : start + half_slots])
        local[r, h] = mine.astype(jnp.float32) + other.astype(jnp.float32)

    def add(value, held):
        return held if value is None else apart(value).astype(jnp.float32) + held

    up, down = [None, None], [None, None]
    for step in range(far, 0, -1):
        for h in range(2):
            if step < far or h == 0:
                up[h] = forward(add(up[h], local[step, h]).astype(jnp.bfloat16))
            if step < far or h == 1:
                down[h] = backward(add(down[h], local[chips - step, h]).astype(jnp.bfloat16))

    own = []
    for h in range(2):
        fitted = add(down[h], add(up[h], local[0, h])).astype(jnp.bfloat16)
        own.append(
            jnp.einsum(
                "sjp,pq->sjq", fitted, metric[0], preferred_element_type=jnp.float32
            ).astype(jnp.bfloat16)
        )

    totals = [jnp.zeros((coef.shape[0], tens.shape[2]), jnp.float32)]
    held = {(0, h): own[h] for h in range(2)}
    up, down = list(own), list(own)

    def apply(step, h, **how):
        pieces = []
        for r in sorted({step, (chips - step) % chips}):
            pieces += [held[r, h], across(held[r, h])]
        group = 2 * (far - step) + h
        total, *more = apply_cells(
            (group_starts[group] * half_slots, group, group + 1),
            bounds,
            order,
            cell,
            totals[-1],
            tens,
            pieces,
            capacity * len(pieces) // 2,
            **how,
        )
        totals.append(total)
        return more

    waiting = [(0, 0), (0, 1)]
    for step in range(1, far + 1):
        for h in range(2):
            if step < far or h == 0:
                up[h] = forward(up[h])
            if step < far or h == 1:
                down[h] = backward(down[h])
        if step == far:
            break
        for h in range(2):
            up[h], down[h], totals[-1] = apart((up[h], down[h], totals[-1]))
            apply(*waiting.pop(0))
            up[h], down[h], totals[-1] = apart((up[h], down[h], totals[-1]))
            held[chips - step, h], held[step, h] = up[h], down[h]
            waiting.append((step, h))
    apply(*waiting.pop(0))
    (taken,) = apply(*waiting.pop(0), take=2 * capacity)
    up[0], down[1], totals[-1], taken = apart((up[0], down[1], totals[-1], taken))
    partial_value, = apply_cells(
        (0, 0, 2),
        bounds,
        order,
        cell,
        totals[-1],
        taken,
        [up[0], across(up[0]), down[1], across(down[1])],
        2 * capacity,
        sorted_blocks=True,
    )
    return sum_over_ctr(partial_value)


def slots_body(tens, coef, aux_of, slot_of, metric):
    owners = lax.axis_size("wide")
    block_count = tens.shape[0]
    capacity = max(2, 2 * block_count // owners)
    total_slots = owners * capacity
    half_form = jnp.einsum("jm,bpm->bjp", coef, tens, preferred_element_type=jnp.float32).astype(
        jnp.bfloat16
    )
    target = aux_of[:, 0]
    series = jnp.arange(block_count)
    matches = target[:, None] == target[None, :]
    earlier = series[None, :] < series[:, None]
    ranking = jnp.sum(jnp.where(matches & earlier, 1, 0), axis=1)
    position = target * capacity + ranking
    selector = position[None, :] == jnp.arange(total_slots)[:, None]
    selector_bf = jnp.where(selector, 1.0, 0.0).astype(jnp.bfloat16)
    outgoing = jnp.einsum(
        "kb,bjp->kjp", selector_bf, half_form, preferred_element_type=jnp.float32
    ).astype(jnp.bfloat16)
    slot_tags = jnp.sum(jnp.where(selector, slot_of[None, :] + 1, 0), axis=1)
    received, tags_in = (
        lax.all_to_all(outgoing, "wide", split_axis=0, concat_axis=0, tiled=True),
        lax.all_to_all(slot_tags, "wide", split_axis=0, concat_axis=0, tiled=True),
    )
    slot_onehot = jnp.where(
        tags_in[None, :] == (jnp.arange(OCC_DEV) + 1)[:, None], 1.0, 0.0
    ).astype(jnp.bfloat16)
    fitted = jnp.einsum(
        "sk,kjp->sjp", slot_onehot, received, preferred_element_type=jnp.float32
    ).astype(jnp.bfloat16)
    weighted = jnp.einsum(
        "sjp,pq->sjq", fitted, metric[0], preferred_element_type=jnp.float32
    ).astype(jnp.bfloat16)
    answers = jnp.einsum(
        "sk,sjq->kjq", slot_onehot, weighted, preferred_element_type=jnp.float32
    ).astype(jnp.bfloat16)
    returned = lax.all_to_all(answers, "wide", split_axis=0, concat_axis=0, tiled=True)
    per_block = jnp.einsum(
        "kb,kjq->bjq", selector_bf, returned, preferred_element_type=jnp.float32
    ).astype(jnp.bfloat16)
    partial_value = jnp.einsum("bjq,bqm->jm", per_block, tens, preferred_element_type=jnp.float32)
    return sum_over_ctr(partial_value)


def body(tens, coef, aux_of, slot_of, metric):
    owners, block_count = lax.axis_size("wide"), tens.shape[0]
    dense = owners * OCC_DEV <= 2 * block_count and owners % 4 == 0
    return (cells_body if dense else slots_body)(tens, coef, aux_of, slot_of, metric)


def solution(mesh):
    placed = (
        P(("wide", "ctr"), None, None),
        P(None, "wide"),
        P(("wide", "ctr"), None),
        P(("wide", "ctr")),
        P("wide", None, None),
    )
    return jax.shard_map(
        body, mesh=mesh, in_specs=placed, out_specs=P(None, ("wide", "ctr")), check_vma=False
    )
```

time: 129 us -> 107 us (0.83)
  local copies, waits for them, and re-layouts: 23.8 us -> 1.24 us
  waiting for transfers between devices: 55.8 us -> 44.5 us
  starting transfers between devices: 35.4 us -> 43.2 us
  Pallas kernels: 8.92 us -> 14.5 us
  matrix products: 1.95 us -> 0.54 us
    unnamed x31 -> x6, local copies, waits for them, and re-layouts: 22 us -> 0.01 us
    ppermute x30 -> x32, waiting for transfers between devices: 33.4 us -> 24.7 us  [the longest x7 19.6 us: cells_body(): backward(add(down[h], local[chips - step, h]).astype(jnp.bfloat16))]
    ppermute x7, starting transfers between devices: 4.11 us -> 10.4 us  [cells_body(): down[h] = backward(down[h])]
    ppermute x30 -> x32, starting transfers between devices: 18 us -> 24 us  [the longest x7 16.8 us: cells_body(): backward(add(down[h], local[chips - step, h]).astype(jnp.bfloat16))]
    pallas_call x2 -> x10, Pallas kernels: 8.92 us -> 14.5 us  [the longest x9 9.87 us: apply_cells(): pl.pallas_call(functools.partial(apply_cells_kernel, (len(pieces), *step)...]
    ppermute x7, starting transfers between devices: 11.7 us -> 7.31 us  [cells_body(): up[h] = forward(up[h])]
    ppermute x7, waiting for transfers between devices: 13.3 us -> 9.22 us  [cells_body(): down[h] = backward(down[h])]
    ppermute x7, waiting for transfers between devices: 6.11 us -> 7.6 us  [cells_body(): up[h] = forward(up[h])]
  transfers between devices with their start and end apart: 45 -> 47, of which waited for: 23 -> 26; matrix products, arithmetic and copies ran while one was open for 14% -> 2% of each run, Pallas kernels for 0% -> 8%
where the time goes in v2:
time: 107 us
  waiting for transfers between devices  44.5 us (42%)
  starting transfers between devices  43.2 us (40%)
  Pallas kernels  14.5 us (14%)
  other arithmetic  2.79 us (3%)
  local copies, waits for them, and re-layouts  1.24 us (1%)
    ppermute x7, waiting for transfers between devices, cells_body(): backward(add(down[h], local[chips - step, h]).astype(jnp.bfloat16))  19.6 us
    ppermute x7, starting transfers between devices, cells_body(): backward(add(down[h], local[chips - step, h]).astype(jnp.bfloat16))  16.8 us
    ppermute x7, starting transfers between devices, cells_body(): down[h] = backward(down[h])  10.4 us
    pallas_call x9, Pallas kernels, apply_cells(): pl.pallas_call(functools.partial(apply_cells_kernel, (len(pieces), *step)...  9.87 us
    ppermute x7, waiting for transfers between devices, cells_body(): down[h] = backward(down[h])  9.22 us
    ppermute x7, waiting for transfers between devices, cells_body(): up[h] = forward(up[h])  7.6 us
    ppermute x7, starting transfers between devices, cells_body(): up[h] = forward(up[h])  7.31 us
    pallas_call x1, Pallas kernels, sum_cells(): pl.pallas_call(functools.partial(sum_cells_kernel, sends), out_shape=tupl...  4.64 us
  transfers between devices with their start and end apart: 47, of which 26 were waited for; matrix products, arithmetic and copies ran while one was open for 2% of the time, Pallas kernels for 8%

profile of v2, /device:TPU:0, one launch (start us, length us, event | category | flops | bytes accessed | tf_op | source)
XLA Modules:
  0.0 107.0 jit_solution(3783789139397799641)
XLA Ops:
  0.9 4.6 %sum_cells.1 = (bf16[128,120,256]{2,1,0:T(8,128)(2,1)S(1)}, bf16[8,120,256]{2,1,0:T(8,128)(2,1)S(1)}, bf16[56,120,256]{2,1,0:T(8,128)(2,1)S(1)}) custom-call(s32[64]{0:T(128)S(1)} %get-tuple-element.100.cell, s32[64]{0:T(128)S(1)} %select_reduce_fusion.again, bf16[64,256,128]{2,1,0:T(8,128)(2,1)} %tens.17, bf16[120,128]{1,0:T(8,128)(2,1)} %coef.1), custom_call_target="tpu_custom_call" | custom-call | flops 503316480 | bytes 12058624 | tf_op jit(solution)/shard_map/sum_cells/pallas_call | solution.py:82
  6.1 1.5 %collective-permute-done = bf16[8,120,256]{2,1,0:T(8,128)(2,1)S(1)} collective-permute-done((bf16[8,120,256]{2,1,0:T(8,128)(2,1)S(1)}, bf16[8,120,256]{2,1,0:T(8,128)(2,1)S(1)}, u32[]{:S(2)}, u32[]{:S(2)}) %collective-permute-start) | collective-permute-done | bytes 491552 | tf_op jit(solution)/shard_map/ppermute | solution.py:216
  8.3 2.7 %collective-permute-start.14 = (bf16[4,120,256]{2,1,0:T(8,128)(2,1)S(1)}, bf16[4,120,256]{2,1,0:T(8,128)(2,1)S(1)}, u32[]{:S(2)}, u32[]{:S(2)}) collective-permute-start(bf16[4,120,256]{2,1,0:T(8,128)(2,1)S(1)} %add_convert_fusion.7), channel_id=1, source_target_pairs={{0,4},{2,10},{8,0},{10,18},{16,8},{18,26},{24,16},{26,30},{28,24},... | collective-permute-start | bytes 737288 | tf_op jit(solution)/shard_map/ppermute | solution.py:236
  11.6 5.4 %collective-permute-done.14 = bf16[4,120,256]{2,1,0:T(8,128)(2,1)S(1)} collective-permute-done((bf16[4,120,256]{2,1,0:T(8,128)(2,1)S(1)}, bf16[4,120,256]{2,1,0:T(8,128)(2,1)S(1)}, u32[]{:S(2)}, u32[]{:S(2)}) %collective-permute-start.14) | collective-permute-done | bytes 245792 | tf_op jit(solution)/shard_map/ppermute | solution.py:236
  17.8 2.0 %collective-permute-start.15 = (bf16[4,120,256]{2,1,0:T(8,128)(2,1)S(1)}, bf16[4,120,256]{2,1,0:T(8,128)(2,1)S(1)}, u32[]{:S(2)}, u32[]{:S(2)}) collective-permute-start(bf16[4,120,256]{2,1,0:T(8,128)(2,1)S(1)} %add_convert_fusion.6), channel_id=1, source_target_pairs={{0,4},{2,10},{8,0},{10,18},{16,8},{18,26},{24,16},{26,30},{28,24},... | collective-permute-start | bytes 737288 | tf_op jit(solution)/shard_map/ppermute | solution.py:236
  20.1 2.0 %collective-permute-start.2 = (bf16[4,120,256]{2,1,0:T(8,128)(2,1)S(1)}, bf16[4,120,256]{2,1,0:T(8,128)(2,1)S(1)}, u32[]{:S(2)}, u32[]{:S(2)}) collective-permute-start(bf16[4,120,256]{2,1,0:T(8,128)(2,1)S(1)} %add_convert_fusion.15), channel_id=1, source_target_pairs={{0,4},{2,10},{8,0},{10,18},{16,8},{18,26},{24,16},{26,30},{28,24},... | collective-permute-start | bytes 737288 | tf_op jit(solution)/shard_map/ppermute | solution.py:236
  22.3 3.8 %collective-permute-done.15 = bf16[4,120,256]{2,1,0:T(8,128)(2,1)S(1)} collective-permute-done((bf16[4,120,256]{2,1,0:T(8,128)(2,1)S(1)}, bf16[4,120,256]{2,1,0:T(8,128)(2,1)S(1)}, u32[]{:S(2)}, u32[]{:S(2)}) %collective-permute-start.15) | collective-permute-done | bytes 245792 | tf_op jit(solution)/shard_map/ppermute | solution.py:236
  26.2 2.5 %collective-permute-start.16 = (bf16[4,120,256]{2,1,0:T(8,128)(2,1)S(1)}, bf16[4,120,256]{2,1,0:T(8,128)(2,1)S(1)}, u32[]{:S(2)}, u32[]{:S(2)}) collective-permute-start(bf16[4,120,256]{2,1,0:T(8,128)(2,1)S(1)} %add_convert_fusion.5), channel_id=1, source_target_pairs={{0,4},{2,10},{8,0},{10,18},{16,8},{18,26},{24,16},{26,30},{28,24},... | collective-permute-start | bytes 737288 | tf_op jit(solution)/shard_map/ppermute | solution.py:236
  29.0 2.4 %collective-permute-done.2 = bf16[4,120,256]{2,1,0:T(8,128)(2,1)S(1)} collective-permute-done((bf16[4,120,256]{2,1,0:T(8,128)(2,1)S(1)}, bf16[4,120,256]{2,1,0:T(8,128)(2,1)S(1)}, u32[]{:S(2)}, u32[]{:S(2)}) %collective-permute-start.2) | collective-permute-done | bytes 245792 | tf_op jit(solution)/shard_map/ppermute | solution.py:236
  31.5 2.5 %collective-permute-start.3 = (bf16[4,120,256]{2,1,0:T(8,128)(2,1)S(1)}, bf16[4,120,256]{2,1,0:T(8,128)(2,1)S(1)}, u32[]{:S(2)}, u32[]{:S(2)}) collective-permute-start(bf16[4,120,256]{2,1,0:T(8,128)(2,1)S(1)} %add_convert_fusion.14), channel_id=1, source_target_pairs={{0,4},{2,10},{8,0},{10,18},{16,8},{18,26},{24,16},{26,30},{28,24},... | collective-permute-start | bytes 737288 | tf_op jit(solution)/shard_map/ppermute | solution.py:236
  34.3 2.4 %collective-permute-done.16 = bf16[4,120,256]{2,1,0:T(8,128)(2,1)S(1)} collective-permute-done((bf16[4,120,256]{2,1,0:T(8,128)(2,1)S(1)}, bf16[4,120,256]{2,1,0:T(8,128)(2,1)S(1)}, u32[]{:S(2)}, u32[]{:S(2)}) %collective-permute-start.16) | collective-permute-done | bytes 245792 | tf_op jit(solution)/shard_map/ppermute | solution.py:236
  36.8 2.5 %collective-permute-start.17 = (bf16[4,120,256]{2,1,0:T(8,128)(2,1)S(1)}, bf16[4,120,256]{2,1,0:T(8,128)(2,1)S(1)}, u32[]{:S(2)}, u32[]{:S(2)}) collective-permute-start(bf16[4,120,256]{2,1,0:T(8,128)(2,1)S(1)} %add_convert_fusion.4), channel_id=1, source_target_pairs={{0,4},{2,10},{8,0},{10,18},{16,8},{18,26},{24,16},{26,30},{28,24},... | collective-permute-start | bytes 737288 | tf_op jit(solution)/shard_map/ppermute | solution.py:236
  39.3 2.1 %collective-permute-done.3 = bf16[4,120,256]{2,1,0:T(8,128)(2,1)S(1)} collective-permute-done((bf16[4,120,256]{2,1,0:T(8,128)(2,1)S(1)}, bf16[4,120,256]{2,1,0:T(8,128)(2,1)S(1)}, u32[]{:S(2)}, u32[]{:S(2)}) %collective-permute-start.3) | collective-permute-done | bytes 245792 | tf_op jit(solution)/shard_map/ppermute | solution.py:236
  41.6 2.5 %collective-permute-start.4 = (bf16[4,120,256]{2,1,0:T(8,128)(2,1)S(1)}, bf16[4,120,256]{2,1,0:T(8,128)(2,1)S(1)}, u32[]{:S(2)}, u32[]{:S(2)}) collective-permute-start(bf16[4,120,256]{2,1,0:T(8,128)(2,1)S(1)} %add_convert_fusion.13), channel_id=1, source_target_pairs={{0,4},{2,10},{8,0},{10,18},{16,8},{18,26},{24,16},{26,30},{28,24},... | collective-permute-start | bytes 737288 | tf_op jit(solution)/shard_map/ppermute | solution.py:236
  45.0 1.9 %collective-permute-start.20 = (bf16[4,120,256]{2,1,0:T(8,128)(2,1)S(1)}, bf16[4,120,256]{2,1,0:T(8,128)(2,1)S(1)}, u32[]{:S(2)}, u32[]{:S(2)}) collective-permute-start(bf16[4,120,256]{2,1,0:T(8,128)(2,1)S(1)} %add_convert_fusion.1), channel_id=1, source_target_pairs={{0,8},{2,6},{8,16},{10,2},{16,24},{18,10},{24,28},{26,18},{28,20},... | collective-permute-start | bytes 737288 | tf_op jit(solution)/shard_map/ppermute | solution.py:234
  46.8 3.6 %collective-permute-done.4 = bf16[4,120,256]{2,1,0:T(8,128)(2,1)S(1)} collective-permute-done((bf16[4,120,256]{2,1,0:T(8,128)(2,1)S(1)}, bf16[4,120,256]{2,1,0:T(8,128)(2,1)S(1)}, u32[]{:S(2)}, u32[]{:S(2)}) %collective-permute-start.4) | collective-permute-done | bytes 245792 | tf_op jit(solution)/shard_map/ppermute | solution.py:236
  51.3 1.9 %collective-permute-start.10 = (bf16[4,120,256]{2,1,0:T(8,128)(2,1)S(1)}, bf16[4,120,256]{2,1,0:T(8,128)(2,1)S(1)}, u32[]{:S(2)}, u32[]{:S(2)}) collective-permute-start(bf16[4,120,256]{2,1,0:T(8,128)(2,1)S(1)} %convolution_convert_fusion.1.refs_0_), channel_id=1, source_target_pairs={{0,4},{2,10},{8,0},{10,18},{16,8},{18,26},{24,16},{26,30},{28,24},... | collective-permute-start | bytes 737288 | tf_op jit(solution)/shard_map/ppermute | solution.py:276
  54.0 0.8 collective-permute-start.21
  54.7 1.9 %collective-permute-start.22 = (bf16[4,120,256]{2,1,0:T(8,128)(2,1)S(1)}, bf16[4,120,256]{2,1,0:T(8,128)(2,1)S(1)}, u32[]{:S(2)}, u32[]{:S(2)}) collective-permute-start(bf16[4,120,256]{2,1,0:T(8,128)(2,1)S(1)} %convolution_convert_fusion.refs_0_), channel_id=1, source_target_pairs={{0,4},{2,10},{8,0},{10,18},{16,8},{18,26},{24,16},{26,30},{28,24},... | collective-permute-start | bytes 737288 | tf_op jit(solution)/shard_map/ppermute | solution.py:276
  56.7 3.2 %collective-permute-done.10.refs_0_ = bf16[4,120,256]{2,1,0:T(8,128)(2,1)S(1)} collective-permute-done((bf16[4,120,256]{2,1,0:T(8,128)(2,1)S(1)}, bf16[4,120,256]{2,1,0:T(8,128)(2,1)S(1)}, u32[]{:S(2)}, u32[]{:S(2)}) %collective-permute-start.10) | collective-permute-done | bytes 245792 | tf_op jit(solution)/shard_map/ppermute | solution.py:276
  60.4 0.8 apply_cells.9.before
  61.2 1.9 %collective-permute-start.12 = (bf16[4,120,256]{2,1,0:T(8,128)(2,1)S(1)}, bf16[4,120,256]{2,1,0:T(8,128)(2,1)S(1)}, u32[]{:S(2)}, u32[]{:S(2)}) collective-permute-start(bf16[4,120,256]{2,1,0:T(8,128)(2,1)S(1)} %collective-permute-done.9.refs_2_), channel_id=1, source_target_pairs={{0,8},{2,6},{8,16},{10,2},{16,24},{18,10},{24,28},{26,18},{28,20},... | collective-permute-start | bytes 737288 | tf_op jit(solution)/shard_map/ppermute | solution.py:274
  63.3 1.4 %collective-permute-done.21.refs_2_ = bf16[4,120,256]{2,1,0:T(8,128)(2,1)S(1)} collective-permute-done((bf16[4,120,256]{2,1,0:T(8,128)(2,1)S(1)}, bf16[4,120,256]{2,1,0:T(8,128)(2,1)S(1)}, u32[]{:S(2)}, u32[]{:S(2)}) %collective-permute-start.21) | collective-permute-done | bytes 245792 | tf_op jit(solution)/shard_map/ppermute | solution.py:274
  64.7 0.9 collective-permute-start.24
  65.6 0.8 apply_cells.10.before
  66.4 1.1 collective-permute-start.28
  67.5 1.7 %collective-permute-done.12.refs_2_ = bf16[4,120,256]{2,1,0:T(8,128)(2,1)S(1)} collective-permute-done((bf16[4,120,256]{2,1,0:T(8,128)(2,1)S(1)}, bf16[4,120,256]{2,1,0:T(8,128)(2,1)S(1)}, u32[]{:S(2)}, u32[]{:S(2)}) %collective-permute-start.12) | collective-permute-done | bytes 245792 | tf_op jit(solution)/shard_map/ppermute | solution.py:274
  69.1 2.6 %collective-permute-start.29 = (bf16[4,120,256]{2,1,0:T(8,128)(2,1)S(1)}, bf16[4,120,256]{2,1,0:T(8,128)(2,1)S(1)}, u32[]{:S(2)}, u32[]{:S(2)}) collective-permute-start(bf16[4,120,256]{2,1,0:T(8,128)(2,1)S(1)} %collective-permute-done.22.refs_0_), channel_id=1, source_target_pairs={{0,4},{2,10},{8,0},{10,18},{16,8},{18,26},{24,16},{26,30},{28,24},... | collective-permute-start | bytes 737288 | tf_op jit(solution)/shard_map/ppermute | solution.py:276
  72.3 1.1 apply_cells.11.before
  73.7 1.8 %collective-permute-start.27 = (bf16[4,120,256]{2,1,0:T(8,128)(2,1)S(1)}, bf16[4,120,256]{2,1,0:T(8,128)(2,1)S(1)}, u32[]{:S(2)}, u32[]{:S(2)}) collective-permute-start(bf16[4,120,256]{2,1,0:T(8,128)(2,1)S(1)} %collective-permute-done.13.refs_0_), channel_id=1, source_target_pairs={{0,4},{2,10},{8,0},{10,18},{16,8},{18,26},{24,16},{26,30},{28,24},... | collective-permute-start | bytes 737288 | tf_op jit(solution)/shard_map/ppermute | solution.py:276
  76.5 1.1 apply_cells.12.before
  77.6 2.0 %collective-permute-start.35 = (bf16[4,120,256]{2,1,0:T(8,128)(2,1)S(1)}, bf16[4,120,256]{2,1,0:T(8,128)(2,1)S(1)}, u32[]{:S(2)}, u32[]{:S(2)}) collective-permute-start(bf16[4,120,256]{2,1,0:T(8,128)(2,1)S(1)} %collective-permute-done.28.refs_2_), channel_id=1, source_target_pairs={{0,8},{2,6},{8,16},{10,2},{16,24},{18,10},{24,28},{26,18},{28,20},... | collective-permute-start | bytes 737288 | tf_op jit(solution)/shard_map/ppermute | solution.py:274
  79.6 2.7 %collective-permute-done.26.refs_2_ = bf16[4,120,256]{2,1,0:T(8,128)(2,1)S(1)} collective-permute-done((bf16[4,120,256]{2,1,0:T(8,128)(2,1)S(1)}, bf16[4,120,256]{2,1,0:T(8,128)(2,1)S(1)}, u32[]{:S(2)}, u32[]{:S(2)}) %collective-permute-start.26) | collective-permute-done | bytes 245792 | tf_op jit(solution)/shard_map/ppermute | solution.py:274
  82.2 1.2 %collective-permute-start.36 = (bf16[4,120,256]{2,1,0:T(8,128)(2,1)S(1)}, bf16[4,120,256]{2,1,0:T(8,128)(2,1)S(1)}, u32[]{:S(2)}, u32[]{:S(2)}) collective-permute-start(bf16[4,120,256]{2,1,0:T(8,128)(2,1)S(1)} %collective-permute-done.29.refs_0_), channel_id=1, source_target_pairs={{0,4},{2,10},{8,0},{10,18},{16,8},{18,26},{24,16},{26,30},{28,24},... | collective-permute-start | bytes 737288 | tf_op jit(solution)/shard_map/ppermute | solution.py:276
  84.0 1.3 %apply_cells.13.before = f32[120,128]{1,0:T(8,128)S(1)} custom-call(s32[11]{0:T(128)S(1)} %select_reduce_fusion.3.bounds, s32[64]{0:T(128)S(1)} %select_reduce_fusion.1.order, s32[64]{0:T(128)S(1)} %get-tuple-element.100.cell, f32[120,128]{1,0:T(8,128)S(1)} %apply_cells.12.before, bf16[64,256,128]{2,1,0:T(8,128)(2,1)S(1)} %copy-done.1, ...), custom_call_target="tpu_custom_call" | custom-call | flops 125829120 | bytes 2031616 | tf_op jit(solution)/shard_map/apply_cells/pallas_call | solution.py:139
  85.3 1.4 %collective-permute-done.35.refs_2_ = bf16[4,120,256]{2,1,0:T(8,128)(2,1)S(1)} collective-permute-done((bf16[4,120,256]{2,1,0:T(8,128)(2,1)S(1)}, bf16[4,120,256]{2,1,0:T(8,128)(2,1)S(1)}, u32[]{:S(2)}, u32[]{:S(2)}) %collective-permute-start.35) | collective-permute-done | bytes 245792 | tf_op jit(solution)/shard_map/ppermute | solution.py:274
  86.8 1.7 %collective-permute-done.36.refs_0_ = bf16[4,120,256]{2,1,0:T(8,128)(2,1)S(1)} collective-permute-done((bf16[4,120,256]{2,1,0:T(8,128)(2,1)S(1)}, bf16[4,120,256]{2,1,0:T(8,128)(2,1)S(1)}, u32[]{:S(2)}, u32[]{:S(2)}) %collective-permute-start.36) | collective-permute-done | bytes 245792 | tf_op jit(solution)/shard_map/ppermute | solution.py:276
  88.5 1.1 %apply_cells.14.before = f32[120,128]{1,0:T(8,128)S(1)} custom-call(s32[11]{0:T(128)S(1)} %select_reduce_fusion.3.bounds, s32[64]{0:T(128)S(1)} %select_reduce_fusion.1.order, s32[64]{0:T(128)S(1)} %get-tuple-element.100.cell, f32[120,128]{1,0:T(8,128)S(1)} %apply_cells.13.before, bf16[64,256,128]{2,1,0:T(8,128)(2,1)S(1)} %copy-done.1, ...), custom_call_target="tpu_custom_call" | custom-call | flops 125829120 | bytes 2031616 | tf_op jit(solution)/shard_map/apply_cells/pallas_call | solution.py:139
  89.5 0.8 collective-permute-start.42
  90.4 0.9 collective-permute-start.39
  91.3 1.1 %collective-permute-start.34 = (bf16[4,120,256]{2,1,0:T(8,128)(2,1)S(1)}, bf16[4,120,256]{2,1,0:T(8,128)(2,1)S(1)}, u32[]{:S(2)}, u32[]{:S(2)}) collective-permute-start(bf16[4,120,256]{2,1,0:T(8,128)(2,1)S(1)} %collective-permute-done.26.refs_2_), channel_id=1, source_target_pairs={{0,8},{2,6},{8,16},{10,2},{16,24},{18,10},{24,28},{26,18},{28,20},... | collective-permute-start | bytes 737288 | tf_op jit(solution)/shard_map/ppermute | solution.py:274
  92.4 1.3 %apply_cells.15.before = f32[120,128]{1,0:T(8,128)S(1)} custom-call(s32[11]{0:T(128)S(1)} %select_reduce_fusion.3.bounds, s32[64]{0:T(128)S(1)} %select_reduce_fusion.1.order, s32[64]{0:T(128)S(1)} %get-tuple-element.100.cell, f32[120,128]{1,0:T(8,128)S(1)} %apply_cells.14.before, bf16[64,256,128]{2,1,0:T(8,128)(2,1)S(1)} %copy-done.1, ...), custom_call_target="tpu_custom_call" | custom-call | flops 125829120 | bytes 2031616 | tf_op jit(solution)/shard_map/apply_cells/pallas_call | solution.py:139
  93.8 1.4 %apply_cells.16 = (f32[120,128]{1,0:T(8,128)S(1)}, bf16[16,256,128]{2,1,0:T(8,128)(2,1)S(1)}) custom-call(s32[11]{0:T(128)S(1)} %select_reduce_fusion.3.bounds, s32[64]{0:T(128)S(1)} %select_reduce_fusion.1.order, s32[64]{0:T(128)S(1)} %get-tuple-element.100.cell, f32[120,128]{1,0:T(8,128)S(1)} %apply_cells.15.before, bf16[64,256,128]{2,1,0:T(8,128)(2,1)S(1)} %copy-done.1, ...), custom_call_target="tpu_custom_call" | custom-call | flops 125829120 | bytes 2031616 | tf_op jit(solution)/shard_map/apply_cells/pallas_call | solution.py:139
  95.1 3.8 %collective-permute-done.39.refs_2_ = bf16[4,120,256]{2,1,0:T(8,128)(2,1)S(1)} collective-permute-done((bf16[4,120,256]{2,1,0:T(8,128)(2,1)S(1)}, bf16[4,120,256]{2,1,0:T(8,128)(2,1)S(1)}, u32[]{:S(2)}, u32[]{:S(2)}) %collective-permute-start.39) | collective-permute-done | bytes 245792 | tf_op jit(solution)/shard_map/ppermute | solution.py:276
  99.4 1.0 collective-permute-done.44.refs_1_
  100.8 1.1 apply_cells.17
  101.9 1.4 %collective-permute-start.46 = (f32[120,64]{1,0:T(8,128)S(1)}, f32[120,64]{1,0:T(8,128)S(1)}, u32[]{:S(2)}, u32[]{:S(2)}) collective-permute-start(f32[120,64]{1,0:T(8,128)S(1)} %slice_select_fusion), channel_id=1, source_target_pairs={{0,1},{1,0},{2,3},{3,2},{4,5},{5,4},{6,7},{7,6},{8,9},{9,8},{10,11... | collective-permute-start | bytes 92168 | tf_op jit(solution)/shard_map/ppermute | solution.py:162
  103.3 2.9 %collective-permute-done.46 = f32[120,64]{1,0:T(8,128)S(1)} collective-permute-done((f32[120,64]{1,0:T(8,128)S(1)}, f32[120,64]{1,0:T(8,128)S(1)}, u32[]{:S(2)}, u32[]{:S(2)}) %collective-permute-start.46) | collective-permute-done | bytes 30752 | tf_op jit(solution)/shard_map/ppermute | solution.py:162
  (90 shorter events, 12.6 us)
Async XLA Ops:
  0.0 51.0 %copy-start = (bf16[1,256,256]{2,1,0:T(8,128)(2,1)S(1)}, bf16[1,256,256]{2,1,0:T(8,128)(2,1)}, u32[]{:S(2)}) copy-start(bf16[1,256,256]{2,1,0:T(8,128)(2,1)} %param.10) | copy-start | bytes 393220
  5.6 2.0 %collective-permute-start = (bf16[8,120,256]{2,1,0:T(8,128)(2,1)S(1)}, bf16[8,120,256]{2,1,0:T(8,128)(2,1)S(1)}, u32[]{:S(2)}, u32[]{:S(2)}) collective-permute-start(bf16[8,120,256]{2,1,0:T(8,128)(2,1)S(1)} %get-tuple-element.53), channel_id=1, source_target_pairs={{0,2},{2,0},{4,6},{6,4},{8,10},{10,8},{12,14},{14,12},{16,18},{18,... | collective-permute-start | bytes 1474568 | tf_op jit(solution)/shard_map/ppermute | solution.py:216
  7.6 9.9 %collective-permute-start.1 = (bf16[56,120,256]{2,1,0:T(8,128)(2,1)S(1)}, bf16[56,120,256]{2,1,0:T(8,128)(2,1)S(1)}, u32[]{:S(2)}, u32[]{:S(2)}) collective-permute-start(bf16[56,120,256]{2,1,0:T(8,128)(2,1)S(1)} %get-tuple-element.55), channel_id=1, source_target_pairs={{0,2},{2,0},{4,6},{6,4},{8,10},{10,8},{12,14},{14,12},{16,18},{18,... | collective-permute-start | bytes 10321928 | tf_op jit(solution)/shard_map/ppermute | solution.py:218
  8.3 8.6 %collective-permute-start.14 = (bf16[4,120,256]{2,1,0:T(8,128)(2,1)S(1)}, bf16[4,120,256]{2,1,0:T(8,128)(2,1)S(1)}, u32[]{:S(2)}, u32[]{:S(2)}) collective-permute-start(bf16[4,120,256]{2,1,0:T(8,128)(2,1)S(1)} %add_convert_fusion.7), channel_id=1, source_target_pairs={{0,4},{2,10},{8,0},{10,18},{16,8},{18,26},{24,16},{26,30},{28,24},... | collective-permute-start | bytes 737288 | tf_op jit(solution)/shard_map/ppermute | solution.py:236
  11.1 6.4 %collective-permute-start.5 = (bf16[4,120,256]{2,1,0:T(8,128)(2,1)S(1)}, bf16[4,120,256]{2,1,0:T(8,128)(2,1)S(1)}, u32[]{:S(2)}, u32[]{:S(2)}) collective-permute-start(bf16[4,120,256]{2,1,0:T(8,128)(2,1)S(1)} %add_convert_fusion.12), channel_id=1, source_target_pairs={{0,8},{2,6},{8,16},{10,2},{16,24},{18,10},{24,28},{26,18},{28,20},... | collective-permute-start | bytes 737288 | tf_op jit(solution)/shard_map/ppermute | solution.py:234
  17.8 8.3 %collective-permute-start.15 = (bf16[4,120,256]{2,1,0:T(8,128)(2,1)S(1)}, bf16[4,120,256]{2,1,0:T(8,128)(2,1)S(1)}, u32[]{:S(2)}, u32[]{:S(2)}) collective-permute-start(bf16[4,120,256]{2,1,0:T(8,128)(2,1)S(1)} %add_convert_fusion.6), channel_id=1, source_target_pairs={{0,4},{2,10},{8,0},{10,18},{16,8},{18,26},{24,16},{26,30},{28,24},... | collective-permute-start | bytes 737288 | tf_op jit(solution)/shard_map/ppermute | solution.py:236
  19.9 8.9 %collective-permute-start.18 = (bf16[4,120,256]{2,1,0:T(8,128)(2,1)S(1)}, bf16[4,120,256]{2,1,0:T(8,128)(2,1)S(1)}, u32[]{:S(2)}, u32[]{:S(2)}) collective-permute-start(bf16[4,120,256]{2,1,0:T(8,128)(2,1)S(1)} %add_convert_fusion.3), channel_id=1, source_target_pairs={{0,8},{2,6},{8,16},{10,2},{16,24},{18,10},{24,28},{26,18},{28,20},... | collective-permute-start | bytes 737288 | tf_op jit(solution)/shard_map/ppermute | solution.py:234
  20.1 11.3 %collective-permute-start.2 = (bf16[4,120,256]{2,1,0:T(8,128)(2,1)S(1)}, bf16[4,120,256]{2,1,0:T(8,128)(2,1)S(1)}, u32[]{:S(2)}, u32[]{:S(2)}) collective-permute-start(bf16[4,120,256]{2,1,0:T(8,128)(2,1)S(1)} %add_convert_fusion.15), channel_id=1, source_target_pairs={{0,4},{2,10},{8,0},{10,18},{16,8},{18,26},{24,16},{26,30},{28,24},... | collective-permute-start | bytes 737288 | tf_op jit(solution)/shard_map/ppermute | solution.py:236
  22.2 11.9 %collective-permute-start.6 = (bf16[4,120,256]{2,1,0:T(8,128)(2,1)S(1)}, bf16[4,120,256]{2,1,0:T(8,128)(2,1)S(1)}, u32[]{:S(2)}, u32[]{:S(2)}) collective-permute-start(bf16[4,120,256]{2,1,0:T(8,128)(2,1)S(1)} %add_convert_fusion.11), channel_id=1, source_target_pairs={{0,8},{2,6},{8,16},{10,2},{16,24},{18,10},{24,28},{26,18},{28,20},... | collective-permute-start | bytes 737288 | tf_op jit(solution)/shard_map/ppermute | solution.py:234
  26.2 10.4 %collective-permute-start.16 = (bf16[4,120,256]{2,1,0:T(8,128)(2,1)S(1)}, bf16[4,120,256]{2,1,0:T(8,128)(2,1)S(1)}, u32[]{:S(2)}, u32[]{:S(2)}) collective-permute-start(bf16[4,120,256]{2,1,0:T(8,128)(2,1)S(1)} %add_convert_fusion.5), channel_id=1, source_target_pairs={{0,4},{2,10},{8,0},{10,18},{16,8},{18,26},{24,16},{26,30},{28,24},... | collective-permute-start | bytes 737288 | tf_op jit(solution)/shard_map/ppermute | solution.py:236
  29.0 15.9 %collective-permute-start.19 = (bf16[4,120,256]{2,1,0:T(8,128)(2,1)S(1)}, bf16[4,120,256]{2,1,0:T(8,128)(2,1)S(1)}, u32[]{:S(2)}, u32[]{:S(2)}) collective-permute-start(bf16[4,120,256]{2,1,0:T(8,128)(2,1)S(1)} %add_convert_fusion.2), channel_id=1, source_target_pairs={{0,8},{2,6},{8,16},{10,2},{16,24},{18,10},{24,28},{26,18},{28,20},... | collective-permute-start | bytes 737288 | tf_op jit(solution)/shard_map/ppermute | solution.py:234
  31.5 9.9 %collective-permute-start.3 = (bf16[4,120,256]{2,1,0:T(8,128)(2,1)S(1)}, bf16[4,120,256]{2,1,0:T(8,128)(2,1)S(1)}, u32[]{:S(2)}, u32[]{:S(2)}) collective-permute-start(bf16[4,120,256]{2,1,0:T(8,128)(2,1)S(1)} %add_convert_fusion.14), channel_id=1, source_target_pairs={{0,4},{2,10},{8,0},{10,18},{16,8},{18,26},{24,16},{26,30},{28,24},... | collective-permute-start | bytes 737288 | tf_op jit(solution)/shard_map/ppermute | solution.py:236
  34.2 10.4 %collective-permute-start.7 = (bf16[4,120,256]{2,1,0:T(8,128)(2,1)S(1)}, bf16[4,120,256]{2,1,0:T(8,128)(2,1)S(1)}, u32[]{:S(2)}, u32[]{:S(2)}) collective-permute-start(bf16[4,120,256]{2,1,0:T(8,128)(2,1)S(1)} %add_convert_fusion.10), channel_id=1, source_target_pairs={{0,8},{2,6},{8,16},{10,2},{16,24},{18,10},{24,28},{26,18},{28,20},... | collective-permute-start | bytes 737288 | tf_op jit(solution)/shard_map/ppermute | solution.py:234
  36.8 16.6 %collective-permute-start.17 = (bf16[4,120,256]{2,1,0:T(8,128)(2,1)S(1)}, bf16[4,120,256]{2,1,0:T(8,128)(2,1)S(1)}, u32[]{:S(2)}, u32[]{:S(2)}) collective-permute-start(bf16[4,120,256]{2,1,0:T(8,128)(2,1)S(1)} %add_convert_fusion.4), channel_id=1, source_target_pairs={{0,4},{2,10},{8,0},{10,18},{16,8},{18,26},{24,16},{26,30},{28,24},... | collective-permute-start | bytes 737288 | tf_op jit(solution)/shard_map/ppermute | solution.py:236
  41.6 8.9 %collective-permute-start.4 = (bf16[4,120,256]{2,1,0:T(8,128)(2,1)S(1)}, bf16[4,120,256]{2,1,0:T(8,128)(2,1)S(1)}, u32[]{:S(2)}, u32[]{:S(2)}) collective-permute-start(bf16[4,120,256]{2,1,0:T(8,128)(2,1)S(1)} %add_convert_fusion.13), channel_id=1, source_target_pairs={{0,4},{2,10},{8,0},{10,18},{16,8},{18,26},{24,16},{26,30},{28,24},... | collective-permute-start | bytes 737288 | tf_op jit(solution)/shard_map/ppermute | solution.py:236
  44.8 6.2 %collective-permute-start.8 = (bf16[4,120,256]{2,1,0:T(8,128)(2,1)S(1)}, bf16[4,120,256]{2,1,0:T(8,128)(2,1)S(1)}, u32[]{:S(2)}, u32[]{:S(2)}) collective-permute-start(bf16[4,120,256]{2,1,0:T(8,128)(2,1)S(1)} %add_convert_fusion.9), channel_id=1, source_target_pairs={{0,8},{2,6},{8,16},{10,2},{16,24},{18,10},{24,28},{26,18},{28,20},... | collective-permute-start | bytes 737288 | tf_op jit(solution)/shard_map/ppermute | solution.py:234
  45.0 8.8 %collective-permute-start.20 = (bf16[4,120,256]{2,1,0:T(8,128)(2,1)S(1)}, bf16[4,120,256]{2,1,0:T(8,128)(2,1)S(1)}, u32[]{:S(2)}, u32[]{:S(2)}) collective-permute-start(bf16[4,120,256]{2,1,0:T(8,128)(2,1)S(1)} %add_convert_fusion.1), channel_id=1, source_target_pairs={{0,8},{2,6},{8,16},{10,2},{16,24},{18,10},{24,28},{26,18},{28,20},... | collective-permute-start | bytes 737288 | tf_op jit(solution)/shard_map/ppermute | solution.py:234
  51.3 8.6 %collective-permute-start.10 = (bf16[4,120,256]{2,1,0:T(8,128)(2,1)S(1)}, bf16[4,120,256]{2,1,0:T(8,128)(2,1)S(1)}, u32[]{:S(2)}, u32[]{:S(2)}) collective-permute-start(bf16[4,120,256]{2,1,0:T(8,128)(2,1)S(1)} %convolution_convert_fusion.1.refs_0_), channel_id=1, source_target_pairs={{0,4},{2,10},{8,0},{10,18},{16,8},{18,26},{24,16},{26,30},{28,24},... | collective-permute-start | bytes 737288 | tf_op jit(solution)/shard_map/ppermute | solution.py:276
  53.2 7.1 %collective-permute-start.9 = (bf16[4,120,256]{2,1,0:T(8,128)(2,1)S(1)}, bf16[4,120,256]{2,1,0:T(8,128)(2,1)S(1)}, u32[]{:S(2)}, u32[]{:S(2)}) collective-permute-start(bf16[4,120,256]{2,1,0:T(8,128)(2,1)S(1)} %convolution_convert_fusion.1.refs_0_), channel_id=1, source_target_pairs={{0,8},{2,6},{8,16},{10,2},{16,24},{18,10},{24,28},{26,18},{28,20},... | collective-permute-start | bytes 737288 | tf_op jit(solution)/shard_map/ppermute | solution.py:274
  53.4 7.0 %collective-permute-start.11 = (bf16[4,120,256]{2,1,0:T(8,128)(2,1)S(1)}, bf16[4,120,256]{2,1,0:T(8,128)(2,1)S(1)}, u32[]{:S(2)}, u32[]{:S(2)}) collective-permute-start(bf16[4,120,256]{2,1,0:T(8,128)(2,1)S(1)} %convolution_convert_fusion.1.refs_0_), channel_id=1, source_target_pairs={{0,2},{2,0},{4,6},{6,4},{8,10},{10,8},{12,14},{14,12},{16,18},{18,... | collective-permute-start | bytes 737288 | tf_op jit(solution)/shard_map/ppermute | solution.py:254
  54.0 10.7 %collective-permute-start.21 = (bf16[4,120,256]{2,1,0:T(8,128)(2,1)S(1)}, bf16[4,120,256]{2,1,0:T(8,128)(2,1)S(1)}, u32[]{:S(2)}, u32[]{:S(2)}) collective-permute-start(bf16[4,120,256]{2,1,0:T(8,128)(2,1)S(1)} %convolution_convert_fusion.refs_0_), channel_id=1, source_target_pairs={{0,8},{2,6},{8,16},{10,2},{16,24},{18,10},{24,28},{26,18},{28,20},... | collective-permute-start | bytes 737288 | tf_op jit(solution)/shard_map/ppermute | solution.py:274
  54.7 10.8 %collective-permute-start.22 = (bf16[4,120,256]{2,1,0:T(8,128)(2,1)S(1)}, bf16[4,120,256]{2,1,0:T(8,128)(2,1)S(1)}, u32[]{:S(2)}, u32[]{:S(2)}) collective-permute-start(bf16[4,120,256]{2,1,0:T(8,128)(2,1)S(1)} %convolution_convert_fusion.refs_0_), channel_id=1, source_target_pairs={{0,4},{2,10},{8,0},{10,18},{16,8},{18,26},{24,16},{26,30},{28,24},... | collective-permute-start | bytes 737288 | tf_op jit(solution)/shard_map/ppermute | solution.py:276
  59.9 5.7 %collective-permute-start.23 = (bf16[4,120,256]{2,1,0:T(8,128)(2,1)S(1)}, bf16[4,120,256]{2,1,0:T(8,128)(2,1)S(1)}, u32[]{:S(2)}, u32[]{:S(2)}) collective-permute-start(bf16[4,120,256]{2,1,0:T(8,128)(2,1)S(1)} %convolution_convert_fusion.refs_0_), channel_id=1, source_target_pairs={{0,2},{2,0},{4,6},{6,4},{8,10},{10,8},{12,14},{14,12},{16,18},{18,... | collective-permute-start | bytes 737288 | tf_op jit(solution)/shard_map/ppermute | solution.py:254
  61.2 7.9 %collective-permute-start.12 = (bf16[4,120,256]{2,1,0:T(8,128)(2,1)S(1)}, bf16[4,120,256]{2,1,0:T(8,128)(2,1)S(1)}, u32[]{:S(2)}, u32[]{:S(2)}) collective-permute-start(bf16[4,120,256]{2,1,0:T(8,128)(2,1)S(1)} %collective-permute-done.9.refs_2_), channel_id=1, source_target_pairs={{0,8},{2,6},{8,16},{10,2},{16,24},{18,10},{24,28},{26,18},{28,20},... | collective-permute-start | bytes 737288 | tf_op jit(solution)/shard_map/ppermute | solution.py:274
  63.2 8.7 %collective-permute-start.13 = (bf16[4,120,256]{2,1,0:T(8,128)(2,1)S(1)}, bf16[4,120,256]{2,1,0:T(8,128)(2,1)S(1)}, u32[]{:S(2)}, u32[]{:S(2)}) collective-permute-start(bf16[4,120,256]{2,1,0:T(8,128)(2,1)S(1)} %collective-permute-done.10.refs_0_), channel_id=1, source_target_pairs={{0,4},{2,10},{8,0},{10,18},{16,8},{18,26},{24,16},{26,30},{28,24},... | collective-permute-start | bytes 737288 | tf_op jit(solution)/shard_map/ppermute | solution.py:276
  64.7 7.1 %collective-permute-start.24 = (bf16[4,120,256]{2,1,0:T(8,128)(2,1)S(1)}, bf16[4,120,256]{2,1,0:T(8,128)(2,1)S(1)}, u32[]{:S(2)}, u32[]{:S(2)}) collective-permute-start(bf16[4,120,256]{2,1,0:T(8,128)(2,1)S(1)} %collective-permute-done.10.refs_0_), channel_id=1, source_target_pairs={{0,2},{2,0},{4,6},{6,4},{8,10},{10,8},{12,14},{14,12},{16,18},{18,... | collective-permute-start | bytes 737288 | tf_op jit(solution)/shard_map/ppermute | solution.py:254
  65.6 6.8 %collective-permute-start.25 = (bf16[4,120,256]{2,1,0:T(8,128)(2,1)S(1)}, bf16[4,120,256]{2,1,0:T(8,128)(2,1)S(1)}, u32[]{:S(2)}, u32[]{:S(2)}) collective-permute-start(bf16[4,120,256]{2,1,0:T(8,128)(2,1)S(1)} %collective-permute-done.9.refs_2_), channel_id=1, source_target_pairs={{0,2},{2,0},{4,6},{6,4},{8,10},{10,8},{12,14},{14,12},{16,18},{18,... | collective-permute-start | bytes 737288 | tf_op jit(solution)/shard_map/ppermute | solution.py:254
  66.4 7.3 %collective-permute-start.28 = (bf16[4,120,256]{2,1,0:T(8,128)(2,1)S(1)}, bf16[4,120,256]{2,1,0:T(8,128)(2,1)S(1)}, u32[]{:S(2)}, u32[]{:S(2)}) collective-permute-start(bf16[4,120,256]{2,1,0:T(8,128)(2,1)S(1)} %collective-permute-done.21.refs_2_), channel_id=1, source_target_pairs={{0,8},{2,6},{8,16},{10,2},{16,24},{18,10},{24,28},{26,18},{28,20},... | collective-permute-start | bytes 737288 | tf_op jit(solution)/shard_map/ppermute | solution.py:274
  69.1 6.9 %collective-permute-start.29 = (bf16[4,120,256]{2,1,0:T(8,128)(2,1)S(1)}, bf16[4,120,256]{2,1,0:T(8,128)(2,1)S(1)}, u32[]{:S(2)}, u32[]{:S(2)}) collective-permute-start(bf16[4,120,256]{2,1,0:T(8,128)(2,1)S(1)} %collective-permute-done.22.refs_0_), channel_id=1, source_target_pairs={{0,4},{2,10},{8,0},{10,18},{16,8},{18,26},{24,16},{26,30},{28,24},... | collective-permute-start | bytes 737288 | tf_op jit(solution)/shard_map/ppermute | solution.py:276
  71.8 4.2 %collective-permute-start.30 = (bf16[4,120,256]{2,1,0:T(8,128)(2,1)S(1)}, bf16[4,120,256]{2,1,0:T(8,128)(2,1)S(1)}, u32[]{:S(2)}, u32[]{:S(2)}) collective-permute-start(bf16[4,120,256]{2,1,0:T(8,128)(2,1)S(1)} %collective-permute-done.22.refs_0_), channel_id=1, source_target_pairs={{0,2},{2,0},{4,6},{6,4},{8,10},{10,8},{12,14},{14,12},{16,18},{18,... | collective-permute-start | bytes 737288 | tf_op jit(solution)/shard_map/ppermute | solution.py:254
  71.8 4.7 %collective-permute-start.31 = (bf16[4,120,256]{2,1,0:T(8,128)(2,1)S(1)}, bf16[4,120,256]{2,1,0:T(8,128)(2,1)S(1)}, u32[]{:S(2)}, u32[]{:S(2)}) collective-permute-start(bf16[4,120,256]{2,1,0:T(8,128)(2,1)S(1)} %collective-permute-done.21.refs_2_), channel_id=1, source_target_pairs={{0,2},{2,0},{4,6},{6,4},{8,10},{10,8},{12,14},{14,12},{16,18},{18,... | collective-permute-start | bytes 737288 | tf_op jit(solution)/shard_map/ppermute | solution.py:254
  73.4 8.8 %collective-permute-start.26 = (bf16[4,120,256]{2,1,0:T(8,128)(2,1)S(1)}, bf16[4,120,256]{2,1,0:T(8,128)(2,1)S(1)}, u32[]{:S(2)}, u32[]{:S(2)}) collective-permute-start(bf16[4,120,256]{2,1,0:T(8,128)(2,1)S(1)} %collective-permute-done.12.refs_2_), channel_id=1, source_target_pairs={{0,8},{2,6},{8,16},{10,2},{16,24},{18,10},{24,28},{26,18},{28,20},... | collective-permute-start | bytes 737288 | tf_op jit(solution)/shard_map/ppermute | solution.py:274
  73.7 9.7 %collective-permute-start.27 = (bf16[4,120,256]{2,1,0:T(8,128)(2,1)S(1)}, bf16[4,120,256]{2,1,0:T(8,128)(2,1)S(1)}, u32[]{:S(2)}, u32[]{:S(2)}) collective-permute-start(bf16[4,120,256]{2,1,0:T(8,128)(2,1)S(1)} %collective-permute-done.13.refs_0_), channel_id=1, source_target_pairs={{0,4},{2,10},{8,0},{10,18},{16,8},{18,26},{24,16},{26,30},{28,24},... | collective-permute-start | bytes 737288 | tf_op jit(solution)/shard_map/ppermute | solution.py:276
  76.0 7.5 %collective-permute-start.32 = (bf16[4,120,256]{2,1,0:T(8,128)(2,1)S(1)}, bf16[4,120,256]{2,1,0:T(8,128)(2,1)S(1)}, u32[]{:S(2)}, u32[]{:S(2)}) collective-permute-start(bf16[4,120,256]{2,1,0:T(8,128)(2,1)S(1)} %collective-permute-done.13.refs_0_), channel_id=1, source_target_pairs={{0,2},{2,0},{4,6},{6,4},{8,10},{10,8},{12,14},{14,12},{16,18},{18,... | collective-permute-start | bytes 737288 | tf_op jit(solution)/shard_map/ppermute | solution.py:254
  76.0 8.0 %collective-permute-start.33 = (bf16[4,120,256]{2,1,0:T(8,128)(2,1)S(1)}, bf16[4,120,256]{2,1,0:T(8,128)(2,1)S(1)}, u32[]{:S(2)}, u32[]{:S(2)}) collective-permute-start(bf16[4,120,256]{2,1,0:T(8,128)(2,1)S(1)} %collective-permute-done.12.refs_2_), channel_id=1, source_target_pairs={{0,2},{2,0},{4,6},{6,4},{8,10},{10,8},{12,14},{14,12},{16,18},{18,... | collective-permute-start | bytes 737288 | tf_op jit(solution)/shard_map/ppermute | solution.py:254
  77.6 9.2 %collective-permute-start.35 = (bf16[4,120,256]{2,1,0:T(8,128)(2,1)S(1)}, bf16[4,120,256]{2,1,0:T(8,128)(2,1)S(1)}, u32[]{:S(2)}, u32[]{:S(2)}) collective-permute-start(bf16[4,120,256]{2,1,0:T(8,128)(2,1)S(1)} %collective-permute-done.28.refs_2_), channel_id=1, source_target_pairs={{0,8},{2,6},{8,16},{10,2},{16,24},{18,10},{24,28},{26,18},{28,20},... | collective-permute-start | bytes 737288 | tf_op jit(solution)/shard_map/ppermute | solution.py:274
  82.2 6.2 %collective-permute-start.36 = (bf16[4,120,256]{2,1,0:T(8,128)(2,1)S(1)}, bf16[4,120,256]{2,1,0:T(8,128)(2,1)S(1)}, u32[]{:S(2)}, u32[]{:S(2)}) collective-permute-start(bf16[4,120,256]{2,1,0:T(8,128)(2,1)S(1)} %collective-permute-done.29.refs_0_), channel_id=1, source_target_pairs={{0,4},{2,10},{8,0},{10,18},{16,8},{18,26},{24,16},{26,30},{28,24},... | collective-permute-start | bytes 737288 | tf_op jit(solution)/shard_map/ppermute | solution.py:276
  83.4 5.0 %collective-permute-start.37 = (bf16[4,120,256]{2,1,0:T(8,128)(2,1)S(1)}, bf16[4,120,256]{2,1,0:T(8,128)(2,1)S(1)}, u32[]{:S(2)}, u32[]{:S(2)}) collective-permute-start(bf16[4,120,256]{2,1,0:T(8,128)(2,1)S(1)} %collective-permute-done.29.refs_0_), channel_id=1, source_target_pairs={{0,2},{2,0},{4,6},{6,4},{8,10},{10,8},{12,14},{14,12},{16,18},{18,... | collective-permute-start | bytes 737288 | tf_op jit(solution)/shard_map/ppermute | solution.py:254
  83.5 5.0 %collective-permute-start.38 = (bf16[4,120,256]{2,1,0:T(8,128)(2,1)S(1)}, bf16[4,120,256]{2,1,0:T(8,128)(2,1)S(1)}, u32[]{:S(2)}, u32[]{:S(2)}) collective-permute-start(bf16[4,120,256]{2,1,0:T(8,128)(2,1)S(1)} %collective-permute-done.28.refs_2_), channel_id=1, source_target_pairs={{0,2},{2,0},{4,6},{6,4},{8,10},{10,8},{12,14},{14,12},{16,18},{18,... | collective-permute-start | bytes 737288 | tf_op jit(solution)/shard_map/ppermute | solution.py:254
  85.3 6.0 %collective-permute-start.40 = (bf16[4,120,256]{2,1,0:T(8,128)(2,1)S(1)}, bf16[4,120,256]{2,1,0:T(8,128)(2,1)S(1)}, u32[]{:S(2)}, u32[]{:S(2)}) collective-permute-start(bf16[4,120,256]{2,1,0:T(8,128)(2,1)S(1)} %collective-permute-done.27.refs_0_), channel_id=1, source_target_pairs={{0,2},{2,0},{4,6},{6,4},{8,10},{10,8},{12,14},{14,12},{16,18},{18,... | collective-permute-start | bytes 737288 | tf_op jit(solution)/shard_map/ppermute | solution.py:254
  88.4 4.0 %collective-permute-start.41 = (bf16[4,120,256]{2,1,0:T(8,128)(2,1)S(1)}, bf16[4,120,256]{2,1,0:T(8,128)(2,1)S(1)}, u32[]{:S(2)}, u32[]{:S(2)}) collective-permute-start(bf16[4,120,256]{2,1,0:T(8,128)(2,1)S(1)} %collective-permute-done.26.refs_2_), channel_id=1, source_target_pairs={{0,2},{2,0},{4,6},{6,4},{8,10},{10,8},{12,14},{14,12},{16,18},{18,... | collective-permute-start | bytes 737288 | tf_op jit(solution)/shard_map/ppermute | solution.py:254
  89.5 4.2 %collective-permute-start.42 = (bf16[4,120,256]{2,1,0:T(8,128)(2,1)S(1)}, bf16[4,120,256]{2,1,0:T(8,128)(2,1)S(1)}, u32[]{:S(2)}, u32[]{:S(2)}) collective-permute-start(bf16[4,120,256]{2,1,0:T(8,128)(2,1)S(1)} %collective-permute-done.36.refs_0_), channel_id=1, source_target_pairs={{0,2},{2,0},{4,6},{6,4},{8,10},{10,8},{12,14},{14,12},{16,18},{18,... | collective-permute-start | bytes 737288 | tf_op jit(solution)/shard_map/ppermute | solution.py:254
  90.3 3.4 %collective-permute-start.43 = (bf16[4,120,256]{2,1,0:T(8,128)(2,1)S(1)}, bf16[4,120,256]{2,1,0:T(8,128)(2,1)S(1)}, u32[]{:S(2)}, u32[]{:S(2)}) collective-permute-start(bf16[4,120,256]{2,1,0:T(8,128)(2,1)S(1)} %collective-permute-done.35.refs_2_), channel_id=1, source_target_pairs={{0,2},{2,0},{4,6},{6,4},{8,10},{10,8},{12,14},{14,12},{16,18},{18,... | collective-permute-start | bytes 737288 | tf_op jit(solution)/shard_map/ppermute | solution.py:254
  90.4 8.5 %collective-permute-start.39 = (bf16[4,120,256]{2,1,0:T(8,128)(2,1)S(1)}, bf16[4,120,256]{2,1,0:T(8,128)(2,1)S(1)}, u32[]{:S(2)}, u32[]{:S(2)}) collective-permute-start(bf16[4,120,256]{2,1,0:T(8,128)(2,1)S(1)} %collective-permute-done.36.refs_0_), channel_id=1, source_target_pairs={{0,4},{2,10},{8,0},{10,18},{16,8},{18,26},{24,16},{26,30},{28,24},... | collective-permute-start | bytes 737288 | tf_op jit(solution)/shard_map/ppermute | solution.py:276
  91.3 7.6 %collective-permute-start.34 = (bf16[4,120,256]{2,1,0:T(8,128)(2,1)S(1)}, bf16[4,120,256]{2,1,0:T(8,128)(2,1)S(1)}, u32[]{:S(2)}, u32[]{:S(2)}) collective-permute-start(bf16[4,120,256]{2,1,0:T(8,128)(2,1)S(1)} %collective-permute-done.26.refs_2_), channel_id=1, source_target_pairs={{0,8},{2,6},{8,16},{10,2},{16,24},{18,10},{24,28},{26,18},{28,20},... | collective-permute-start | bytes 737288 | tf_op jit(solution)/shard_map/ppermute | solution.py:274
  98.9 1.5 %collective-permute-start.44 = (bf16[4,120,256]{2,1,0:T(8,128)(2,1)S(1)}, bf16[4,120,256]{2,1,0:T(8,128)(2,1)S(1)}, u32[]{:S(2)}, u32[]{:S(2)}) collective-permute-start(bf16[4,120,256]{2,1,0:T(8,128)(2,1)S(1)} %collective-permute-done.34.refs_0_), channel_id=1, source_target_pairs={{0,2},{2,0},{4,6},{6,4},{8,10},{10,8},{12,14},{14,12},{16,18},{18,... | collective-permute-start | bytes 737288 | tf_op jit(solution)/shard_map/ppermute | solution.py:295
  98.9 1.9 %collective-permute-start.45 = (bf16[4,120,256]{2,1,0:T(8,128)(2,1)S(1)}, bf16[4,120,256]{2,1,0:T(8,128)(2,1)S(1)}, u32[]{:S(2)}, u32[]{:S(2)}) collective-permute-start(bf16[4,120,256]{2,1,0:T(8,128)(2,1)S(1)} %collective-permute-done.39.refs_2_), channel_id=1, source_target_pairs={{0,2},{2,0},{4,6},{6,4},{8,10},{10,8},{12,14},{14,12},{16,18},{18,... | collective-permute-start | bytes 737288 | tf_op jit(solution)/shard_map/ppermute | solution.py:295
  101.9 4.3 %collective-permute-start.46 = (f32[120,64]{1,0:T(8,128)S(1)}, f32[120,64]{1,0:T(8,128)S(1)}, u32[]{:S(2)}, u32[]{:S(2)}) collective-permute-start(f32[120,64]{1,0:T(8,128)S(1)} %slice_select_fusion), channel_id=1, source_target_pairs={{0,1},{1,0},{2,3},{3,2},{4,5},{5,4},{6,7},{7,6},{8,9},{9,8},{10,11... | collective-permute-start | bytes 92168 | tf_op jit(solution)/shard_map/ppermute | solution.py:162
  (2 other events, 34.9 us)

commit v3 on v2

--- a/solution.py
+++ b/solution.py
@@ -11,6 +11,7 @@
 GROUP = 4
 CHUNKS = 8
 KERNEL_VMEM = 28 << 20
+APPLY_VMEM = 12 << 20
 
 
 def ring_place(chip, chips):
@@ -105,61 +106,72 @@
     )
 
 
-def apply_cells_kernel(step, sorted_blocks, bounds, order, cell, before, tens, *refs):
-    count, first, low, high = step
-    pieces, outs, held = refs[:count], refs[count:-1], refs[-1]
-    slots = pieces[0].shape[0]
-    for p, piece in enumerate(pieces):
-        held[p * slots : (p + 1) * slots] = piece[...]
-    empty = count * slots
+def apply_cells_kernel(group, takes, bounds, order, cell, before, mine, other, first, second, *refs):
+    outs, held = refs[:-1], refs[-1]
+    half = first.shape[0]
+    held[:half], held[half : 2 * half] = first[...], second[...]
+    empty = 2 * half
     held[empty] = jnp.zeros(held.shape[1:], held.dtype)
-    start, stop, last = bounds[low], bounds[high], order.shape[0] - 1
-
-    def group(g, total):
-        for u in range(GROUP):
-            k = start + g * GROUP + u
-            b = order[jnp.minimum(k, last)]
-            here = jnp.where(k < stop, cell[b] - first, empty)
-            at = jnp.minimum(k, tens.shape[0] - 1) if sorted_blocks else b
-            total = total + jnp.dot(held[here], tens[at], preferred_element_type=jnp.float32)
-        return total
-
-    outs[0][...] = lax.fori_loop(0, (stop - start + GROUP - 1) // GROUP, group, before[...])
-    if len(outs) > 1:
-        for k in range(outs[1].shape[0]):
-            outs[1][k] = tens[order[k]]
-
-
-def apply_cells(step, bounds, order, cell, before, tens, pieces, most, sorted_blocks=False, take=0):
+    last = order.shape[1] - 1
+    for d, tens in enumerate((mine, other)):
+        start, stop = bounds[d, group], bounds[d, group + 1]
+
+        def some(g, total):
+            for u in range(GROUP):
+                k = start + g * GROUP + u
+                b = order[d, jnp.minimum(k, last)]
+                here = jnp.where(k < stop, cell[d, b] - 2 * half * group, empty)
+                if tens.shape[0] <= last:
+                    b = jnp.minimum(k, tens.shape[0] - 1)
+                total = total + jnp.dot(held[here], tens[b], preferred_element_type=jnp.float32)
+            return total
+
+        outs[0][d] = lax.fori_loop(0, (stop - start + GROUP - 1) // GROUP, some, before[d])
+        for k in range(takes):
+            outs[1 + d][k] = tens[order[d, k]] if tens.shape[0] > last else tens[k]
+
+
+def apply_cells(group, tables, before, tens, pieces, takes=0):
     rows, width = pieces[0].shape[1:]
-    cells = len(pieces) * pieces[0].shape[0]
     outs = [jax.ShapeDtypeStruct(before.shape, jnp.float32)]
-    if take:
-        outs.append(jax.ShapeDtypeStruct((take, *tens.shape[1:]), tens.dtype))
+    if takes:
+        outs += [jax.ShapeDtypeStruct((takes, *tens[0].shape[1:]), tens[0].dtype)] * 2
+    arrays = [before, *tens, *pieces]
     return pl.pallas_call(
-        functools.partial(apply_cells_kernel, (len(pieces), *step), sorted_blocks),
+        functools.partial(apply_cells_kernel, group, takes),
         out_shape=tuple(outs),
         grid_spec=pltpu.PrefetchScalarGridSpec(
             num_scalar_prefetch=3,
             grid=(1,),
-            in_specs=[whole(before), whole(tens)] + [whole(piece) for piece in pieces],
+            in_specs=[whole(array) for array in arrays],
             out_specs=tuple(whole(out) for out in outs),
-            scratch_shapes=[pltpu.VMEM((cells + 1, rows, width), jnp.bfloat16)],
+            scratch_shapes=[pltpu.VMEM((2 * pieces[0].shape[0] + 1, rows, width), jnp.bfloat16)],
         ),
-        compiler_params=pltpu.CompilerParams(vmem_limit_bytes=KERNEL_VMEM),
-        cost_estimate=cost(min(most, tens.shape[0]), tens, rows, 2 * cells * rows * width),
+        compiler_params=pltpu.CompilerParams(vmem_limit_bytes=APPLY_VMEM),
+        cost_estimate=cost(16, tens[0], rows, 4 * pieces[0].size),
         name="apply_cells",
-    )(bounds, order, cell, before, tens, *pieces)
+    )(*tables, *arrays)
 
 
 def sum_over_ctr(partial_value):
+    return lax.psum_scatter(partial_value, "ctr", scatter_dimension=1, tiled=True)
+
+
+def sum_over_cores_and_ctr(total, owners):
+    cores = [(k, k ^ 1) for k in range(owners)]
     if lax.axis_size("ctr") != 2:
-        return lax.psum_scatter(partial_value, "ctr", scatter_dimension=1, tiled=True)
-    width = partial_value.shape[1] // 2
-    low, high = partial_value[:, :width], partial_value[:, width:]
-    first = lax.axis_index("ctr") == 0
-    mine, other = jnp.where(first, low, high), jnp.where(first, high, low)
-    return mine + lax.ppermute(other, "ctr", [(0, 1), (1, 0)])
+        return sum_over_ctr(total[0] + lax.ppermute(total[1], "wide", cores))
+    width = total.shape[2] // 2
+    low, high = total[:, :, :width], total[:, :, width:]
+    lower = lax.axis_index("ctr") == 0
+    mine, other = jnp.where(lower, low, high), jnp.where(lower, high, low)
+    diagonal = [(2 * a + y, 2 * b + 1 - y) for a, b in cores for y in range(2)]
+    parts = (
+        lax.ppermute(other[0], "ctr", [(0, 1), (1, 0)]),
+        lax.ppermute(other[1], ("wide", "ctr"), diagonal),
+        lax.ppermute(mine[1], "wide", cores),
+    )
+    return (mine[0] + parts[2]) + (parts[0] + parts[1])
 
 
 def cells_body(tens, coef, aux_of, slot_of, metric):
@@ -177,63 +189,67 @@
     )
 
     half_slots = slots // 2
-    pieces_of, group_starts = {}, []
-    for step in range(far, -1, -1):
-        for h in range(2):
-            group_starts.append(len(pieces_of))
-            for r in sorted({step, (chips - step) % chips}):
-                for kind in range(2):
-                    pieces_of[r, h, kind] = len(pieces_of)
-    group_starts.append(len(pieces_of))
-    cells = len(pieces_of) * half_slots
+    long, short = (0, 1), (1, 0)
+    turns = [(long, far)] + [(pair, step) for step in range(far - 1, 0, -1) for pair in (short, long)]
+    groups = [[(far, 0), (far, 1)]]
+    for step in range(far - 1, 0, -1):
+        groups += [[(chips - step, pair[0]), (step, pair[1])] for pair in (long, short)]
+    groups.append([(0, 0), (0, 1)])
+    numbers = {way: k for k, way in enumerate(way for group in groups for way in group)}
+    held_cells = len(numbers) * half_slots
+
+    def cell_of(target, slot):
+        ahead = ring_place(target // 2, chips) - place
+        ahead = jnp.where(target % 2 == 0, ahead, -ahead) % chips
+        step = jnp.minimum(ahead, chips - ahead)
+        half, back = slot // half_slots, jnp.where(ahead < far, 1, 0)
+        between = 2 + (far - 1 - step) * 4 + jnp.where(half == back, 0, 2) + back
+        number = jnp.where(step == far, half, jnp.where(step == 0, 4 * far - 2 + half, between))
+        return number * half_slots + slot % half_slots
 
     target = aux_of[:, 0]
-    ahead = ring_place(target // 2, chips) - place
-    ahead = jnp.where(target % 2 == 0, ahead, -ahead) % chips
-    step_of = jnp.minimum(ahead, chips - ahead)
-    paired = jnp.where((step_of == 0) | (step_of == far), 0, 1)
-    piece = jnp.where(step_of == far, 0, 4 + (far - 1 - step_of) * 8)
-    piece += (slot_of // half_slots) * (2 + 2 * paired) + 2 * paired * jnp.where(ahead > far, 1, 0)
-    piece += jnp.where(target % 2 == core, 0, 1)
-    cell = piece * half_slots + slot_of % half_slots
+    mine_first = jnp.where(target % 2 == core, 0, held_cells)
+    cell = cell_of(target, slot_of) + mine_first
     series = jnp.arange(block_count)
-    key = cell * block_count + series
-    rank = jnp.sum(jnp.where(key[None, :] < key[:, None], 1, 0), axis=1)
-    order = jnp.sum(jnp.where(rank[None, :] == series[:, None], series[None, :], 0), axis=1)
-    limits = jnp.array([start * half_slots for start in group_starts], jnp.int32)
-    bounds = jnp.sum(jnp.where(cell[None, :] < limits[:, None], 1, 0), axis=1)
+    same = (cell[None, :] == cell[:, None]) & (series[None, :] < series[:, None])
+    again = jnp.sum(jnp.where(same, 1, 0), axis=1)
 
     apart = lax.optimization_barrier
     capacity = 2 * block_count // owners
-    same = (cell[None, :] == cell[:, None]) & (series[None, :] < series[:, None])
-    again = jnp.sum(jnp.where(same, 1, 0), axis=1)
-    sent = [(r, h) for r, h, kind in pieces_of if kind == 1]
-    sends = [[], []]
-    for r, h in sent:
-        start = pieces_of[r, h, 1] * half_slots
-        sends[r != far] += range(start, start + half_slots)
-    sums, *others = sum_cells(cell, again, tens, coef, cells, sends)
-    got = [across(others[0])]
-    got[0], others[1] = apart((got[0], others[1]))
-    got.append(across(others[1]))
+    early = [(r, h) for pair, step in turns[:2] for r, h in ((step, pair[0]), (chips - step, pair[1]))]
+    parts = [early, [way for way in numbers if way not in early]]
+    sends = []
+    for part in parts:
+        starts = [held_cells + numbers[way] * half_slots for way in part]
+        sends.append([c for start in starts for c in range(start, start + half_slots)])
+    sums, *others = sum_cells(cell, again, tens, coef, 2 * held_cells, sends)
     local = {}
-    for k, (r, h) in enumerate(sent):
-        start = pieces_of[r, h, 0] * half_slots
-        mine = apart(sums[start : start + half_slots])
-        start = (k if r == far else k - 2) * half_slots
-        other = apart(got[r != far][start : start + half_slots])
-        local[r, h] = mine.astype(jnp.float32) + other.astype(jnp.float32)
+    for p, part in enumerate(parts):
+        got = across(others[p])
+        if p == 0:
+            other_names = across(target * slots + slot_of)
+            got, other_names, *others[1:] = apart((got, other_names, *others[1:]))
+        for k, way in enumerate(part):
+            start = numbers[way] * half_slots
+            mine = apart(sums[start : start + half_slots])
+            other = apart(got[k * half_slots : (k + 1) * half_slots])
+            local[way] = mine.astype(jnp.float32) + other.astype(jnp.float32)
 
     def add(value, held):
-        return held if value is None else apart(value).astype(jnp.float32) + held
-
-    up, down = [None, None], [None, None]
-    for step in range(far, 0, -1):
-        for h in range(2):
-            if step < far or h == 0:
-                up[h] = forward(add(up[h], local[step, h]).astype(jnp.bfloat16))
-            if step < far or h == 1:
-                down[h] = backward(add(down[h], local[chips - step, h]).astype(jnp.bfloat16))
+        return held if value is None else value.astype(jnp.float32) + held
+
+    up, down, sent = [None, None], [None, None], ()
+    for pair, step in turns:
+        ahead, back = up[pair[0]], down[pair[1]]
+        if ahead is not None:
+            ahead, back, *sent = apart((ahead, back, *sent))
+        ahead = add(ahead, local[step, pair[0]]).astype(jnp.bfloat16)
+        back = add(back, local[chips - step, pair[1]]).astype(jnp.bfloat16)
+        sent = (ahead, back)
+        up[pair[0]], down[pair[1]] = forward(ahead), backward(back)
+        if (pair, step) == turns[6]:
+            *sent, tens_out = apart((*sent, tens))
+            other_tens = across(tens_out)
 
     own = []
     for h in range(2):
@@ -244,59 +260,32 @@
             ).astype(jnp.bfloat16)
         )
 
-    totals = [jnp.zeros((coef.shape[0], tens.shape[2]), jnp.float32)]
-    held = {(0, h): own[h] for h in range(2)}
-    up, down = list(own), list(own)
-
-    def apply(step, h, **how):
-        pieces = []
-        for r in sorted({step, (chips - step) % chips}):
-            pieces += [held[r, h], across(held[r, h])]
-        group = 2 * (far - step) + h
-        total, *more = apply_cells(
-            (group_starts[group] * half_slots, group, group + 1),
-            bounds,
-            order,
-            cell,
-            totals[-1],
-            tens,
-            pieces,
-            capacity * len(pieces) // 2,
-            **how,
-        )
-        totals.append(total)
-        return more
-
-    waiting = [(0, 0), (0, 1)]
-    for step in range(1, far + 1):
-        for h in range(2):
-            if step < far or h == 0:
-                up[h] = forward(up[h])
-            if step < far or h == 1:
-                down[h] = backward(down[h])
-        if step == far:
-            break
-        for h in range(2):
-            up[h], down[h], totals[-1] = apart((up[h], down[h], totals[-1]))
-            apply(*waiting.pop(0))
-            up[h], down[h], totals[-1] = apart((up[h], down[h], totals[-1]))
-            held[chips - step, h], held[step, h] = up[h], down[h]
-            waiting.append((step, h))
-    apply(*waiting.pop(0))
-    (taken,) = apply(*waiting.pop(0), take=2 * capacity)
-    up[0], down[1], totals[-1], taken = apart((up[0], down[1], totals[-1], taken))
-    partial_value, = apply_cells(
-        (0, 0, 2),
-        bounds,
-        order,
-        cell,
-        totals[-1],
-        taken,
-        [up[0], across(up[0]), down[1], across(down[1])],
-        2 * capacity,
-        sorted_blocks=True,
-    )
-    return sum_over_ctr(partial_value)
+    tables = []
+    for aux, slot in ((target, slot_of), (other_names // slots, other_names % slots)):
+        held = jnp.where(aux % 2 == core, cell_of(aux, slot), held_cells)
+        key = held * block_count + series
+        rank = jnp.sum(jnp.where(key[None, :] < key[:, None], 1, 0), axis=1)
+        order = jnp.sum(jnp.where(rank[None, :] == series[:, None], series[None, :], 0), axis=1)
+        limits = jnp.arange(len(groups) + 1) * 2 * half_slots
+        tables.append((jnp.sum(jnp.where(held[None, :] < limits[:, None], 1, 0), axis=1), order, held))
+    tables = [jnp.stack(table) for table in zip(*tables)]
+
+    both = (tens, other_tens)
+    total = jnp.zeros((2, coef.shape[0], tens.shape[2]), jnp.float32)
+    up, down = [forward(own[h]) for h in range(2)], [backward(own[h]) for h in range(2)]
+    uses = [(pair, step) for step in range(1, far) for pair in (long, short)]
+    total, *taken = apply_cells(len(groups) - 1, tables, total, both, own, 0 if uses else capacity)
+    for pair, step in uses:
+        ahead, back = up[pair[0]], down[pair[1]]
+        ahead, back, total = apart((ahead, back, total))
+        if step + 1 < far or pair == long:
+            up[pair[0]], down[pair[1]] = forward(ahead), backward(back)
+        group = groups.index([(chips - step, pair[0]), (step, pair[1])])
+        takes = capacity if (pair, step) == uses[-1] else 0
+        total, *more = apply_cells(group, tables, total, both, [ahead, back], takes)
+        taken = more or taken
+    (total,) = apply_cells(0, tables, total, taken, [up[0], down[1]])
+    return sum_over_cores_and_ctr(total, owners)
 
 
 def slots_body(tens, coef, aux_of, slot_of, metric):

time: 107 us -> 101 us (0.944)
  starting transfers between devices: 43.2 us -> 34.9 us
  local copies, waits for them, and re-layouts: 1.24 us -> 5.63 us
  waiting for transfers between devices: 44.5 us -> 41.5 us
    ppermute x47 -> x35, starting transfers between devices: 43.2 us -> 34.9 us  [the longest x24 27.4 us: cells_body(): up[pair[0]], down[pair[1]] = (forward(ahead), backward(back))]
    unnamed x6 -> x10, local copies, waits for them, and re-layouts: 0.01 us -> 4.39 us
    ppermute x47 -> x35, waiting for transfers between devices: 44.5 us -> 41.5 us  [the longest x24 31.7 us: cells_body(): up[pair[0]], down[pair[1]] = (forward(ahead), backward(back))]
    pallas_call x9 -> x8, Pallas kernels: 9.87 us -> 9.78 us  [apply_cells(): pl.pallas_call(functools.partial(apply_cells_kernel, group, takes), out_s...]
  transfers between devices with their start and end apart: 47 -> 35, of which waited for: 26 -> 24; matrix products, arithmetic and copies ran while one was open for 2% -> 3% of each run, Pallas kernels for 8% -> 9%
where the time goes in v3:
time: 101 us; the launch traced here: 100 us
  waiting for transfers between devices  41.5 us (41%)
  starting transfers between devices  34.9 us (35%)
  Pallas kernels  14.4 us (14%)
  local copies, waits for them, and re-layouts  5.63 us (6%)
  other arithmetic  3.13 us (3%)
    ppermute x24, waiting for transfers between devices, cells_body(): up[pair[0]], down[pair[1]] = (forward(ahead), backward(back))  31.7 us
    ppermute x24, starting transfers between devices, cells_body(): up[pair[0]], down[pair[1]] = (forward(ahead), backward(back))  27.4 us
    pallas_call x8, Pallas kernels, apply_cells(): pl.pallas_call(functools.partial(apply_cells_kernel, group, takes), out_s...  9.78 us
    pallas_call x1, Pallas kernels, sum_cells(): pl.pallas_call(functools.partial(sum_cells_kernel, sends), out_shape=tupl...  4.63 us
    unnamed x10, local copies, waits for them, and re-layouts  4.39 us
    ppermute x2, waiting for transfers between devices, cells_body(): backward(own[h])  4.36 us
    ppermute x2, starting transfers between devices, cells_body(): backward(own[h])  2.94 us
    ppermute x1, waiting for transfers between devices, cells_body(): other_names = across(target * slots + slot_of)  2.11 us
  transfers between devices with their start and end apart: 35, of which 24 were waited for; matrix products, arithmetic and copies ran while one was open for 3% of the time, Pallas kernels for 9%

profile of v3, /device:TPU:0, one launch (start us, length us, event | category | flops | bytes accessed | tf_op | source)
XLA Modules:
  0.0 100.5 jit_solution(15117737220609660359)
XLA Ops:
  0.0 0.7 iota_add_fusion.1
  0.9 4.6 %sum_cells.1 = (bf16[128,120,256]{2,1,0:T(8,128)(2,1)S(1)}, bf16[16,120,256]{2,1,0:T(8,128)(2,1)S(1)}, bf16[48,120,256]{2,1,0:T(8,128)(2,1)S(1)}) custom-call(s32[64]{0:T(128)S(1)} %fusion.7.cell, s32[64]{0:T(128)S(1)} %select_reduce_fusion.4.again, bf16[64,256,128]{2,1,0:T(8,128)(2,1)} %mine.13, bf16[120,128]{1,0:T(8,128)(2,1)} %coef.1), custom_call_target="tpu_custom_call" | custom-call | flops 503316480 | bytes 12058624 | tf_op jit(solution)/shard_map/sum_cells/pallas_call | solution.py:83
  6.2 2.1 %collective-permute-done.1 = s32[64]{0:T(128)S(1)} collective-permute-done((s32[64]{0:T(128)S(1)}, s32[64]{0:T(128)S(1)}, u32[]{:S(2)}, u32[]{:S(2)}) %collective-permute-start.1) | collective-permute-done | bytes 288 | tf_op jit(solution)/shard_map/ppermute | solution.py:230
  9.1 2.7 %collective-permute-start.3 = (bf16[4,120,256]{2,1,0:T(8,128)(2,1)S(1)}, bf16[4,120,256]{2,1,0:T(8,128)(2,1)S(1)}, u32[]{:S(2)}, u32[]{:S(2)}) collective-permute-start(bf16[4,120,256]{2,1,0:T(8,128)(2,1)S(1)} %add_convert_fusion.14), channel_id=1, source_target_pairs={{0,4},{2,10},{8,0},{10,18},{16,8},{18,26},{24,16},{26,30},{28,24},... | collective-permute-start | bytes 737288 | tf_op jit(solution)/shard_map/ppermute | solution.py:249
  12.0 2.0 %collective-permute-start.8 = (bf16[4,120,256]{2,1,0:T(8,128)(2,1)S(1)}, bf16[4,120,256]{2,1,0:T(8,128)(2,1)S(1)}, u32[]{:S(2)}, u32[]{:S(2)}) collective-permute-start(bf16[4,120,256]{2,1,0:T(8,128)(2,1)S(1)} %add_convert_fusion.12), channel_id=1, source_target_pairs={{0,4},{2,10},{8,0},{10,18},{16,8},{18,26},{24,16},{26,30},{28,24},... | collective-permute-start | bytes 737288 | tf_op jit(solution)/shard_map/ppermute | solution.py:249
  14.2 3.8 %collective-permute-done.3 = bf16[4,120,256]{2,1,0:T(8,128)(2,1)S(1)} collective-permute-done((bf16[4,120,256]{2,1,0:T(8,128)(2,1)S(1)}, bf16[4,120,256]{2,1,0:T(8,128)(2,1)S(1)}, u32[]{:S(2)}, u32[]{:S(2)}) %collective-permute-start.3) | collective-permute-done | bytes 245792 | tf_op jit(solution)/shard_map/ppermute | solution.py:249
  18.0 2.7 %collective-permute-done.2 = bf16[4,120,256]{2,1,0:T(8,128)(2,1)S(1)} collective-permute-done((bf16[4,120,256]{2,1,0:T(8,128)(2,1)S(1)}, bf16[4,120,256]{2,1,0:T(8,128)(2,1)S(1)}, u32[]{:S(2)}, u32[]{:S(2)}) %collective-permute-start.2) | collective-permute-done | bytes 245792 | tf_op jit(solution)/shard_map/ppermute | solution.py:249
  21.1 1.6 %collective-permute-start.6 = (bf16[4,120,256]{2,1,0:T(8,128)(2,1)S(1)}, bf16[4,120,256]{2,1,0:T(8,128)(2,1)S(1)}, u32[]{:S(2)}, u32[]{:S(2)}) collective-permute-start(bf16[4,120,256]{2,1,0:T(8,128)(2,1)S(1)} %add_convert_fusion.10), channel_id=1, source_target_pairs={{0,4},{2,10},{8,0},{10,18},{16,8},{18,26},{24,16},{26,30},{28,24},... | collective-permute-start | bytes 737288 | tf_op jit(solution)/shard_map/ppermute | solution.py:249
  24.0 3.6 %collective-permute-start.12 = (bf16[4,120,256]{2,1,0:T(8,128)(2,1)S(1)}, bf16[4,120,256]{2,1,0:T(8,128)(2,1)S(1)}, u32[]{:S(2)}, u32[]{:S(2)}) collective-permute-start(bf16[4,120,256]{2,1,0:T(8,128)(2,1)S(1)} %add_convert_fusion.8), channel_id=1, source_target_pairs={{0,4},{2,10},{8,0},{10,18},{16,8},{18,26},{24,16},{26,30},{28,24},... | collective-permute-start | bytes 737288 | tf_op jit(solution)/shard_map/ppermute | solution.py:249
  27.8 2.1 %collective-permute-done.6 = bf16[4,120,256]{2,1,0:T(8,128)(2,1)S(1)} collective-permute-done((bf16[4,120,256]{2,1,0:T(8,128)(2,1)S(1)}, bf16[4,120,256]{2,1,0:T(8,128)(2,1)S(1)}, u32[]{:S(2)}, u32[]{:S(2)}) %collective-permute-start.6) | collective-permute-done | bytes 245792 | tf_op jit(solution)/shard_map/ppermute | solution.py:249
  29.8 1.5 %collective-permute-done.5 = bf16[4,120,256]{2,1,0:T(8,128)(2,1)S(1)} collective-permute-done((bf16[4,120,256]{2,1,0:T(8,128)(2,1)S(1)}, bf16[4,120,256]{2,1,0:T(8,128)(2,1)S(1)}, u32[]{:S(2)}, u32[]{:S(2)}) %collective-permute-start.5) | collective-permute-done | bytes 245792 | tf_op jit(solution)/shard_map/ppermute | solution.py:249
  31.5 2.0 %collective-permute-start.10 = (bf16[4,120,256]{2,1,0:T(8,128)(2,1)S(1)}, bf16[4,120,256]{2,1,0:T(8,128)(2,1)S(1)}, u32[]{:S(2)}, u32[]{:S(2)}) collective-permute-start(bf16[4,120,256]{2,1,0:T(8,128)(2,1)S(1)} %add_convert_fusion.6), channel_id=1, source_target_pairs={{0,4},{2,10},{8,0},{10,18},{16,8},{18,26},{24,16},{26,30},{28,24},... | collective-permute-start | bytes 737288 | tf_op jit(solution)/shard_map/ppermute | solution.py:249
  33.7 1.4 %collective-permute-done.12 = bf16[4,120,256]{2,1,0:T(8,128)(2,1)S(1)} collective-permute-done((bf16[4,120,256]{2,1,0:T(8,128)(2,1)S(1)}, bf16[4,120,256]{2,1,0:T(8,128)(2,1)S(1)}, u32[]{:S(2)}, u32[]{:S(2)}) %collective-permute-start.12) | collective-permute-done | bytes 245792 | tf_op jit(solution)/shard_map/ppermute | solution.py:249
  35.1 1.3 %collective-permute-done.11 = bf16[4,120,256]{2,1,0:T(8,128)(2,1)S(1)} collective-permute-done((bf16[4,120,256]{2,1,0:T(8,128)(2,1)S(1)}, bf16[4,120,256]{2,1,0:T(8,128)(2,1)S(1)}, u32[]{:S(2)}, u32[]{:S(2)}) %collective-permute-start.11) | collective-permute-done | bytes 245792 | tf_op jit(solution)/shard_map/ppermute | solution.py:249
  36.6 3.6 %collective-permute-done.10 = bf16[4,120,256]{2,1,0:T(8,128)(2,1)S(1)} collective-permute-done((bf16[4,120,256]{2,1,0:T(8,128)(2,1)S(1)}, bf16[4,120,256]{2,1,0:T(8,128)(2,1)S(1)}, u32[]{:S(2)}, u32[]{:S(2)}) %collective-permute-start.10) | collective-permute-done | bytes 245792 | tf_op jit(solution)/shard_map/ppermute | solution.py:249
  40.8 1.2 %collective-permute-start.16 = (bf16[4,120,256]{2,1,0:T(8,128)(2,1)S(1)}, bf16[4,120,256]{2,1,0:T(8,128)(2,1)S(1)}, u32[]{:S(2)}, u32[]{:S(2)}) collective-permute-start(bf16[4,120,256]{2,1,0:T(8,128)(2,1)S(1)} %add_convert_fusion.4), channel_id=1, source_target_pairs={{0,4},{2,10},{8,0},{10,18},{16,8},{18,26},{24,16},{26,30},{28,24},... | collective-permute-start | bytes 737288 | tf_op jit(solution)/shard_map/ppermute | solution.py:249
  42.0 0.9 collective-permute-start.17
  43.3 1.4 %collective-permute-start.14 = (bf16[4,120,256]{2,1,0:T(8,128)(2,1)S(1)}, bf16[4,120,256]{2,1,0:T(8,128)(2,1)S(1)}, u32[]{:S(2)}, u32[]{:S(2)}) collective-permute-start(bf16[4,120,256]{2,1,0:T(8,128)(2,1)S(1)} %add_convert_fusion.5), channel_id=1, source_target_pairs={{0,8},{2,6},{8,16},{10,2},{16,24},{18,10},{24,28},{26,18},{28,20},... | collective-permute-start | bytes 737288 | tf_op jit(solution)/shard_map/ppermute | solution.py:249
  44.7 0.7 collective-permute-start.13
  45.4 4.2 %collective-permute-done.16 = bf16[4,120,256]{2,1,0:T(8,128)(2,1)S(1)} collective-permute-done((bf16[4,120,256]{2,1,0:T(8,128)(2,1)S(1)}, bf16[4,120,256]{2,1,0:T(8,128)(2,1)S(1)}, u32[]{:S(2)}, u32[]{:S(2)}) %collective-permute-start.16) | collective-permute-done | bytes 245792 | tf_op jit(solution)/shard_map/ppermute | solution.py:249
  49.6 1.3 %collective-permute-done.17 = bf16[4,120,256]{2,1,0:T(8,128)(2,1)S(1)} collective-permute-done((bf16[4,120,256]{2,1,0:T(8,128)(2,1)S(1)}, bf16[4,120,256]{2,1,0:T(8,128)(2,1)S(1)}, u32[]{:S(2)}, u32[]{:S(2)}) %collective-permute-start.17) | collective-permute-done | bytes 245792 | tf_op jit(solution)/shard_map/ppermute | solution.py:249
  51.2 1.0 collective-permute-start.19
  52.1 2.4 %collective-permute-done.14 = bf16[4,120,256]{2,1,0:T(8,128)(2,1)S(1)} collective-permute-done((bf16[4,120,256]{2,1,0:T(8,128)(2,1)S(1)}, bf16[4,120,256]{2,1,0:T(8,128)(2,1)S(1)}, u32[]{:S(2)}, u32[]{:S(2)}) %collective-permute-start.14) | collective-permute-done | bytes 245792 | tf_op jit(solution)/shard_map/ppermute | solution.py:249
  55.1 1.2 %collective-permute-start.20 = (bf16[4,120,256]{2,1,0:T(8,128)(2,1)S(1)}, bf16[4,120,256]{2,1,0:T(8,128)(2,1)S(1)}, u32[]{:S(2)}, u32[]{:S(2)}) collective-permute-start(bf16[4,120,256]{2,1,0:T(8,128)(2,1)S(1)} %convolution_convert_fusion.1.second), channel_id=1, source_target_pairs={{0,4},{2,10},{8,0},{10,18},{16,8},{18,26},{24,16},{26,30},{28,24},... | collective-permute-start | bytes 737288 | tf_op jit(solution)/shard_map/ppermute | solution.py:275
  56.4 1.8 %collective-permute-start.18 = (bf16[4,120,256]{2,1,0:T(8,128)(2,1)S(1)}, bf16[4,120,256]{2,1,0:T(8,128)(2,1)S(1)}, u32[]{:S(2)}, u32[]{:S(2)}) collective-permute-start(bf16[4,120,256]{2,1,0:T(8,128)(2,1)S(1)} %convolution_convert_fusion.first), channel_id=1, source_target_pairs={{0,4},{2,10},{8,0},{10,18},{16,8},{18,26},{24,16},{26,30},{28,24},... | collective-permute-start | bytes 737288 | tf_op jit(solution)/shard_map/ppermute | solution.py:275
  58.5 1.1 %apply_cells.8.before = f32[2,120,128]{2,1,0:T(8,128)S(1)} custom-call(s32[2,9]{1,0:T(2,128)S(1)} %pad_add_fusion.bounds, s32[2,64]{1,0:T(2,128)S(1)} %get-tuple-element.126.order, s32[2,64]{1,0:T(2,128)S(1)} %get-tuple-element.127.cell, f32[2,120,128]{2,1,0:T(8,128)S(1)} %broadcast_in_dim.87.before, bf16[64,256,128]{2,1,0:T(8,128)(2,1)S(1)} %copy-done.1, ...), custom_call_target="tpu_custom_call" | custom-call | flops 125829120 | bytes 1540096 | tf_op jit(solution)/shard_map/apply_cells/pallas_call | solution.py:140
  59.6 2.5 %collective-permute-done.20.second = bf16[4,120,256]{2,1,0:T(8,128)(2,1)S(1)} collective-permute-done((bf16[4,120,256]{2,1,0:T(8,128)(2,1)S(1)}, bf16[4,120,256]{2,1,0:T(8,128)(2,1)S(1)}, u32[]{:S(2)}, u32[]{:S(2)}) %collective-permute-start.20) | collective-permute-done | bytes 245792 | tf_op jit(solution)/shard_map/ppermute | solution.py:275
  62.7 1.5 %collective-permute-start.25 = (bf16[4,120,256]{2,1,0:T(8,128)(2,1)S(1)}, bf16[4,120,256]{2,1,0:T(8,128)(2,1)S(1)}, u32[]{:S(2)}, u32[]{:S(2)}) collective-permute-start(bf16[4,120,256]{2,1,0:T(8,128)(2,1)S(1)} %collective-permute-done.20.second), channel_id=1, source_target_pairs={{0,4},{2,10},{8,0},{10,18},{16,8},{18,26},{24,16},{26,30},{28,24},... | collective-permute-start | bytes 737288 | tf_op jit(solution)/shard_map/ppermute | solution.py:282
  64.2 1.3 %apply_cells.9.before = f32[2,120,128]{2,1,0:T(8,128)S(1)} custom-call(s32[2,9]{1,0:T(2,128)S(1)} %pad_add_fusion.bounds, s32[2,64]{1,0:T(2,128)S(1)} %get-tuple-element.126.order, s32[2,64]{1,0:T(2,128)S(1)} %get-tuple-element.127.cell, f32[2,120,128]{2,1,0:T(8,128)S(1)} %apply_cells.8.before, bf16[64,256,128]{2,1,0:T(8,128)(2,1)S(1)} %copy-done.1, ...), custom_call_target="tpu_custom_call" | custom-call | flops 125829120 | bytes 1540096 | tf_op jit(solution)/shard_map/apply_cells/pallas_call | solution.py:140
  65.5 1.9 %collective-permute-done.18.second = bf16[4,120,256]{2,1,0:T(8,128)(2,1)S(1)} collective-permute-done((bf16[4,120,256]{2,1,0:T(8,128)(2,1)S(1)}, bf16[4,120,256]{2,1,0:T(8,128)(2,1)S(1)}, u32[]{:S(2)}, u32[]{:S(2)}) %collective-permute-start.18) | collective-permute-done | bytes 245792 | tf_op jit(solution)/shard_map/ppermute | solution.py:275
  68.0 1.5 %collective-permute-start.23 = (bf16[4,120,256]{2,1,0:T(8,128)(2,1)S(1)}, bf16[4,120,256]{2,1,0:T(8,128)(2,1)S(1)}, u32[]{:S(2)}, u32[]{:S(2)}) collective-permute-start(bf16[4,120,256]{2,1,0:T(8,128)(2,1)S(1)} %collective-permute-done.18.second), channel_id=1, source_target_pairs={{0,4},{2,10},{8,0},{10,18},{16,8},{18,26},{24,16},{26,30},{28,24},... | collective-permute-start | bytes 737288 | tf_op jit(solution)/shard_map/ppermute | solution.py:282
  69.5 1.1 %apply_cells.10.before = f32[2,120,128]{2,1,0:T(8,128)S(1)} custom-call(s32[2,9]{1,0:T(2,128)S(1)} %pad_add_fusion.bounds, s32[2,64]{1,0:T(2,128)S(1)} %get-tuple-element.126.order, s32[2,64]{1,0:T(2,128)S(1)} %get-tuple-element.127.cell, f32[2,120,128]{2,1,0:T(8,128)S(1)} %apply_cells.9.before, bf16[64,256,128]{2,1,0:T(8,128)(2,1)S(1)} %copy-done.1, ...), custom_call_target="tpu_custom_call" | custom-call | flops 125829120 | bytes 1540096 | tf_op jit(solution)/shard_map/apply_cells/pallas_call | solution.py:140
  70.6 1.8 %collective-permute-done.24.first = bf16[4,120,256]{2,1,0:T(8,128)(2,1)S(1)} collective-permute-done((bf16[4,120,256]{2,1,0:T(8,128)(2,1)S(1)}, bf16[4,120,256]{2,1,0:T(8,128)(2,1)S(1)}, u32[]{:S(2)}, u32[]{:S(2)}) %collective-permute-start.24) | collective-permute-done | bytes 245792 | tf_op jit(solution)/shard_map/ppermute | solution.py:282
  72.6 1.8 %collective-permute-start.28 = (bf16[4,120,256]{2,1,0:T(8,128)(2,1)S(1)}, bf16[4,120,256]{2,1,0:T(8,128)(2,1)S(1)}, u32[]{:S(2)}, u32[]{:S(2)}) collective-permute-start(bf16[4,120,256]{2,1,0:T(8,128)(2,1)S(1)} %collective-permute-done.24.first), channel_id=1, source_target_pairs={{0,8},{2,6},{8,16},{10,2},{16,24},{18,10},{24,28},{26,18},{28,20},... | collective-permute-start | bytes 737288 | tf_op jit(solution)/shard_map/ppermute | solution.py:282
  74.7 1.3 %apply_cells.11.before = f32[2,120,128]{2,1,0:T(8,128)S(1)} custom-call(s32[2,9]{1,0:T(2,128)S(1)} %pad_add_fusion.bounds, s32[2,64]{1,0:T(2,128)S(1)} %get-tuple-element.126.order, s32[2,64]{1,0:T(2,128)S(1)} %get-tuple-element.127.cell, f32[2,120,128]{2,1,0:T(8,128)S(1)} %apply_cells.10.before, bf16[64,256,128]{2,1,0:T(8,128)(2,1)S(1)} %copy-done.1, ...), custom_call_target="tpu_custom_call" | custom-call | flops 125829120 | bytes 1540096 | tf_op jit(solution)/shard_map/apply_cells/pallas_call | solution.py:140
  76.0 1.6 %collective-permute-done.22.first = bf16[4,120,256]{2,1,0:T(8,128)(2,1)S(1)} collective-permute-done((bf16[4,120,256]{2,1,0:T(8,128)(2,1)S(1)}, bf16[4,120,256]{2,1,0:T(8,128)(2,1)S(1)}, u32[]{:S(2)}, u32[]{:S(2)}) %collective-permute-start.22) | collective-permute-done | bytes 245792 | tf_op jit(solution)/shard_map/ppermute | solution.py:282
  77.9 1.8 %collective-permute-start.26 = (bf16[4,120,256]{2,1,0:T(8,128)(2,1)S(1)}, bf16[4,120,256]{2,1,0:T(8,128)(2,1)S(1)}, u32[]{:S(2)}, u32[]{:S(2)}) collective-permute-start(bf16[4,120,256]{2,1,0:T(8,128)(2,1)S(1)} %collective-permute-done.22.first), channel_id=1, source_target_pairs={{0,8},{2,6},{8,16},{10,2},{16,24},{18,10},{24,28},{26,18},{28,20},... | collective-permute-start | bytes 737288 | tf_op jit(solution)/shard_map/ppermute | solution.py:282
  80.0 1.3 %apply_cells.12.before = f32[2,120,128]{2,1,0:T(8,128)S(1)} custom-call(s32[2,9]{1,0:T(2,128)S(1)} %pad_add_fusion.bounds, s32[2,64]{1,0:T(2,128)S(1)} %get-tuple-element.126.order, s32[2,64]{1,0:T(2,128)S(1)} %get-tuple-element.127.cell, f32[2,120,128]{2,1,0:T(8,128)S(1)} %apply_cells.11.before, bf16[64,256,128]{2,1,0:T(8,128)(2,1)S(1)} %copy-done.1, ...), custom_call_target="tpu_custom_call" | custom-call | flops 125829120 | bytes 1540096 | tf_op jit(solution)/shard_map/apply_cells/pallas_call | solution.py:140
  81.3 1.6 %collective-permute-done.28.first = bf16[4,120,256]{2,1,0:T(8,128)(2,1)S(1)} collective-permute-done((bf16[4,120,256]{2,1,0:T(8,128)(2,1)S(1)}, bf16[4,120,256]{2,1,0:T(8,128)(2,1)S(1)}, u32[]{:S(2)}, u32[]{:S(2)}) %collective-permute-start.28) | collective-permute-done | bytes 245792 | tf_op jit(solution)/shard_map/ppermute | solution.py:282
  83.3 2.0 %collective-permute-start.30 = (bf16[4,120,256]{2,1,0:T(8,128)(2,1)S(1)}, bf16[4,120,256]{2,1,0:T(8,128)(2,1)S(1)}, u32[]{:S(2)}, u32[]{:S(2)}) collective-permute-start(bf16[4,120,256]{2,1,0:T(8,128)(2,1)S(1)} %collective-permute-done.28.first), channel_id=1, source_target_pairs={{0,8},{2,6},{8,16},{10,2},{16,24},{18,10},{24,28},{26,18},{28,20},... | collective-permute-start | bytes 737288 | tf_op jit(solution)/shard_map/ppermute | solution.py:282
  85.4 2.2 %copy-done.2 = bf16[64,256,128]{2,1,0:T(8,128)(2,1)S(1)} copy-done((bf16[64,256,128]{2,1,0:T(8,128)(2,1)S(1)}, bf16[64,256,128]{2,1,0:T(8,128)(2,1)}, u32[]{:S(2)}) %copy-start.2) | copy-done | bytes 4194328
  87.5 2.2 %copy-done.4 = bf16[64,256,128]{2,1,0:T(8,128)(2,1)S(1)} copy-done((bf16[64,256,128]{2,1,0:T(8,128)(2,1)S(1)}, bf16[64,256,128]{2,1,0:T(8,128)(2,1)}, u32[]{:S(2)}) %copy-start.4) | copy-done | bytes 4194328
  89.7 1.5 %apply_cells.13.before = f32[2,120,128]{2,1,0:T(8,128)S(1)} custom-call(s32[2,9]{1,0:T(2,128)S(1)} %pad_add_fusion.bounds, s32[2,64]{1,0:T(2,128)S(1)} %get-tuple-element.126.order, s32[2,64]{1,0:T(2,128)S(1)} %get-tuple-element.127.cell, f32[2,120,128]{2,1,0:T(8,128)S(1)} %apply_cells.12.before, bf16[64,256,128]{2,1,0:T(8,128)(2,1)S(1)} %copy-done.2, ...), custom_call_target="tpu_custom_call" | custom-call | flops 125829120 | bytes 1540096 | tf_op jit(solution)/shard_map/apply_cells/pallas_call | solution.py:140
  91.3 1.1 %apply_cells.14 = (f32[2,120,128]{2,1,0:T(8,128)S(1)}, bf16[8,256,128]{2,1,0:T(8,128)(2,1)S(1)}, bf16[8,256,128]{2,1,0:T(8,128)(2,1)S(1)}) custom-call(s32[2,9]{1,0:T(2,128)S(1)} %pad_add_fusion.bounds, s32[2,64]{1,0:T(2,128)S(1)} %get-tuple-element.126.order, s32[2,64]{1,0:T(2,128)S(1)} %get-tuple-element.127.cell, f32[2,120,128]{2,1,0:T(8,128)S(1)} %apply_cells.13.before, ...), custom_call_target="tpu_custom_call" | custom-call | flops 125829120 | bytes 1540096 | tf_op jit(solution)/shard_map/apply_cells/pallas_call | solution.py:140
  92.9 1.1 %apply_cells.15 = f32[2,120,128]{2,1,0:T(8,128)S(1)} custom-call(s32[2,9]{1,0:T(2,128)S(1)} %pad_add_fusion.bounds, s32[2,64]{1,0:T(2,128)S(1)} %get-tuple-element.126.order, s32[2,64]{1,0:T(2,128)S(1)} %get-tuple-element.127.cell, f32[2,120,128]{2,1,0:T(8,128)S(1)} %get-tuple-element.78.before, bf16[8,256,128]{2,1,0:T(8,128)(2,1)S(1)} %get-tuple-element.79.mine, ...), custom_call_target="tpu_custom_call" | custom-call | flops 125829120 | bytes 1540096 | tf_op jit(solution)/shard_map/apply_cells/pallas_call | solution.py:140
  94.2 1.6 %collective-permute-start.33 = (f32[120,64]{1,0:T(8,128)S(1)}, f32[120,64]{1,0:T(8,128)S(1)}, u32[]{:S(2)}, u32[]{:S(2)}) collective-permute-start(f32[120,64]{1,0:T(8,128)S(1)} %get-tuple-element.122), channel_id=1, source_target_pairs={{0,1},{1,0},{2,3},{3,2},{4,5},{5,4},{6,7},{7,6},{8,9},{9,8},{10,11... | collective-permute-start | bytes 92168 | tf_op jit(solution)/shard_map/ppermute | solution.py:170
  96.4 2.1 %collective-permute-done.33 = f32[120,64]{1,0:T(8,128)S(1)} collective-permute-done((f32[120,64]{1,0:T(8,128)S(1)}, f32[120,64]{1,0:T(8,128)S(1)}, u32[]{:S(2)}, u32[]{:S(2)}) %collective-permute-start.33) | collective-permute-done | bytes 30752 | tf_op jit(solution)/shard_map/ppermute | solution.py:170
  98.4 1.3 %collective-permute-done.34 = f32[120,64]{1,0:T(8,128)S(1)} collective-permute-done((f32[120,64]{1,0:T(8,128)S(1)}, f32[120,64]{1,0:T(8,128)S(1)}, u32[]{:S(2)}, u32[]{:S(2)}) %collective-permute-start.34) | collective-permute-done | bytes 30752 | tf_op jit(solution)/shard_map/ppermute | solution.py:171
  (78 shorter events, 11.6 us)
Async XLA Ops:
  0.0 50.9 %copy-start = (bf16[1,256,256]{2,1,0:T(8,128)(2,1)S(1)}, bf16[1,256,256]{2,1,0:T(8,128)(2,1)}, u32[]{:S(2)}) copy-start(bf16[1,256,256]{2,1,0:T(8,128)(2,1)} %param.9) | copy-start | bytes 393220
  5.6 2.7 %collective-permute-start = (bf16[16,120,256]{2,1,0:T(8,128)(2,1)S(1)}, bf16[16,120,256]{2,1,0:T(8,128)(2,1)S(1)}, u32[]{:S(2)}, u32[]{:S(2)}) collective-permute-start(bf16[16,120,256]{2,1,0:T(8,128)(2,1)S(1)} %get-tuple-element.43), channel_id=1, source_target_pairs={{0,2},{2,0},{4,6},{6,4},{8,10},{10,8},{12,14},{14,12},{16,18},{18,... | collective-permute-start | bytes 2949128 | tf_op jit(solution)/shard_map/ppermute | solution.py:228
  6.1 2.2 %collective-permute-start.1 = (s32[64]{0:T(128)S(1)}, s32[64]{0:T(128)S(1)}, u32[]{:S(2)}, u32[]{:S(2)}) collective-permute-start(s32[64]{0:T(128)S(1)} %get-tuple-element.125), channel_id=1, source_target_pairs={{0,2},{2,0},{4,6},{6,4},{8,10},{10,8},{12,14},{14,12},{16,18},{18,... | collective-permute-start | bytes 776 | tf_op jit(solution)/shard_map/ppermute | solution.py:230
  8.3 12.5 %collective-permute-start.4 = (bf16[48,120,256]{2,1,0:T(8,128)(2,1)S(1)}, bf16[48,120,256]{2,1,0:T(8,128)(2,1)S(1)}, u32[]{:S(2)}, u32[]{:S(2)}) collective-permute-start(bf16[48,120,256]{2,1,0:T(8,128)(2,1)S(1)} %get-tuple-element.49), channel_id=1, source_target_pairs={{0,2},{2,0},{4,6},{6,4},{8,10},{10,8},{12,14},{14,12},{16,18},{18,... | collective-permute-start | bytes 8847368 | tf_op jit(solution)/shard_map/ppermute | solution.py:228
  9.1 8.9 %collective-permute-start.3 = (bf16[4,120,256]{2,1,0:T(8,128)(2,1)S(1)}, bf16[4,120,256]{2,1,0:T(8,128)(2,1)S(1)}, u32[]{:S(2)}, u32[]{:S(2)}) collective-permute-start(bf16[4,120,256]{2,1,0:T(8,128)(2,1)S(1)} %add_convert_fusion.14), channel_id=1, source_target_pairs={{0,4},{2,10},{8,0},{10,18},{16,8},{18,26},{24,16},{26,30},{28,24},... | collective-permute-start | bytes 737288 | tf_op jit(solution)/shard_map/ppermute | solution.py:249
  11.8 8.9 %collective-permute-start.2 = (bf16[4,120,256]{2,1,0:T(8,128)(2,1)S(1)}, bf16[4,120,256]{2,1,0:T(8,128)(2,1)S(1)}, u32[]{:S(2)}, u32[]{:S(2)}) collective-permute-start(bf16[4,120,256]{2,1,0:T(8,128)(2,1)S(1)} %add_convert_fusion.15), channel_id=1, source_target_pairs={{0,8},{2,6},{8,16},{10,2},{16,24},{18,10},{24,28},{26,18},{28,20},... | collective-permute-start | bytes 737288 | tf_op jit(solution)/shard_map/ppermute | solution.py:249
  12.0 11.3 %collective-permute-start.8 = (bf16[4,120,256]{2,1,0:T(8,128)(2,1)S(1)}, bf16[4,120,256]{2,1,0:T(8,128)(2,1)S(1)}, u32[]{:S(2)}, u32[]{:S(2)}) collective-permute-start(bf16[4,120,256]{2,1,0:T(8,128)(2,1)S(1)} %add_convert_fusion.12), channel_id=1, source_target_pairs={{0,4},{2,10},{8,0},{10,18},{16,8},{18,26},{24,16},{26,30},{28,24},... | collective-permute-start | bytes 737288 | tf_op jit(solution)/shard_map/ppermute | solution.py:249
  14.1 9.8 %collective-permute-start.7 = (bf16[4,120,256]{2,1,0:T(8,128)(2,1)S(1)}, bf16[4,120,256]{2,1,0:T(8,128)(2,1)S(1)}, u32[]{:S(2)}, u32[]{:S(2)}) collective-permute-start(bf16[4,120,256]{2,1,0:T(8,128)(2,1)S(1)} %add_convert_fusion.13), channel_id=1, source_target_pairs={{0,8},{2,6},{8,16},{10,2},{16,24},{18,10},{24,28},{26,18},{28,20},... | collective-permute-start | bytes 737288 | tf_op jit(solution)/shard_map/ppermute | solution.py:249
  21.1 19.4 %copy-start.1 = (bf16[64,256,128]{2,1,0:T(8,128)(2,1)S(1)}, bf16[64,256,128]{2,1,0:T(8,128)(2,1)}, u32[]{:S(2)}) copy-start(bf16[64,256,128]{2,1,0:T(8,128)(2,1)} %mine.13) | copy-start | bytes 12582916
  21.1 8.8 %collective-permute-start.6 = (bf16[4,120,256]{2,1,0:T(8,128)(2,1)S(1)}, bf16[4,120,256]{2,1,0:T(8,128)(2,1)S(1)}, u32[]{:S(2)}, u32[]{:S(2)}) collective-permute-start(bf16[4,120,256]{2,1,0:T(8,128)(2,1)S(1)} %add_convert_fusion.10), channel_id=1, source_target_pairs={{0,4},{2,10},{8,0},{10,18},{16,8},{18,26},{24,16},{26,30},{28,24},... | collective-permute-start | bytes 737288 | tf_op jit(solution)/shard_map/ppermute | solution.py:249
  22.8 8.6 %collective-permute-start.5 = (bf16[4,120,256]{2,1,0:T(8,128)(2,1)S(1)}, bf16[4,120,256]{2,1,0:T(8,128)(2,1)S(1)}, u32[]{:S(2)}, u32[]{:S(2)}) collective-permute-start(bf16[4,120,256]{2,1,0:T(8,128)(2,1)S(1)} %add_convert_fusion.11), channel_id=1, source_target_pairs={{0,8},{2,6},{8,16},{10,2},{16,24},{18,10},{24,28},{26,18},{28,20},... | collective-permute-start | bytes 737288 | tf_op jit(solution)/shard_map/ppermute | solution.py:249
  24.0 11.1 %collective-permute-start.12 = (bf16[4,120,256]{2,1,0:T(8,128)(2,1)S(1)}, bf16[4,120,256]{2,1,0:T(8,128)(2,1)S(1)}, u32[]{:S(2)}, u32[]{:S(2)}) collective-permute-start(bf16[4,120,256]{2,1,0:T(8,128)(2,1)S(1)} %add_convert_fusion.8), channel_id=1, source_target_pairs={{0,4},{2,10},{8,0},{10,18},{16,8},{18,26},{24,16},{26,30},{28,24},... | collective-permute-start | bytes 737288 | tf_op jit(solution)/shard_map/ppermute | solution.py:249
  27.7 8.7 %collective-permute-start.11 = (bf16[4,120,256]{2,1,0:T(8,128)(2,1)S(1)}, bf16[4,120,256]{2,1,0:T(8,128)(2,1)S(1)}, u32[]{:S(2)}, u32[]{:S(2)}) collective-permute-start(bf16[4,120,256]{2,1,0:T(8,128)(2,1)S(1)} %add_convert_fusion.9), channel_id=1, source_target_pairs={{0,8},{2,6},{8,16},{10,2},{16,24},{18,10},{24,28},{26,18},{28,20},... | collective-permute-start | bytes 737288 | tf_op jit(solution)/shard_map/ppermute | solution.py:249
  31.5 8.7 %collective-permute-start.10 = (bf16[4,120,256]{2,1,0:T(8,128)(2,1)S(1)}, bf16[4,120,256]{2,1,0:T(8,128)(2,1)S(1)}, u32[]{:S(2)}, u32[]{:S(2)}) collective-permute-start(bf16[4,120,256]{2,1,0:T(8,128)(2,1)S(1)} %add_convert_fusion.6), channel_id=1, source_target_pairs={{0,4},{2,10},{8,0},{10,18},{16,8},{18,26},{24,16},{26,30},{28,24},... | collective-permute-start | bytes 737288 | tf_op jit(solution)/shard_map/ppermute | solution.py:249
  33.6 6.7 %collective-permute-start.9 = (bf16[4,120,256]{2,1,0:T(8,128)(2,1)S(1)}, bf16[4,120,256]{2,1,0:T(8,128)(2,1)S(1)}, u32[]{:S(2)}, u32[]{:S(2)}) collective-permute-start(bf16[4,120,256]{2,1,0:T(8,128)(2,1)S(1)} %add_convert_fusion.7), channel_id=1, source_target_pairs={{0,8},{2,6},{8,16},{10,2},{16,24},{18,10},{24,28},{26,18},{28,20},... | collective-permute-start | bytes 737288 | tf_op jit(solution)/shard_map/ppermute | solution.py:249
  40.4 18.0 %collective-permute-start.21 = (bf16[64,256,128]{2,1,0:T(8,128)(2,1)S(1)}, bf16[64,256,128]{2,1,0:T(8,128)(2,1)S(1)}, u32[]{:S(2)}, u32[]{:S(2)}) collective-permute-start(bf16[64,256,128]{2,1,0:T(8,128)(2,1)S(1)} %copy-done.1), channel_id=1, source_target_pairs={{0,2},{2,0},{4,6},{6,4},{8,10},{10,8},{12,14},{14,12},{16,18},{18,... | collective-permute-start | bytes 12582920 | tf_op jit(solution)/shard_map/ppermute | solution.py:252
  40.8 8.7 %collective-permute-start.16 = (bf16[4,120,256]{2,1,0:T(8,128)(2,1)S(1)}, bf16[4,120,256]{2,1,0:T(8,128)(2,1)S(1)}, u32[]{:S(2)}, u32[]{:S(2)}) collective-permute-start(bf16[4,120,256]{2,1,0:T(8,128)(2,1)S(1)} %add_convert_fusion.4), channel_id=1, source_target_pairs={{0,4},{2,10},{8,0},{10,18},{16,8},{18,26},{24,16},{26,30},{28,24},... | collective-permute-start | bytes 737288 | tf_op jit(solution)/shard_map/ppermute | solution.py:249
  42.0 8.9 %collective-permute-start.17 = (bf16[4,120,256]{2,1,0:T(8,128)(2,1)S(1)}, bf16[4,120,256]{2,1,0:T(8,128)(2,1)S(1)}, u32[]{:S(2)}, u32[]{:S(2)}) collective-permute-start(bf16[4,120,256]{2,1,0:T(8,128)(2,1)S(1)} %add_convert_fusion.1), channel_id=1, source_target_pairs={{0,8},{2,6},{8,16},{10,2},{16,24},{18,10},{24,28},{26,18},{28,20},... | collective-permute-start | bytes 737288 | tf_op jit(solution)/shard_map/ppermute | solution.py:249
  43.3 11.2 %collective-permute-start.14 = (bf16[4,120,256]{2,1,0:T(8,128)(2,1)S(1)}, bf16[4,120,256]{2,1,0:T(8,128)(2,1)S(1)}, u32[]{:S(2)}, u32[]{:S(2)}) collective-permute-start(bf16[4,120,256]{2,1,0:T(8,128)(2,1)S(1)} %add_convert_fusion.5), channel_id=1, source_target_pairs={{0,8},{2,6},{8,16},{10,2},{16,24},{18,10},{24,28},{26,18},{28,20},... | collective-permute-start | bytes 737288 | tf_op jit(solution)/shard_map/ppermute | solution.py:249
  44.7 10.1 %collective-permute-start.13 = (bf16[4,120,256]{2,1,0:T(8,128)(2,1)S(1)}, bf16[4,120,256]{2,1,0:T(8,128)(2,1)S(1)}, u32[]{:S(2)}, u32[]{:S(2)}) collective-permute-start(bf16[4,120,256]{2,1,0:T(8,128)(2,1)S(1)} %add_convert_fusion.3), channel_id=1, source_target_pairs={{0,4},{2,10},{8,0},{10,18},{16,8},{18,26},{24,16},{26,30},{28,24},... | collective-permute-start | bytes 737288 | tf_op jit(solution)/shard_map/ppermute | solution.py:249
  51.2 8.4 %collective-permute-start.19 = (bf16[4,120,256]{2,1,0:T(8,128)(2,1)S(1)}, bf16[4,120,256]{2,1,0:T(8,128)(2,1)S(1)}, u32[]{:S(2)}, u32[]{:S(2)}) collective-permute-start(bf16[4,120,256]{2,1,0:T(8,128)(2,1)S(1)} %convolution_convert_fusion.first), channel_id=1, source_target_pairs={{0,8},{2,6},{8,16},{10,2},{16,24},{18,10},{24,28},{26,18},{28,20},... | collective-permute-start | bytes 737288 | tf_op jit(solution)/shard_map/ppermute | solution.py:275
  55.1 7.0 %collective-permute-start.20 = (bf16[4,120,256]{2,1,0:T(8,128)(2,1)S(1)}, bf16[4,120,256]{2,1,0:T(8,128)(2,1)S(1)}, u32[]{:S(2)}, u32[]{:S(2)}) collective-permute-start(bf16[4,120,256]{2,1,0:T(8,128)(2,1)S(1)} %convolution_convert_fusion.1.second), channel_id=1, source_target_pairs={{0,4},{2,10},{8,0},{10,18},{16,8},{18,26},{24,16},{26,30},{28,24},... | collective-permute-start | bytes 737288 | tf_op jit(solution)/shard_map/ppermute | solution.py:275
  56.4 11.0 %collective-permute-start.18 = (bf16[4,120,256]{2,1,0:T(8,128)(2,1)S(1)}, bf16[4,120,256]{2,1,0:T(8,128)(2,1)S(1)}, u32[]{:S(2)}, u32[]{:S(2)}) collective-permute-start(bf16[4,120,256]{2,1,0:T(8,128)(2,1)S(1)} %convolution_convert_fusion.first), channel_id=1, source_target_pairs={{0,4},{2,10},{8,0},{10,18},{16,8},{18,26},{24,16},{26,30},{28,24},... | collective-permute-start | bytes 737288 | tf_op jit(solution)/shard_map/ppermute | solution.py:275
  58.2 9.2 %collective-permute-start.15 = (bf16[4,120,256]{2,1,0:T(8,128)(2,1)S(1)}, bf16[4,120,256]{2,1,0:T(8,128)(2,1)S(1)}, u32[]{:S(2)}, u32[]{:S(2)}) collective-permute-start(bf16[4,120,256]{2,1,0:T(8,128)(2,1)S(1)} %convolution_convert_fusion.1.second), channel_id=1, source_target_pairs={{0,8},{2,6},{8,16},{10,2},{16,24},{18,10},{24,28},{26,18},{28,20},... | collective-permute-start | bytes 737288 | tf_op jit(solution)/shard_map/ppermute | solution.py:275
  58.5 21.5 %copy-start.3 = (bf16[64,256,128]{2,1,0:T(8,128)(2,1)}, bf16[64,256,128]{2,1,0:T(8,128)(2,1)S(1)}, u32[]{:S(2)}) copy-start(bf16[64,256,128]{2,1,0:T(8,128)(2,1)S(1)} %collective-permute-done.21.other) | copy-start | bytes 12582916
  62.1 10.2 %collective-permute-start.24 = (bf16[4,120,256]{2,1,0:T(8,128)(2,1)S(1)}, bf16[4,120,256]{2,1,0:T(8,128)(2,1)S(1)}, u32[]{:S(2)}, u32[]{:S(2)}) collective-permute-start(bf16[4,120,256]{2,1,0:T(8,128)(2,1)S(1)} %collective-permute-done.19.first), channel_id=1, source_target_pairs={{0,8},{2,6},{8,16},{10,2},{16,24},{18,10},{24,28},{26,18},{28,20},... | collective-permute-start | bytes 737288 | tf_op jit(solution)/shard_map/ppermute | solution.py:282
  62.7 9.9 %collective-permute-start.25 = (bf16[4,120,256]{2,1,0:T(8,128)(2,1)S(1)}, bf16[4,120,256]{2,1,0:T(8,128)(2,1)S(1)}, u32[]{:S(2)}, u32[]{:S(2)}) collective-permute-start(bf16[4,120,256]{2,1,0:T(8,128)(2,1)S(1)} %collective-permute-done.20.second), channel_id=1, source_target_pairs={{0,4},{2,10},{8,0},{10,18},{16,8},{18,26},{24,16},{26,30},{28,24},... | collective-permute-start | bytes 737288 | tf_op jit(solution)/shard_map/ppermute | solution.py:282
  67.4 10.2 %collective-permute-start.22 = (bf16[4,120,256]{2,1,0:T(8,128)(2,1)S(1)}, bf16[4,120,256]{2,1,0:T(8,128)(2,1)S(1)}, u32[]{:S(2)}, u32[]{:S(2)}) collective-permute-start(bf16[4,120,256]{2,1,0:T(8,128)(2,1)S(1)} %collective-permute-done.15.first), channel_id=1, source_target_pairs={{0,8},{2,6},{8,16},{10,2},{16,24},{18,10},{24,28},{26,18},{28,20},... | collective-permute-start | bytes 737288 | tf_op jit(solution)/shard_map/ppermute | solution.py:282
  68.0 9.9 %collective-permute-start.23 = (bf16[4,120,256]{2,1,0:T(8,128)(2,1)S(1)}, bf16[4,120,256]{2,1,0:T(8,128)(2,1)S(1)}, u32[]{:S(2)}, u32[]{:S(2)}) collective-permute-start(bf16[4,120,256]{2,1,0:T(8,128)(2,1)S(1)} %collective-permute-done.18.second), channel_id=1, source_target_pairs={{0,4},{2,10},{8,0},{10,18},{16,8},{18,26},{24,16},{26,30},{28,24},... | collective-permute-start | bytes 737288 | tf_op jit(solution)/shard_map/ppermute | solution.py:282
  72.6 10.2 %collective-permute-start.28 = (bf16[4,120,256]{2,1,0:T(8,128)(2,1)S(1)}, bf16[4,120,256]{2,1,0:T(8,128)(2,1)S(1)}, u32[]{:S(2)}, u32[]{:S(2)}) collective-permute-start(bf16[4,120,256]{2,1,0:T(8,128)(2,1)S(1)} %collective-permute-done.24.first), channel_id=1, source_target_pairs={{0,8},{2,6},{8,16},{10,2},{16,24},{18,10},{24,28},{26,18},{28,20},... | collective-permute-start | bytes 737288 | tf_op jit(solution)/shard_map/ppermute | solution.py:282
  74.4 8.9 %collective-permute-start.29 = (bf16[4,120,256]{2,1,0:T(8,128)(2,1)S(1)}, bf16[4,120,256]{2,1,0:T(8,128)(2,1)S(1)}, u32[]{:S(2)}, u32[]{:S(2)}) collective-permute-start(bf16[4,120,256]{2,1,0:T(8,128)(2,1)S(1)} %collective-permute-done.25.second), channel_id=1, source_target_pairs={{0,4},{2,10},{8,0},{10,18},{16,8},{18,26},{24,16},{26,30},{28,24},... | collective-permute-start | bytes 737288 | tf_op jit(solution)/shard_map/ppermute | solution.py:282
  77.9 13.4 %collective-permute-start.26 = (bf16[4,120,256]{2,1,0:T(8,128)(2,1)S(1)}, bf16[4,120,256]{2,1,0:T(8,128)(2,1)S(1)}, u32[]{:S(2)}, u32[]{:S(2)}) collective-permute-start(bf16[4,120,256]{2,1,0:T(8,128)(2,1)S(1)} %collective-permute-done.22.first), channel_id=1, source_target_pairs={{0,8},{2,6},{8,16},{10,2},{16,24},{18,10},{24,28},{26,18},{28,20},... | collective-permute-start | bytes 737288 | tf_op jit(solution)/shard_map/ppermute | solution.py:282
  79.7 11.6 %collective-permute-start.27 = (bf16[4,120,256]{2,1,0:T(8,128)(2,1)S(1)}, bf16[4,120,256]{2,1,0:T(8,128)(2,1)S(1)}, u32[]{:S(2)}, u32[]{:S(2)}) collective-permute-start(bf16[4,120,256]{2,1,0:T(8,128)(2,1)S(1)} %collective-permute-done.23.second), channel_id=1, source_target_pairs={{0,4},{2,10},{8,0},{10,18},{16,8},{18,26},{24,16},{26,30},{28,24},... | collective-permute-start | bytes 737288 | tf_op jit(solution)/shard_map/ppermute | solution.py:282
  83.3 9.1 %collective-permute-start.30 = (bf16[4,120,256]{2,1,0:T(8,128)(2,1)S(1)}, bf16[4,120,256]{2,1,0:T(8,128)(2,1)S(1)}, u32[]{:S(2)}, u32[]{:S(2)}) collective-permute-start(bf16[4,120,256]{2,1,0:T(8,128)(2,1)S(1)} %collective-permute-done.28.first), channel_id=1, source_target_pairs={{0,8},{2,6},{8,16},{10,2},{16,24},{18,10},{24,28},{26,18},{28,20},... | collective-permute-start | bytes 737288 | tf_op jit(solution)/shard_map/ppermute | solution.py:282
  85.4 7.6 %collective-permute-start.31 = (bf16[4,120,256]{2,1,0:T(8,128)(2,1)S(1)}, bf16[4,120,256]{2,1,0:T(8,128)(2,1)S(1)}, u32[]{:S(2)}, u32[]{:S(2)}) collective-permute-start(bf16[4,120,256]{2,1,0:T(8,128)(2,1)S(1)} %collective-permute-done.29.second), channel_id=1, source_target_pairs={{0,4},{2,10},{8,0},{10,18},{16,8},{18,26},{24,16},{26,30},{28,24},... | collective-permute-start | bytes 737288 | tf_op jit(solution)/shard_map/ppermute | solution.py:282
  85.4 2.2 %copy-start.2 = (bf16[64,256,128]{2,1,0:T(8,128)(2,1)S(1)}, bf16[64,256,128]{2,1,0:T(8,128)(2,1)}, u32[]{:S(2)}) copy-start(bf16[64,256,128]{2,1,0:T(8,128)(2,1)} %mine.13) | copy-start | bytes 12582916
  87.5 2.2 %copy-start.4 = (bf16[64,256,128]{2,1,0:T(8,128)(2,1)S(1)}, bf16[64,256,128]{2,1,0:T(8,128)(2,1)}, u32[]{:S(2)}) copy-start(bf16[64,256,128]{2,1,0:T(8,128)(2,1)} %copy-done.3) | copy-start | bytes 12582916
  94.2 4.3 %collective-permute-start.33 = (f32[120,64]{1,0:T(8,128)S(1)}, f32[120,64]{1,0:T(8,128)S(1)}, u32[]{:S(2)}, u32[]{:S(2)}) collective-permute-start(f32[120,64]{1,0:T(8,128)S(1)} %get-tuple-element.122), channel_id=1, source_target_pairs={{0,1},{1,0},{2,3},{3,2},{4,5},{5,4},{6,7},{7,6},{8,9},{9,8},{10,11... | collective-permute-start | bytes 92168 | tf_op jit(solution)/shard_map/ppermute | solution.py:170
  95.7 4.0 %collective-permute-start.34 = (f32[120,64]{1,0:T(8,128)S(1)}, f32[120,64]{1,0:T(8,128)S(1)}, u32[]{:S(2)}, u32[]{:S(2)}) collective-permute-start(f32[120,64]{1,0:T(8,128)S(1)} %get-tuple-element.121), channel_id=1, source_target_pairs={{0,3},{1,2},{2,1},{3,0},{4,7},{5,6},{6,5},{7,4},{8,11},{9,10},{10,... | collective-permute-start | bytes 92168 | tf_op jit(solution)/shard_map/ppermute | solution.py:171
  95.7 4.0 %collective-permute-start.32 = (f32[120,64]{1,0:T(8,128)S(1)}, f32[120,64]{1,0:T(8,128)S(1)}, u32[]{:S(2)}, u32[]{:S(2)}) collective-permute-start(f32[120,64]{1,0:T(8,128)S(1)} %slice_bitcast_fusion.2), channel_id=1, source_target_pairs={{0,2},{2,0},{4,6},{6,4},{8,10},{10,8},{12,14},{14,12},{16,18},{18,... | collective-permute-start | bytes 92168 | tf_op jit(solution)/shard_map/ppermute | solution.py:172

commit v4 on v3

--- a/solution.py
+++ b/solution.py
@@ -9,7 +9,7 @@
 
 OCC_DEV = 8
 GROUP = 4
-CHUNKS = 8
+CHUNKS = (0, 4, 8, 12, 16)
 KERNEL_VMEM = 28 << 20
 APPLY_VMEM = 12 << 20
 
@@ -43,18 +43,18 @@
 def sum_cells_kernel(sends, cell, again, tens, coef, *refs):
     out, copied, (blocks, rows_in, totals, arrived) = refs[0], refs[1:-4], refs[-4:]
     block_count = tens.shape[0]
-    chunk = block_count // CHUNKS
-    copies = [pltpu.make_async_copy(coef, rows_in, arrived.at[CHUNKS])]
-    for c in range(CHUNKS):
-        part = slice(c * chunk, (c + 1) * chunk)
+    edges = [block_count * e // 16 for e in CHUNKS]
+    copies = [pltpu.make_async_copy(coef, rows_in, arrived.at[len(edges) - 1])]
+    for c, (start, stop) in enumerate(zip(edges, edges[1:])):
+        part = slice(start, stop)
         copies.append(pltpu.make_async_copy(tens.at[part], blocks.at[part], arrived.at[c]))
     for copy in copies:
         copy.start()
     out[...] = jnp.zeros_like(out)
     copies[0].wait()
-    for c in range(CHUNKS):
+    for c, (first, stop) in enumerate(zip(edges, edges[1:])):
         copies[1 + c].wait()
-        for start in range(c * chunk, (c + 1) * chunk, GROUP):
+        for start in range(first, stop, GROUP):
             halves = [
                 lax.dot_general(
                     rows_in[...],
@@ -92,7 +92,7 @@
                 pltpu.VMEM(tens.shape, tens.dtype),
                 pltpu.VMEM(coef.shape, coef.dtype),
                 pltpu.VMEM((cells, rows, width), jnp.float32),
-                pltpu.SemaphoreType.DMA((CHUNKS + 1,)),
+                pltpu.SemaphoreType.DMA((len(CHUNKS),)),
             ],
         ),
         compiler_params=pltpu.CompilerParams(vmem_limit_bytes=KERNEL_VMEM),
@@ -106,7 +106,7 @@
     )
 
 
-def apply_cells_kernel(group, takes, bounds, order, cell, before, mine, other, first, second, *refs):
+def apply_cells_kernel(group, takes, turned, batch, bounds, order, cell, before, mine, other, first, second, *refs):
     outs, held = refs[:-1], refs[-1]
     half = first.shape[0]
     held[:half], held[half : 2 * half] = first[...], second[...]
@@ -117,8 +117,8 @@
         start, stop = bounds[d, group], bounds[d, group + 1]
 
         def some(g, total):
-            for u in range(GROUP):
-                k = start + g * GROUP + u
+            for u in range(batch):
+                k = start + g * batch + u
                 b = order[d, jnp.minimum(k, last)]
                 here = jnp.where(k < stop, cell[d, b] - 2 * half * group, empty)
                 if tens.shape[0] <= last:
@@ -126,19 +126,21 @@
                 total = total + jnp.dot(held[here], tens[b], preferred_element_type=jnp.float32)
             return total
 
-        outs[0][d] = lax.fori_loop(0, (stop - start + GROUP - 1) // GROUP, some, before[d])
+        total = lax.fori_loop(0, (stop - start + batch - 1) // batch, some, before[d])
+        outs[0][d] = total.T if turned else total
         for k in range(takes):
             outs[1 + d][k] = tens[order[d, k]] if tens.shape[0] > last else tens[k]
 
 
-def apply_cells(group, tables, before, tens, pieces, takes=0):
+def apply_cells(group, tables, before, tens, pieces, takes=0, turned=False):
     rows, width = pieces[0].shape[1:]
-    outs = [jax.ShapeDtypeStruct(before.shape, jnp.float32)]
+    shape = (before.shape[0], before.shape[2], before.shape[1]) if turned else before.shape
+    outs = [jax.ShapeDtypeStruct(shape, jnp.float32)]
     if takes:
         outs += [jax.ShapeDtypeStruct((takes, *tens[0].shape[1:]), tens[0].dtype)] * 2
     arrays = [before, *tens, *pieces]
     return pl.pallas_call(
-        functools.partial(apply_cells_kernel, group, takes),
+        functools.partial(apply_cells_kernel, group, takes, turned, 2 * GROUP if turned else GROUP),
         out_shape=tuple(outs),
         grid_spec=pltpu.PrefetchScalarGridSpec(
             num_scalar_prefetch=3,
@@ -160,9 +162,9 @@
 def sum_over_cores_and_ctr(total, owners):
     cores = [(k, k ^ 1) for k in range(owners)]
     if lax.axis_size("ctr") != 2:
-        return sum_over_ctr(total[0] + lax.ppermute(total[1], "wide", cores))
-    width = total.shape[2] // 2
-    low, high = total[:, :, :width], total[:, :, width:]
+        return sum_over_ctr((total[0] + lax.ppermute(total[1], "wide", cores)).T)
+    width = total.shape[1] // 2
+    low, high = total[:, :width], total[:, width:]
     lower = lax.axis_index("ctr") == 0
     mine, other = jnp.where(lower, low, high), jnp.where(lower, high, low)
     diagonal = [(2 * a + y, 2 * b + 1 - y) for a, b in cores for y in range(2)]
@@ -171,7 +173,7 @@
         lax.ppermute(other[1], ("wide", "ctr"), diagonal),
         lax.ppermute(mine[1], "wide", cores),
     )
-    return (mine[0] + parts[2]) + (parts[0] + parts[1])
+    return ((mine[0] + parts[2]) + (parts[0] + parts[1])).T
 
 
 def cells_body(tens, coef, aux_of, slot_of, metric):
@@ -229,6 +231,9 @@
         if p == 0:
             other_names = across(target * slots + slot_of)
             got, other_names, *others[1:] = apart((got, other_names, *others[1:]))
+        if p == 1:
+            got, tens_out = apart((got, tens))
+            other_tens = across(tens_out)
         for k, way in enumerate(part):
             start = numbers[way] * half_slots
             mine = apart(sums[start : start + half_slots])
@@ -247,9 +252,6 @@
         back = add(back, local[chips - step, pair[1]]).astype(jnp.bfloat16)
         sent = (ahead, back)
         up[pair[0]], down[pair[1]] = forward(ahead), backward(back)
-        if (pair, step) == turns[6]:
-            *sent, tens_out = apart((*sent, tens))
-            other_tens = across(tens_out)
 
     own = []
     for h in range(2):
@@ -284,7 +286,7 @@
         takes = capacity if (pair, step) == uses[-1] else 0
         total, *more = apply_cells(group, tables, total, both, [ahead, back], takes)
         taken = more or taken
-    (total,) = apply_cells(0, tables, total, taken, [up[0], down[1]])
+    (total,) = apply_cells(0, tables, total, taken, [up[0], down[1]], turned=True)
     return sum_over_cores_and_ctr(total, owners)
 
 
@@ -334,7 +336,7 @@
 
 def body(tens, coef, aux_of, slot_of, metric):
     owners, block_count = lax.axis_size("wide"), tens.shape[0]
-    dense = owners * OCC_DEV <= 2 * block_count and owners % 4 == 0
+    dense = owners * OCC_DEV <= 2 * block_count and owners % 4 == 0 and block_count % 64 == 0
     return (cells_body if dense else slots_body)(tens, coef, aux_of, slot_of, metric)
 
 

time: 101 us -> 98.1 us (0.971)
  waiting for transfers between devices: 41.5 us -> 36.5 us
  starting transfers between devices: 34.9 us -> 37.1 us
    ppermute x24, waiting for transfers between devices: 31.7 us -> 25.8 us  [cells_body(): up[pair[0]], down[pair[1]] = (forward(ahead), backward(back))]
    ppermute x2, waiting for transfers between devices: 0.01 us -> 3.1 us  [cells_body(): forward(own[h])]
    ppermute x24, starting transfers between devices: 27.4 us -> 29.7 us  [cells_body(): up[pair[0]], down[pair[1]] = (forward(ahead), backward(back))]
    ppermute x2, waiting for transfers between devices: 4.36 us -> 2.76 us  [cells_body(): backward(own[h])]
  transfers between devices with their start and end apart: 35 -> 35, of which waited for: 24 -> 23; matrix products, arithmetic and copies ran while one was open for 3% -> 3% of each run, Pallas kernels for 9% -> 10%
where the time goes in v4:
time: 98.1 us; the launch traced here: 97.9 us
  starting transfers between devices  37.1 us (38%)
  waiting for transfers between devices  36.5 us (37%)
  Pallas kernels  14.9 us (15%)
  local copies, waits for them, and re-layouts  4.93 us (5%)
  other arithmetic  3.6 us (4%)
    ppermute x24, starting transfers between devices, cells_body(): up[pair[0]], down[pair[1]] = (forward(ahead), backward(back))  29.7 us
    ppermute x24, waiting for transfers between devices, cells_body(): up[pair[0]], down[pair[1]] = (forward(ahead), backward(back))  25.8 us
    pallas_call x8, Pallas kernels, apply_cells(): pl.pallas_call(functools.partial(apply_cells_kernel, group, takes, turned...  10.8 us
    unnamed x10, local copies, waits for them, and re-layouts  4.39 us
    pallas_call x1, Pallas kernels, sum_cells(): pl.pallas_call(functools.partial(sum_cells_kernel, sends), out_shape=tupl...  4.15 us
    ppermute x2, waiting for transfers between devices, cells_body(): forward(own[h])  3.1 us
    ppermute x2, waiting for transfers between devices, cells_body(): backward(own[h])  2.76 us
    ppermute x2, starting transfers between devices, cells_body(): backward(own[h])  2.28 us
  transfers between devices with their start and end apart: 35, of which 23 were waited for; matrix products, arithmetic and copies ran while one was open for 3% of the time, Pallas kernels for 10%

profile of v4, /device:TPU:0, one launch (start us, length us, event | category | flops | bytes accessed | tf_op | source)
XLA Modules:
  0.0 97.9 jit_solution(4884957678251628480)
XLA Ops:
  0.9 4.1 %sum_cells.1 = (bf16[128,120,256]{2,1,0:T(8,128)(2,1)S(1)}, bf16[16,120,256]{2,1,0:T(8,128)(2,1)S(1)}, bf16[48,120,256]{2,1,0:T(8,128)(2,1)S(1)}) custom-call(s32[64]{0:T(128)S(1)} %fusion.8.cell, s32[64]{0:T(128)S(1)} %select_reduce_fusion.4.again, bf16[64,256,128]{2,1,0:T(8,128)(2,1)} %mine.13, bf16[120,128]{1,0:T(8,128)(2,1)} %coef.1), custom_call_target="tpu_custom_call" | custom-call | flops 503316480 | bytes 12058624 | tf_op jit(solution)/shard_map/sum_cells/pallas_call | solution.py:83
  5.7 2.1 %collective-permute-done.1 = s32[64]{0:T(128)S(1)} collective-permute-done((s32[64]{0:T(128)S(1)}, s32[64]{0:T(128)S(1)}, u32[]{:S(2)}, u32[]{:S(2)}) %collective-permute-start.1) | collective-permute-done | bytes 288 | tf_op jit(solution)/shard_map/ppermute | solution.py:232
  8.9 2.7 %collective-permute-start.3 = (bf16[4,120,256]{2,1,0:T(8,128)(2,1)S(1)}, bf16[4,120,256]{2,1,0:T(8,128)(2,1)S(1)}, u32[]{:S(2)}, u32[]{:S(2)}) collective-permute-start(bf16[4,120,256]{2,1,0:T(8,128)(2,1)S(1)} %add_convert_fusion.14), channel_id=1, source_target_pairs={{0,4},{2,10},{8,0},{10,18},{16,8},{18,26},{24,16},{26,30},{28,24},... | collective-permute-start | bytes 737288 | tf_op jit(solution)/shard_map/ppermute | solution.py:254
  11.9 2.0 %collective-permute-start.8 = (bf16[4,120,256]{2,1,0:T(8,128)(2,1)S(1)}, bf16[4,120,256]{2,1,0:T(8,128)(2,1)S(1)}, u32[]{:S(2)}, u32[]{:S(2)}) collective-permute-start(bf16[4,120,256]{2,1,0:T(8,128)(2,1)S(1)} %add_convert_fusion.12), channel_id=1, source_target_pairs={{0,4},{2,10},{8,0},{10,18},{16,8},{18,26},{24,16},{26,30},{28,24},... | collective-permute-start | bytes 737288 | tf_op jit(solution)/shard_map/ppermute | solution.py:254
  13.9 2.5 %collective-permute-start.7 = (bf16[4,120,256]{2,1,0:T(8,128)(2,1)S(1)}, bf16[4,120,256]{2,1,0:T(8,128)(2,1)S(1)}, u32[]{:S(2)}, u32[]{:S(2)}) collective-permute-start(bf16[4,120,256]{2,1,0:T(8,128)(2,1)S(1)} %add_convert_fusion.13), channel_id=1, source_target_pairs={{0,8},{2,6},{8,16},{10,2},{16,24},{18,10},{24,28},{26,18},{28,20},... | collective-permute-start | bytes 737288 | tf_op jit(solution)/shard_map/ppermute | solution.py:254
  16.8 1.0 %collective-permute-done.3 = bf16[4,120,256]{2,1,0:T(8,128)(2,1)S(1)} collective-permute-done((bf16[4,120,256]{2,1,0:T(8,128)(2,1)S(1)}, bf16[4,120,256]{2,1,0:T(8,128)(2,1)S(1)}, u32[]{:S(2)}, u32[]{:S(2)}) %collective-permute-start.3) | collective-permute-done | bytes 245792 | tf_op jit(solution)/shard_map/ppermute | solution.py:254
  17.8 2.7 %collective-permute-done.2 = bf16[4,120,256]{2,1,0:T(8,128)(2,1)S(1)} collective-permute-done((bf16[4,120,256]{2,1,0:T(8,128)(2,1)S(1)}, bf16[4,120,256]{2,1,0:T(8,128)(2,1)S(1)}, u32[]{:S(2)}, u32[]{:S(2)}) %collective-permute-start.2) | collective-permute-done | bytes 245792 | tf_op jit(solution)/shard_map/ppermute | solution.py:254
  20.9 1.6 %collective-permute-start.6 = (bf16[4,120,256]{2,1,0:T(8,128)(2,1)S(1)}, bf16[4,120,256]{2,1,0:T(8,128)(2,1)S(1)}, u32[]{:S(2)}, u32[]{:S(2)}) collective-permute-start(bf16[4,120,256]{2,1,0:T(8,128)(2,1)S(1)} %add_convert_fusion.10), channel_id=1, source_target_pairs={{0,4},{2,10},{8,0},{10,18},{16,8},{18,26},{24,16},{26,30},{28,24},... | collective-permute-start | bytes 737288 | tf_op jit(solution)/shard_map/ppermute | solution.py:254
  23.9 3.6 %collective-permute-start.12 = (bf16[4,120,256]{2,1,0:T(8,128)(2,1)S(1)}, bf16[4,120,256]{2,1,0:T(8,128)(2,1)S(1)}, u32[]{:S(2)}, u32[]{:S(2)}) collective-permute-start(bf16[4,120,256]{2,1,0:T(8,128)(2,1)S(1)} %add_convert_fusion.8), channel_id=1, source_target_pairs={{0,4},{2,10},{8,0},{10,18},{16,8},{18,26},{24,16},{26,30},{28,24},... | collective-permute-start | bytes 737288 | tf_op jit(solution)/shard_map/ppermute | solution.py:254
  27.6 2.0 %collective-permute-done.6 = bf16[4,120,256]{2,1,0:T(8,128)(2,1)S(1)} collective-permute-done((bf16[4,120,256]{2,1,0:T(8,128)(2,1)S(1)}, bf16[4,120,256]{2,1,0:T(8,128)(2,1)S(1)}, u32[]{:S(2)}, u32[]{:S(2)}) %collective-permute-start.6) | collective-permute-done | bytes 245792 | tf_op jit(solution)/shard_map/ppermute | solution.py:254
  29.6 1.5 %collective-permute-done.5 = bf16[4,120,256]{2,1,0:T(8,128)(2,1)S(1)} collective-permute-done((bf16[4,120,256]{2,1,0:T(8,128)(2,1)S(1)}, bf16[4,120,256]{2,1,0:T(8,128)(2,1)S(1)}, u32[]{:S(2)}, u32[]{:S(2)}) %collective-permute-start.5) | collective-permute-done | bytes 245792 | tf_op jit(solution)/shard_map/ppermute | solution.py:254
  31.3 2.0 %collective-permute-start.10 = (bf16[4,120,256]{2,1,0:T(8,128)(2,1)S(1)}, bf16[4,120,256]{2,1,0:T(8,128)(2,1)S(1)}, u32[]{:S(2)}, u32[]{:S(2)}) collective-permute-start(bf16[4,120,256]{2,1,0:T(8,128)(2,1)S(1)} %add_convert_fusion.6), channel_id=1, source_target_pairs={{0,4},{2,10},{8,0},{10,18},{16,8},{18,26},{24,16},{26,30},{28,24},... | collective-permute-start | bytes 737288 | tf_op jit(solution)/shard_map/ppermute | solution.py:254
  33.5 1.4 %collective-permute-done.12 = bf16[4,120,256]{2,1,0:T(8,128)(2,1)S(1)} collective-permute-done((bf16[4,120,256]{2,1,0:T(8,128)(2,1)S(1)}, bf16[4,120,256]{2,1,0:T(8,128)(2,1)S(1)}, u32[]{:S(2)}, u32[]{:S(2)}) %collective-permute-start.12) | collective-permute-done | bytes 245792 | tf_op jit(solution)/shard_map/ppermute | solution.py:254
  34.9 1.3 %collective-permute-done.11 = bf16[4,120,256]{2,1,0:T(8,128)(2,1)S(1)} collective-permute-done((bf16[4,120,256]{2,1,0:T(8,128)(2,1)S(1)}, bf16[4,120,256]{2,1,0:T(8,128)(2,1)S(1)}, u32[]{:S(2)}, u32[]{:S(2)}) %collective-permute-start.11) | collective-permute-done | bytes 245792 | tf_op jit(solution)/shard_map/ppermute | solution.py:254
  36.3 2.2 %collective-permute-start.16 = (bf16[4,120,256]{2,1,0:T(8,128)(2,1)S(1)}, bf16[4,120,256]{2,1,0:T(8,128)(2,1)S(1)}, u32[]{:S(2)}, u32[]{:S(2)}) collective-permute-start(bf16[4,120,256]{2,1,0:T(8,128)(2,1)S(1)} %add_convert_fusion.4), channel_id=1, source_target_pairs={{0,4},{2,10},{8,0},{10,18},{16,8},{18,26},{24,16},{26,30},{28,24},... | collective-permute-start | bytes 737288 | tf_op jit(solution)/shard_map/ppermute | solution.py:254
  38.7 1.5 %collective-permute-done.10 = bf16[4,120,256]{2,1,0:T(8,128)(2,1)S(1)} collective-permute-done((bf16[4,120,256]{2,1,0:T(8,128)(2,1)S(1)}, bf16[4,120,256]{2,1,0:T(8,128)(2,1)S(1)}, u32[]{:S(2)}, u32[]{:S(2)}) %collective-permute-start.10) | collective-permute-done | bytes 245792 | tf_op jit(solution)/shard_map/ppermute | solution.py:254
  40.2 1.6 %collective-permute-done.9 = bf16[4,120,256]{2,1,0:T(8,128)(2,1)S(1)} collective-permute-done((bf16[4,120,256]{2,1,0:T(8,128)(2,1)S(1)}, bf16[4,120,256]{2,1,0:T(8,128)(2,1)S(1)}, u32[]{:S(2)}, u32[]{:S(2)}) %collective-permute-start.9) | collective-permute-done | bytes 245792 | tf_op jit(solution)/shard_map/ppermute | solution.py:254
  42.2 2.0 %collective-permute-start.13 = (bf16[4,120,256]{2,1,0:T(8,128)(2,1)S(1)}, bf16[4,120,256]{2,1,0:T(8,128)(2,1)S(1)}, u32[]{:S(2)}, u32[]{:S(2)}) collective-permute-start(bf16[4,120,256]{2,1,0:T(8,128)(2,1)S(1)} %add_convert_fusion.3), channel_id=1, source_target_pairs={{0,4},{2,10},{8,0},{10,18},{16,8},{18,26},{24,16},{26,30},{28,24},... | collective-permute-start | bytes 737288 | tf_op jit(solution)/shard_map/ppermute | solution.py:254
  44.1 1.3 %collective-permute-done.16 = bf16[4,120,256]{2,1,0:T(8,128)(2,1)S(1)} collective-permute-done((bf16[4,120,256]{2,1,0:T(8,128)(2,1)S(1)}, bf16[4,120,256]{2,1,0:T(8,128)(2,1)S(1)}, u32[]{:S(2)}, u32[]{:S(2)}) %collective-permute-start.16) | collective-permute-done | bytes 245792 | tf_op jit(solution)/shard_map/ppermute | solution.py:254
  45.4 4.7 %collective-permute-done.17 = bf16[4,120,256]{2,1,0:T(8,128)(2,1)S(1)} collective-permute-done((bf16[4,120,256]{2,1,0:T(8,128)(2,1)S(1)}, bf16[4,120,256]{2,1,0:T(8,128)(2,1)S(1)}, u32[]{:S(2)}, u32[]{:S(2)}) %collective-permute-start.17) | collective-permute-done | bytes 245792 | tf_op jit(solution)/shard_map/ppermute | solution.py:254
  50.4 1.4 %collective-permute-start.19 = (bf16[4,120,256]{2,1,0:T(8,128)(2,1)S(1)}, bf16[4,120,256]{2,1,0:T(8,128)(2,1)S(1)}, u32[]{:S(2)}, u32[]{:S(2)}) collective-permute-start(bf16[4,120,256]{2,1,0:T(8,128)(2,1)S(1)} %convolution_convert_fusion.first), channel_id=1, source_target_pairs={{0,8},{2,6},{8,16},{10,2},{16,24},{18,10},{24,28},{26,18},{28,20},... | collective-permute-start | bytes 737288 | tf_op jit(solution)/shard_map/ppermute | solution.py:277
  52.9 1.6 %collective-permute-start.18 = (bf16[4,120,256]{2,1,0:T(8,128)(2,1)S(1)}, bf16[4,120,256]{2,1,0:T(8,128)(2,1)S(1)}, u32[]{:S(2)}, u32[]{:S(2)}) collective-permute-start(bf16[4,120,256]{2,1,0:T(8,128)(2,1)S(1)} %convolution_convert_fusion.first), channel_id=1, source_target_pairs={{0,4},{2,10},{8,0},{10,18},{16,8},{18,26},{24,16},{26,30},{28,24},... | collective-permute-start | bytes 737288 | tf_op jit(solution)/shard_map/ppermute | solution.py:277
  55.0 1.1 %apply_cells.8.before = f32[2,120,128]{2,1,0:T(8,128)S(1)} custom-call(s32[2,9]{1,0:T(2,128)S(1)} %pad_add_fusion.bounds, s32[2,64]{1,0:T(2,128)S(1)} %get-tuple-element.128.order, s32[2,64]{1,0:T(2,128)S(1)} %get-tuple-element.129.cell, f32[2,120,128]{2,1,0:T(8,128)S(1)} %broadcast_in_dim.87.before, bf16[64,256,128]{2,1,0:T(8,128)(2,1)S(1)} %copy-done.1, ...), custom_call_target="tpu_custom_call" | custom-call | flops 125829120 | bytes 1540096 | tf_op jit(solution)/shard_map/apply_cells/pallas_call | solution.py:142
  56.1 3.1 %collective-permute-done.19.first = bf16[4,120,256]{2,1,0:T(8,128)(2,1)S(1)} collective-permute-done((bf16[4,120,256]{2,1,0:T(8,128)(2,1)S(1)}, bf16[4,120,256]{2,1,0:T(8,128)(2,1)S(1)}, u32[]{:S(2)}, u32[]{:S(2)}) %collective-permute-start.19) | collective-permute-done | bytes 245792 | tf_op jit(solution)/shard_map/ppermute | solution.py:277
  59.2 1.0 %collective-permute-done.20.second = bf16[4,120,256]{2,1,0:T(8,128)(2,1)S(1)} collective-permute-done((bf16[4,120,256]{2,1,0:T(8,128)(2,1)S(1)}, bf16[4,120,256]{2,1,0:T(8,128)(2,1)S(1)}, u32[]{:S(2)}, u32[]{:S(2)}) %collective-permute-start.20) | collective-permute-done | bytes 245792 | tf_op jit(solution)/shard_map/ppermute | solution.py:277
  60.3 1.9 %collective-permute-start.24 = (bf16[4,120,256]{2,1,0:T(8,128)(2,1)S(1)}, bf16[4,120,256]{2,1,0:T(8,128)(2,1)S(1)}, u32[]{:S(2)}, u32[]{:S(2)}) collective-permute-start(bf16[4,120,256]{2,1,0:T(8,128)(2,1)S(1)} %collective-permute-done.19.first), channel_id=1, source_target_pairs={{0,8},{2,6},{8,16},{10,2},{16,24},{18,10},{24,28},{26,18},{28,20},... | collective-permute-start | bytes 737288 | tf_op jit(solution)/shard_map/ppermute | solution.py:284
  62.3 1.5 %apply_cells.9.before = f32[2,120,128]{2,1,0:T(8,128)S(1)} custom-call(s32[2,9]{1,0:T(2,128)S(1)} %pad_add_fusion.bounds, s32[2,64]{1,0:T(2,128)S(1)} %get-tuple-element.128.order, s32[2,64]{1,0:T(2,128)S(1)} %get-tuple-element.129.cell, f32[2,120,128]{2,1,0:T(8,128)S(1)} %apply_cells.8.before, bf16[64,256,128]{2,1,0:T(8,128)(2,1)S(1)} %copy-done.1, ...), custom_call_target="tpu_custom_call" | custom-call | flops 125829120 | bytes 1540096 | tf_op jit(solution)/shard_map/apply_cells/pallas_call | solution.py:142
  63.8 1.7 %collective-permute-done.18.second = bf16[4,120,256]{2,1,0:T(8,128)(2,1)S(1)} collective-permute-done((bf16[4,120,256]{2,1,0:T(8,128)(2,1)S(1)}, bf16[4,120,256]{2,1,0:T(8,128)(2,1)S(1)}, u32[]{:S(2)}, u32[]{:S(2)}) %collective-permute-start.18) | collective-permute-done | bytes 245792 | tf_op jit(solution)/shard_map/ppermute | solution.py:277
  65.5 1.9 %collective-permute-start.22 = (bf16[4,120,256]{2,1,0:T(8,128)(2,1)S(1)}, bf16[4,120,256]{2,1,0:T(8,128)(2,1)S(1)}, u32[]{:S(2)}, u32[]{:S(2)}) collective-permute-start(bf16[4,120,256]{2,1,0:T(8,128)(2,1)S(1)} %collective-permute-done.15.first), channel_id=1, source_target_pairs={{0,8},{2,6},{8,16},{10,2},{16,24},{18,10},{24,28},{26,18},{28,20},... | collective-permute-start | bytes 737288 | tf_op jit(solution)/shard_map/ppermute | solution.py:284
  67.6 1.3 %apply_cells.10.before = f32[2,120,128]{2,1,0:T(8,128)S(1)} custom-call(s32[2,9]{1,0:T(2,128)S(1)} %pad_add_fusion.bounds, s32[2,64]{1,0:T(2,128)S(1)} %get-tuple-element.128.order, s32[2,64]{1,0:T(2,128)S(1)} %get-tuple-element.129.cell, f32[2,120,128]{2,1,0:T(8,128)S(1)} %apply_cells.9.before, bf16[64,256,128]{2,1,0:T(8,128)(2,1)S(1)} %copy-done.1, ...), custom_call_target="tpu_custom_call" | custom-call | flops 125829120 | bytes 1540096 | tf_op jit(solution)/shard_map/apply_cells/pallas_call | solution.py:142
  68.9 0.9 collective-permute-done.24.first
  69.8 1.3 %collective-permute-done.25.second = bf16[4,120,256]{2,1,0:T(8,128)(2,1)S(1)} collective-permute-done((bf16[4,120,256]{2,1,0:T(8,128)(2,1)S(1)}, bf16[4,120,256]{2,1,0:T(8,128)(2,1)S(1)}, u32[]{:S(2)}, u32[]{:S(2)}) %collective-permute-start.25) | collective-permute-done | bytes 245792 | tf_op jit(solution)/shard_map/ppermute | solution.py:284
  71.0 1.6 %collective-permute-start.28 = (bf16[4,120,256]{2,1,0:T(8,128)(2,1)S(1)}, bf16[4,120,256]{2,1,0:T(8,128)(2,1)S(1)}, u32[]{:S(2)}, u32[]{:S(2)}) collective-permute-start(bf16[4,120,256]{2,1,0:T(8,128)(2,1)S(1)} %collective-permute-done.24.first), channel_id=1, source_target_pairs={{0,8},{2,6},{8,16},{10,2},{16,24},{18,10},{24,28},{26,18},{28,20},... | collective-permute-start | bytes 737288 | tf_op jit(solution)/shard_map/ppermute | solution.py:284
  73.1 1.1 %apply_cells.11.before = f32[2,120,128]{2,1,0:T(8,128)S(1)} custom-call(s32[2,9]{1,0:T(2,128)S(1)} %pad_add_fusion.bounds, s32[2,64]{1,0:T(2,128)S(1)} %get-tuple-element.128.order, s32[2,64]{1,0:T(2,128)S(1)} %get-tuple-element.129.cell, f32[2,120,128]{2,1,0:T(8,128)S(1)} %apply_cells.10.before, bf16[64,256,128]{2,1,0:T(8,128)(2,1)S(1)} %copy-done.1, ...), custom_call_target="tpu_custom_call" | custom-call | flops 125829120 | bytes 1540096 | tf_op jit(solution)/shard_map/apply_cells/pallas_call | solution.py:142
  75.0 1.3 %collective-permute-done.23.second = bf16[4,120,256]{2,1,0:T(8,128)(2,1)S(1)} collective-permute-done((bf16[4,120,256]{2,1,0:T(8,128)(2,1)S(1)}, bf16[4,120,256]{2,1,0:T(8,128)(2,1)S(1)}, u32[]{:S(2)}, u32[]{:S(2)}) %collective-permute-start.23) | collective-permute-done | bytes 245792 | tf_op jit(solution)/shard_map/ppermute | solution.py:284
  76.3 1.6 %collective-permute-start.26 = (bf16[4,120,256]{2,1,0:T(8,128)(2,1)S(1)}, bf16[4,120,256]{2,1,0:T(8,128)(2,1)S(1)}, u32[]{:S(2)}, u32[]{:S(2)}) collective-permute-start(bf16[4,120,256]{2,1,0:T(8,128)(2,1)S(1)} %collective-permute-done.22.first), channel_id=1, source_target_pairs={{0,8},{2,6},{8,16},{10,2},{16,24},{18,10},{24,28},{26,18},{28,20},... | collective-permute-start | bytes 737288 | tf_op jit(solution)/shard_map/ppermute | solution.py:284
  78.3 1.5 %apply_cells.12.before = f32[2,120,128]{2,1,0:T(8,128)S(1)} custom-call(s32[2,9]{1,0:T(2,128)S(1)} %pad_add_fusion.bounds, s32[2,64]{1,0:T(2,128)S(1)} %get-tuple-element.128.order, s32[2,64]{1,0:T(2,128)S(1)} %get-tuple-element.129.cell, f32[2,120,128]{2,1,0:T(8,128)S(1)} %apply_cells.11.before, bf16[64,256,128]{2,1,0:T(8,128)(2,1)S(1)} %copy-done.1, ...), custom_call_target="tpu_custom_call" | custom-call | flops 125829120 | bytes 1540096 | tf_op jit(solution)/shard_map/apply_cells/pallas_call | solution.py:142
  80.3 1.3 %collective-permute-done.29.second = bf16[4,120,256]{2,1,0:T(8,128)(2,1)S(1)} collective-permute-done((bf16[4,120,256]{2,1,0:T(8,128)(2,1)S(1)}, bf16[4,120,256]{2,1,0:T(8,128)(2,1)S(1)}, u32[]{:S(2)}, u32[]{:S(2)}) %collective-permute-start.29) | collective-permute-done | bytes 245792 | tf_op jit(solution)/shard_map/ppermute | solution.py:284
  81.6 1.6 %collective-permute-start.30 = (bf16[4,120,256]{2,1,0:T(8,128)(2,1)S(1)}, bf16[4,120,256]{2,1,0:T(8,128)(2,1)S(1)}, u32[]{:S(2)}, u32[]{:S(2)}) collective-permute-start(bf16[4,120,256]{2,1,0:T(8,128)(2,1)S(1)} %collective-permute-done.28.first), channel_id=1, source_target_pairs={{0,8},{2,6},{8,16},{10,2},{16,24},{18,10},{24,28},{26,18},{28,20},... | collective-permute-start | bytes 737288 | tf_op jit(solution)/shard_map/ppermute | solution.py:284
  83.6 2.2 %copy-done.2 = bf16[64,256,128]{2,1,0:T(8,128)(2,1)S(1)} copy-done((bf16[64,256,128]{2,1,0:T(8,128)(2,1)S(1)}, bf16[64,256,128]{2,1,0:T(8,128)(2,1)}, u32[]{:S(2)}) %copy-start.2) | copy-done | bytes 4194328
  85.8 2.2 %copy-done.4 = bf16[64,256,128]{2,1,0:T(8,128)(2,1)S(1)} copy-done((bf16[64,256,128]{2,1,0:T(8,128)(2,1)S(1)}, bf16[64,256,128]{2,1,0:T(8,128)(2,1)}, u32[]{:S(2)}) %copy-start.4) | copy-done | bytes 4194328
  88.0 1.5 %apply_cells.13.before = f32[2,120,128]{2,1,0:T(8,128)S(1)} custom-call(s32[2,9]{1,0:T(2,128)S(1)} %pad_add_fusion.bounds, s32[2,64]{1,0:T(2,128)S(1)} %get-tuple-element.128.order, s32[2,64]{1,0:T(2,128)S(1)} %get-tuple-element.129.cell, f32[2,120,128]{2,1,0:T(8,128)S(1)} %apply_cells.12.before, bf16[64,256,128]{2,1,0:T(8,128)(2,1)S(1)} %copy-done.2, ...), custom_call_target="tpu_custom_call" | custom-call | flops 125829120 | bytes 1540096 | tf_op jit(solution)/shard_map/apply_cells/pallas_call | solution.py:142
  89.5 1.4 %apply_cells.14 = (f32[2,120,128]{2,1,0:T(8,128)S(1)}, bf16[8,256,128]{2,1,0:T(8,128)(2,1)S(1)}, bf16[8,256,128]{2,1,0:T(8,128)(2,1)S(1)}) custom-call(s32[2,9]{1,0:T(2,128)S(1)} %pad_add_fusion.bounds, s32[2,64]{1,0:T(2,128)S(1)} %get-tuple-element.128.order, s32[2,64]{1,0:T(2,128)S(1)} %get-tuple-element.129.cell, f32[2,120,128]{2,1,0:T(8,128)S(1)} %apply_cells.13.before, ...), custom_call_target="tpu_custom_call" | custom-call | flops 125829120 | bytes 1540096 | tf_op jit(solution)/shard_map/apply_cells/pallas_call | solution.py:142
  90.9 1.4 %apply_cells.15 = f32[2,128,120]{2,1,0:T(8,128)S(1)} custom-call(s32[2,9]{1,0:T(2,128)S(1)} %pad_add_fusion.bounds, s32[2,64]{1,0:T(2,128)S(1)} %get-tuple-element.128.order, s32[2,64]{1,0:T(2,128)S(1)} %get-tuple-element.129.cell, f32[2,120,128]{2,1,0:T(8,128)S(1)} %get-tuple-element.80.before, bf16[8,256,128]{2,1,0:T(8,128)(2,1)S(1)} %get-tuple-element.81.mine, ...), custom_call_target="tpu_custom_call" | custom-call | flops 125829120 | bytes 1540096 | tf_op jit(solution)/shard_map/apply_cells/pallas_call | solution.py:142
  92.4 1.3 %collective-permute-start.33 = (f32[64,120]{1,0:T(8,128)S(1)}, f32[64,120]{1,0:T(8,128)S(1)}, u32[]{:S(2)}, u32[]{:S(2)}) collective-permute-start(f32[64,120]{1,0:T(8,128)S(1)} %get-tuple-element.126), channel_id=1, source_target_pairs={{0,1},{1,0},{2,3},{3,2},{4,5},{5,4},{6,7},{7,6},{8,9},{9,8},{10,11... | collective-permute-start | bytes 92168 | tf_op jit(solution)/shard_map/ppermute | solution.py:172
  93.7 0.9 collective-permute-start.32
  94.6 1.8 %collective-permute-done.33 = f32[64,120]{1,0:T(8,128)S(1)} collective-permute-done((f32[64,120]{1,0:T(8,128)S(1)}, f32[64,120]{1,0:T(8,128)S(1)}, u32[]{:S(2)}, u32[]{:S(2)}) %collective-permute-start.33) | collective-permute-done | bytes 30752 | tf_op jit(solution)/shard_map/ppermute | solution.py:172
  96.4 1.0 collective-permute-done.34
  (77 shorter events, 11.5 us)
Async XLA Ops:
  0.0 50.1 %copy-start = (bf16[1,256,256]{2,1,0:T(8,128)(2,1)S(1)}, bf16[1,256,256]{2,1,0:T(8,128)(2,1)}, u32[]{:S(2)}) copy-start(bf16[1,256,256]{2,1,0:T(8,128)(2,1)} %param.9) | copy-start | bytes 393220
  5.1 2.7 %collective-permute-start = (bf16[16,120,256]{2,1,0:T(8,128)(2,1)S(1)}, bf16[16,120,256]{2,1,0:T(8,128)(2,1)S(1)}, u32[]{:S(2)}, u32[]{:S(2)}) collective-permute-start(bf16[16,120,256]{2,1,0:T(8,128)(2,1)S(1)} %get-tuple-element.44), channel_id=1, source_target_pairs={{0,2},{2,0},{4,6},{6,4},{8,10},{10,8},{12,14},{14,12},{16,18},{18,... | collective-permute-start | bytes 2949128 | tf_op jit(solution)/shard_map/ppermute | solution.py:230
  5.6 2.2 %collective-permute-start.1 = (s32[64]{0:T(128)S(1)}, s32[64]{0:T(128)S(1)}, u32[]{:S(2)}, u32[]{:S(2)}) collective-permute-start(s32[64]{0:T(128)S(1)} %get-tuple-element.127), channel_id=1, source_target_pairs={{0,2},{2,0},{4,6},{6,4},{8,10},{10,8},{12,14},{14,12},{16,18},{18,... | collective-permute-start | bytes 776 | tf_op jit(solution)/shard_map/ppermute | solution.py:232
  7.8 6.0 %collective-permute-start.4 = (bf16[48,120,256]{2,1,0:T(8,128)(2,1)S(1)}, bf16[48,120,256]{2,1,0:T(8,128)(2,1)S(1)}, u32[]{:S(2)}, u32[]{:S(2)}) collective-permute-start(bf16[48,120,256]{2,1,0:T(8,128)(2,1)S(1)} %get-tuple-element.50), channel_id=1, source_target_pairs={{0,2},{2,0},{4,6},{6,4},{8,10},{10,8},{12,14},{14,12},{16,18},{18,... | collective-permute-start | bytes 8847368 | tf_op jit(solution)/shard_map/ppermute | solution.py:230
  8.2 5.7 %copy-start.1 = (bf16[64,256,128]{2,1,0:T(8,128)(2,1)S(1)}, bf16[64,256,128]{2,1,0:T(8,128)(2,1)}, u32[]{:S(2)}) copy-start(bf16[64,256,128]{2,1,0:T(8,128)(2,1)} %mine.13) | copy-start | bytes 12582916
  8.9 8.9 %collective-permute-start.3 = (bf16[4,120,256]{2,1,0:T(8,128)(2,1)S(1)}, bf16[4,120,256]{2,1,0:T(8,128)(2,1)S(1)}, u32[]{:S(2)}, u32[]{:S(2)}) collective-permute-start(bf16[4,120,256]{2,1,0:T(8,128)(2,1)S(1)} %add_convert_fusion.14), channel_id=1, source_target_pairs={{0,4},{2,10},{8,0},{10,18},{16,8},{18,26},{24,16},{26,30},{28,24},... | collective-permute-start | bytes 737288 | tf_op jit(solution)/shard_map/ppermute | solution.py:254
  11.6 8.9 %collective-permute-start.2 = (bf16[4,120,256]{2,1,0:T(8,128)(2,1)S(1)}, bf16[4,120,256]{2,1,0:T(8,128)(2,1)S(1)}, u32[]{:S(2)}, u32[]{:S(2)}) collective-permute-start(bf16[4,120,256]{2,1,0:T(8,128)(2,1)S(1)} %add_convert_fusion.15), channel_id=1, source_target_pairs={{0,8},{2,6},{8,16},{10,2},{16,24},{18,10},{24,28},{26,18},{28,20},... | collective-permute-start | bytes 737288 | tf_op jit(solution)/shard_map/ppermute | solution.py:254
  11.9 11.3 %collective-permute-start.8 = (bf16[4,120,256]{2,1,0:T(8,128)(2,1)S(1)}, bf16[4,120,256]{2,1,0:T(8,128)(2,1)S(1)}, u32[]{:S(2)}, u32[]{:S(2)}) collective-permute-start(bf16[4,120,256]{2,1,0:T(8,128)(2,1)S(1)} %add_convert_fusion.12), channel_id=1, source_target_pairs={{0,4},{2,10},{8,0},{10,18},{16,8},{18,26},{24,16},{26,30},{28,24},... | collective-permute-start | bytes 737288 | tf_op jit(solution)/shard_map/ppermute | solution.py:254
  13.8 41.2 %collective-permute-start.21 = (bf16[64,256,128]{2,1,0:T(8,128)(2,1)S(1)}, bf16[64,256,128]{2,1,0:T(8,128)(2,1)S(1)}, u32[]{:S(2)}, u32[]{:S(2)}) collective-permute-start(bf16[64,256,128]{2,1,0:T(8,128)(2,1)S(1)} %copy-done.1), channel_id=1, source_target_pairs={{0,2},{2,0},{4,6},{6,4},{8,10},{10,8},{12,14},{14,12},{16,18},{18,... | collective-permute-start | bytes 12582920 | tf_op jit(solution)/shard_map/ppermute | solution.py:236
  13.9 9.8 %collective-permute-start.7 = (bf16[4,120,256]{2,1,0:T(8,128)(2,1)S(1)}, bf16[4,120,256]{2,1,0:T(8,128)(2,1)S(1)}, u32[]{:S(2)}, u32[]{:S(2)}) collective-permute-start(bf16[4,120,256]{2,1,0:T(8,128)(2,1)S(1)} %add_convert_fusion.13), channel_id=1, source_target_pairs={{0,8},{2,6},{8,16},{10,2},{16,24},{18,10},{24,28},{26,18},{28,20},... | collective-permute-start | bytes 737288 | tf_op jit(solution)/shard_map/ppermute | solution.py:254
  20.9 8.7 %collective-permute-start.6 = (bf16[4,120,256]{2,1,0:T(8,128)(2,1)S(1)}, bf16[4,120,256]{2,1,0:T(8,128)(2,1)S(1)}, u32[]{:S(2)}, u32[]{:S(2)}) collective-permute-start(bf16[4,120,256]{2,1,0:T(8,128)(2,1)S(1)} %add_convert_fusion.10), channel_id=1, source_target_pairs={{0,4},{2,10},{8,0},{10,18},{16,8},{18,26},{24,16},{26,30},{28,24},... | collective-permute-start | bytes 737288 | tf_op jit(solution)/shard_map/ppermute | solution.py:254
  22.6 8.5 %collective-permute-start.5 = (bf16[4,120,256]{2,1,0:T(8,128)(2,1)S(1)}, bf16[4,120,256]{2,1,0:T(8,128)(2,1)S(1)}, u32[]{:S(2)}, u32[]{:S(2)}) collective-permute-start(bf16[4,120,256]{2,1,0:T(8,128)(2,1)S(1)} %add_convert_fusion.11), channel_id=1, source_target_pairs={{0,8},{2,6},{8,16},{10,2},{16,24},{18,10},{24,28},{26,18},{28,20},... | collective-permute-start | bytes 737288 | tf_op jit(solution)/shard_map/ppermute | solution.py:254
  23.9 11.0 %collective-permute-start.12 = (bf16[4,120,256]{2,1,0:T(8,128)(2,1)S(1)}, bf16[4,120,256]{2,1,0:T(8,128)(2,1)S(1)}, u32[]{:S(2)}, u32[]{:S(2)}) collective-permute-start(bf16[4,120,256]{2,1,0:T(8,128)(2,1)S(1)} %add_convert_fusion.8), channel_id=1, source_target_pairs={{0,4},{2,10},{8,0},{10,18},{16,8},{18,26},{24,16},{26,30},{28,24},... | collective-permute-start | bytes 737288 | tf_op jit(solution)/shard_map/ppermute | solution.py:254
  27.5 8.6 %collective-permute-start.11 = (bf16[4,120,256]{2,1,0:T(8,128)(2,1)S(1)}, bf16[4,120,256]{2,1,0:T(8,128)(2,1)S(1)}, u32[]{:S(2)}, u32[]{:S(2)}) collective-permute-start(bf16[4,120,256]{2,1,0:T(8,128)(2,1)S(1)} %add_convert_fusion.9), channel_id=1, source_target_pairs={{0,8},{2,6},{8,16},{10,2},{16,24},{18,10},{24,28},{26,18},{28,20},... | collective-permute-start | bytes 737288 | tf_op jit(solution)/shard_map/ppermute | solution.py:254
  31.3 8.9 %collective-permute-start.10 = (bf16[4,120,256]{2,1,0:T(8,128)(2,1)S(1)}, bf16[4,120,256]{2,1,0:T(8,128)(2,1)S(1)}, u32[]{:S(2)}, u32[]{:S(2)}) collective-permute-start(bf16[4,120,256]{2,1,0:T(8,128)(2,1)S(1)} %add_convert_fusion.6), channel_id=1, source_target_pairs={{0,4},{2,10},{8,0},{10,18},{16,8},{18,26},{24,16},{26,30},{28,24},... | collective-permute-start | bytes 737288 | tf_op jit(solution)/shard_map/ppermute | solution.py:254
  33.3 8.4 %collective-permute-start.9 = (bf16[4,120,256]{2,1,0:T(8,128)(2,1)S(1)}, bf16[4,120,256]{2,1,0:T(8,128)(2,1)S(1)}, u32[]{:S(2)}, u32[]{:S(2)}) collective-permute-start(bf16[4,120,256]{2,1,0:T(8,128)(2,1)S(1)} %add_convert_fusion.7), channel_id=1, source_target_pairs={{0,8},{2,6},{8,16},{10,2},{16,24},{18,10},{24,28},{26,18},{28,20},... | collective-permute-start | bytes 737288 | tf_op jit(solution)/shard_map/ppermute | solution.py:254
  36.3 9.2 %collective-permute-start.16 = (bf16[4,120,256]{2,1,0:T(8,128)(2,1)S(1)}, bf16[4,120,256]{2,1,0:T(8,128)(2,1)S(1)}, u32[]{:S(2)}, u32[]{:S(2)}) collective-permute-start(bf16[4,120,256]{2,1,0:T(8,128)(2,1)S(1)} %add_convert_fusion.4), channel_id=1, source_target_pairs={{0,4},{2,10},{8,0},{10,18},{16,8},{18,26},{24,16},{26,30},{28,24},... | collective-permute-start | bytes 737288 | tf_op jit(solution)/shard_map/ppermute | solution.py:254
  38.6 13.2 %collective-permute-start.14 = (bf16[4,120,256]{2,1,0:T(8,128)(2,1)S(1)}, bf16[4,120,256]{2,1,0:T(8,128)(2,1)S(1)}, u32[]{:S(2)}, u32[]{:S(2)}) collective-permute-start(bf16[4,120,256]{2,1,0:T(8,128)(2,1)S(1)} %add_convert_fusion.5), channel_id=1, source_target_pairs={{0,8},{2,6},{8,16},{10,2},{16,24},{18,10},{24,28},{26,18},{28,20},... | collective-permute-start | bytes 737288 | tf_op jit(solution)/shard_map/ppermute | solution.py:254
  41.9 8.2 %collective-permute-start.17 = (bf16[4,120,256]{2,1,0:T(8,128)(2,1)S(1)}, bf16[4,120,256]{2,1,0:T(8,128)(2,1)S(1)}, u32[]{:S(2)}, u32[]{:S(2)}) collective-permute-start(bf16[4,120,256]{2,1,0:T(8,128)(2,1)S(1)} %add_convert_fusion.1), channel_id=1, source_target_pairs={{0,8},{2,6},{8,16},{10,2},{16,24},{18,10},{24,28},{26,18},{28,20},... | collective-permute-start | bytes 737288 | tf_op jit(solution)/shard_map/ppermute | solution.py:254
  42.2 9.7 %collective-permute-start.13 = (bf16[4,120,256]{2,1,0:T(8,128)(2,1)S(1)}, bf16[4,120,256]{2,1,0:T(8,128)(2,1)S(1)}, u32[]{:S(2)}, u32[]{:S(2)}) collective-permute-start(bf16[4,120,256]{2,1,0:T(8,128)(2,1)S(1)} %add_convert_fusion.3), channel_id=1, source_target_pairs={{0,4},{2,10},{8,0},{10,18},{16,8},{18,26},{24,16},{26,30},{28,24},... | collective-permute-start | bytes 737288 | tf_op jit(solution)/shard_map/ppermute | solution.py:254
  50.4 8.8 %collective-permute-start.19 = (bf16[4,120,256]{2,1,0:T(8,128)(2,1)S(1)}, bf16[4,120,256]{2,1,0:T(8,128)(2,1)S(1)}, u32[]{:S(2)}, u32[]{:S(2)}) collective-permute-start(bf16[4,120,256]{2,1,0:T(8,128)(2,1)S(1)} %convolution_convert_fusion.first), channel_id=1, source_target_pairs={{0,8},{2,6},{8,16},{10,2},{16,24},{18,10},{24,28},{26,18},{28,20},... | collective-permute-start | bytes 737288 | tf_op jit(solution)/shard_map/ppermute | solution.py:277
  52.1 8.2 %collective-permute-start.20 = (bf16[4,120,256]{2,1,0:T(8,128)(2,1)S(1)}, bf16[4,120,256]{2,1,0:T(8,128)(2,1)S(1)}, u32[]{:S(2)}, u32[]{:S(2)}) collective-permute-start(bf16[4,120,256]{2,1,0:T(8,128)(2,1)S(1)} %convolution_convert_fusion.1.second), channel_id=1, source_target_pairs={{0,4},{2,10},{8,0},{10,18},{16,8},{18,26},{24,16},{26,30},{28,24},... | collective-permute-start | bytes 737288 | tf_op jit(solution)/shard_map/ppermute | solution.py:277
  52.9 12.6 %collective-permute-start.18 = (bf16[4,120,256]{2,1,0:T(8,128)(2,1)S(1)}, bf16[4,120,256]{2,1,0:T(8,128)(2,1)S(1)}, u32[]{:S(2)}, u32[]{:S(2)}) collective-permute-start(bf16[4,120,256]{2,1,0:T(8,128)(2,1)S(1)} %convolution_convert_fusion.first), channel_id=1, source_target_pairs={{0,4},{2,10},{8,0},{10,18},{16,8},{18,26},{24,16},{26,30},{28,24},... | collective-permute-start | bytes 737288 | tf_op jit(solution)/shard_map/ppermute | solution.py:277
  54.5 11.0 %collective-permute-start.15 = (bf16[4,120,256]{2,1,0:T(8,128)(2,1)S(1)}, bf16[4,120,256]{2,1,0:T(8,128)(2,1)S(1)}, u32[]{:S(2)}, u32[]{:S(2)}) collective-permute-start(bf16[4,120,256]{2,1,0:T(8,128)(2,1)S(1)} %convolution_convert_fusion.1.second), channel_id=1, source_target_pairs={{0,8},{2,6},{8,16},{10,2},{16,24},{18,10},{24,28},{26,18},{28,20},... | collective-permute-start | bytes 737288 | tf_op jit(solution)/shard_map/ppermute | solution.py:277
  55.0 23.3 %copy-start.3 = (bf16[64,256,128]{2,1,0:T(8,128)(2,1)}, bf16[64,256,128]{2,1,0:T(8,128)(2,1)S(1)}, u32[]{:S(2)}) copy-start(bf16[64,256,128]{2,1,0:T(8,128)(2,1)S(1)} %collective-permute-done.21.other) | copy-start | bytes 12582916
  60.3 9.5 %collective-permute-start.24 = (bf16[4,120,256]{2,1,0:T(8,128)(2,1)S(1)}, bf16[4,120,256]{2,1,0:T(8,128)(2,1)S(1)}, u32[]{:S(2)}, u32[]{:S(2)}) collective-permute-start(bf16[4,120,256]{2,1,0:T(8,128)(2,1)S(1)} %collective-permute-done.19.first), channel_id=1, source_target_pairs={{0,8},{2,6},{8,16},{10,2},{16,24},{18,10},{24,28},{26,18},{28,20},... | collective-permute-start | bytes 737288 | tf_op jit(solution)/shard_map/ppermute | solution.py:284
  62.1 8.9 %collective-permute-start.25 = (bf16[4,120,256]{2,1,0:T(8,128)(2,1)S(1)}, bf16[4,120,256]{2,1,0:T(8,128)(2,1)S(1)}, u32[]{:S(2)}, u32[]{:S(2)}) collective-permute-start(bf16[4,120,256]{2,1,0:T(8,128)(2,1)S(1)} %collective-permute-done.20.second), channel_id=1, source_target_pairs={{0,4},{2,10},{8,0},{10,18},{16,8},{18,26},{24,16},{26,30},{28,24},... | collective-permute-start | bytes 737288 | tf_op jit(solution)/shard_map/ppermute | solution.py:284
  65.5 9.5 %collective-permute-start.22 = (bf16[4,120,256]{2,1,0:T(8,128)(2,1)S(1)}, bf16[4,120,256]{2,1,0:T(8,128)(2,1)S(1)}, u32[]{:S(2)}, u32[]{:S(2)}) collective-permute-start(bf16[4,120,256]{2,1,0:T(8,128)(2,1)S(1)} %collective-permute-done.15.first), channel_id=1, source_target_pairs={{0,8},{2,6},{8,16},{10,2},{16,24},{18,10},{24,28},{26,18},{28,20},... | collective-permute-start | bytes 737288 | tf_op jit(solution)/shard_map/ppermute | solution.py:284
  67.4 8.9 %collective-permute-start.23 = (bf16[4,120,256]{2,1,0:T(8,128)(2,1)S(1)}, bf16[4,120,256]{2,1,0:T(8,128)(2,1)S(1)}, u32[]{:S(2)}, u32[]{:S(2)}) collective-permute-start(bf16[4,120,256]{2,1,0:T(8,128)(2,1)S(1)} %collective-permute-done.18.second), channel_id=1, source_target_pairs={{0,4},{2,10},{8,0},{10,18},{16,8},{18,26},{24,16},{26,30},{28,24},... | collective-permute-start | bytes 737288 | tf_op jit(solution)/shard_map/ppermute | solution.py:284
  71.0 9.3 %collective-permute-start.28 = (bf16[4,120,256]{2,1,0:T(8,128)(2,1)S(1)}, bf16[4,120,256]{2,1,0:T(8,128)(2,1)S(1)}, u32[]{:S(2)}, u32[]{:S(2)}) collective-permute-start(bf16[4,120,256]{2,1,0:T(8,128)(2,1)S(1)} %collective-permute-done.24.first), channel_id=1, source_target_pairs={{0,8},{2,6},{8,16},{10,2},{16,24},{18,10},{24,28},{26,18},{28,20},... | collective-permute-start | bytes 737288 | tf_op jit(solution)/shard_map/ppermute | solution.py:284
  72.7 8.9 %collective-permute-start.29 = (bf16[4,120,256]{2,1,0:T(8,128)(2,1)S(1)}, bf16[4,120,256]{2,1,0:T(8,128)(2,1)S(1)}, u32[]{:S(2)}, u32[]{:S(2)}) collective-permute-start(bf16[4,120,256]{2,1,0:T(8,128)(2,1)S(1)} %collective-permute-done.25.second), channel_id=1, source_target_pairs={{0,4},{2,10},{8,0},{10,18},{16,8},{18,26},{24,16},{26,30},{28,24},... | collective-permute-start | bytes 737288 | tf_op jit(solution)/shard_map/ppermute | solution.py:284
  76.3 13.2 %collective-permute-start.26 = (bf16[4,120,256]{2,1,0:T(8,128)(2,1)S(1)}, bf16[4,120,256]{2,1,0:T(8,128)(2,1)S(1)}, u32[]{:S(2)}, u32[]{:S(2)}) collective-permute-start(bf16[4,120,256]{2,1,0:T(8,128)(2,1)S(1)} %collective-permute-done.22.first), channel_id=1, source_target_pairs={{0,8},{2,6},{8,16},{10,2},{16,24},{18,10},{24,28},{26,18},{28,20},... | collective-permute-start | bytes 737288 | tf_op jit(solution)/shard_map/ppermute | solution.py:284
  77.9 11.6 %collective-permute-start.27 = (bf16[4,120,256]{2,1,0:T(8,128)(2,1)S(1)}, bf16[4,120,256]{2,1,0:T(8,128)(2,1)S(1)}, u32[]{:S(2)}, u32[]{:S(2)}) collective-permute-start(bf16[4,120,256]{2,1,0:T(8,128)(2,1)S(1)} %collective-permute-done.23.second), channel_id=1, source_target_pairs={{0,4},{2,10},{8,0},{10,18},{16,8},{18,26},{24,16},{26,30},{28,24},... | collective-permute-start | bytes 737288 | tf_op jit(solution)/shard_map/ppermute | solution.py:284
  81.6 9.3 %collective-permute-start.30 = (bf16[4,120,256]{2,1,0:T(8,128)(2,1)S(1)}, bf16[4,120,256]{2,1,0:T(8,128)(2,1)S(1)}, u32[]{:S(2)}, u32[]{:S(2)}) collective-permute-start(bf16[4,120,256]{2,1,0:T(8,128)(2,1)S(1)} %collective-permute-done.28.first), channel_id=1, source_target_pairs={{0,8},{2,6},{8,16},{10,2},{16,24},{18,10},{24,28},{26,18},{28,20},... | collective-permute-start | bytes 737288 | tf_op jit(solution)/shard_map/ppermute | solution.py:284
  83.2 7.7 %collective-permute-start.31 = (bf16[4,120,256]{2,1,0:T(8,128)(2,1)S(1)}, bf16[4,120,256]{2,1,0:T(8,128)(2,1)S(1)}, u32[]{:S(2)}, u32[]{:S(2)}) collective-permute-start(bf16[4,120,256]{2,1,0:T(8,128)(2,1)S(1)} %collective-permute-done.29.second), channel_id=1, source_target_pairs={{0,4},{2,10},{8,0},{10,18},{16,8},{18,26},{24,16},{26,30},{28,24},... | collective-permute-start | bytes 737288 | tf_op jit(solution)/shard_map/ppermute | solution.py:284
  83.6 2.2 %copy-start.2 = (bf16[64,256,128]{2,1,0:T(8,128)(2,1)S(1)}, bf16[64,256,128]{2,1,0:T(8,128)(2,1)}, u32[]{:S(2)}) copy-start(bf16[64,256,128]{2,1,0:T(8,128)(2,1)} %mine.13) | copy-start | bytes 12582916
  85.8 2.2 %copy-start.4 = (bf16[64,256,128]{2,1,0:T(8,128)(2,1)S(1)}, bf16[64,256,128]{2,1,0:T(8,128)(2,1)}, u32[]{:S(2)}) copy-start(bf16[64,256,128]{2,1,0:T(8,128)(2,1)} %copy-done.3) | copy-start | bytes 12582916
  92.4 4.0 %collective-permute-start.33 = (f32[64,120]{1,0:T(8,128)S(1)}, f32[64,120]{1,0:T(8,128)S(1)}, u32[]{:S(2)}, u32[]{:S(2)}) collective-permute-start(f32[64,120]{1,0:T(8,128)S(1)} %get-tuple-element.126), channel_id=1, source_target_pairs={{0,1},{1,0},{2,3},{3,2},{4,5},{5,4},{6,7},{7,6},{8,9},{9,8},{10,11... | collective-permute-start | bytes 92168 | tf_op jit(solution)/shard_map/ppermute | solution.py:172
  93.7 3.6 %collective-permute-start.34 = (f32[64,120]{1,0:T(8,128)S(1)}, f32[64,120]{1,0:T(8,128)S(1)}, u32[]{:S(2)}, u32[]{:S(2)}) collective-permute-start(f32[64,120]{1,0:T(8,128)S(1)} %get-tuple-element.125), channel_id=1, source_target_pairs={{0,3},{1,2},{2,1},{3,0},{4,7},{5,6},{6,5},{7,4},{8,11},{9,10},{10,... | collective-permute-start | bytes 92168 | tf_op jit(solution)/shard_map/ppermute | solution.py:173
  93.7 3.6 %collective-permute-start.32 = (f32[64,120]{1,0:T(8,128)S(1)}, f32[64,120]{1,0:T(8,128)S(1)}, u32[]{:S(2)}, u32[]{:S(2)}) collective-permute-start(f32[64,120]{1,0:T(8,128)S(1)} %slice_bitcast_fusion.2), channel_id=1, source_target_pairs={{0,2},{2,0},{4,6},{6,4},{8,10},{10,8},{12,14},{14,12},{16,18},{18,... | collective-permute-start | bytes 92168 | tf_op jit(solution)/shard_map/ppermute | solution.py:174

commit v5 on v4

--- a/solution.py
+++ b/solution.py
@@ -55,15 +55,12 @@
     for c, (first, stop) in enumerate(zip(edges, edges[1:])):
         copies[1 + c].wait()
         for start in range(first, stop, GROUP):
-            halves = [
-                lax.dot_general(
-                    rows_in[...],
-                    blocks[b],
-                    (((1,), (1,)), ((), ())),
-                    preferred_element_type=jnp.float32,
-                )
-                for b in range(start, start + GROUP)
-            ]
+            width = blocks.shape[1]
+            group = blocks[start : start + GROUP].reshape(GROUP * width, blocks.shape[2])
+            product = lax.dot_general(
+                rows_in[...], group, (((1,), (1,)), ((), ())), preferred_element_type=jnp.float32
+            )
+            halves = [product[:, u * width : (u + 1) * width] for u in range(GROUP)]
             for b, half in zip(range(start, start + GROUP), halves):
                 here = cell[b]
                 half = half.astype(jnp.bfloat16).astype(jnp.float32)
@@ -218,25 +215,27 @@
 
     apart = lax.optimization_barrier
     capacity = 2 * block_count // owners
-    early = [(r, h) for pair, step in turns[:2] for r, h in ((step, pair[0]), (chips - step, pair[1]))]
+    early = [(r, h) for pair, step in turns[:1] for r, h in ((step, pair[0]), (chips - step, pair[1]))]
     parts = [early, [way for way in numbers if way not in early]]
     sends = []
     for part in parts:
         starts = [held_cells + numbers[way] * half_slots for way in part]
         sends.append([c for start in starts for c in range(start, start + half_slots)])
-    sums, *others = sum_cells(cell, again, tens, coef, 2 * held_cells, sends)
+    starts = [numbers[way] * half_slots for way in early]
+    kept = [[c for c in range(start, start + half_slots)] for start in starts]
+    sums, *others = sum_cells(cell, again, tens, coef, 2 * held_cells, sends + kept)
     local = {}
     for p, part in enumerate(parts):
         got = across(others[p])
         if p == 0:
             other_names = across(target * slots + slot_of)
-            got, other_names, *others[1:] = apart((got, other_names, *others[1:]))
+            got, other_names, others[1] = apart((got, other_names, others[1]))
         if p == 1:
             got, tens_out = apart((got, tens))
             other_tens = across(tens_out)
         for k, way in enumerate(part):
             start = numbers[way] * half_slots
-            mine = apart(sums[start : start + half_slots])
+            mine = others[2 + k] if p == 0 else apart(sums[start : start + half_slots])
             other = apart(got[k * half_slots : (k + 1) * half_slots])
             local[way] = mine.astype(jnp.float32) + other.astype(jnp.float32)
 
@@ -248,6 +247,8 @@
         ahead, back = up[pair[0]], down[pair[1]]
         if ahead is not None:
             ahead, back, *sent = apart((ahead, back, *sent))
+            if (pair, step) == turns[3]:
+                ahead, names, other_names = apart((ahead, target * slots + slot_of, other_names))
         ahead = add(ahead, local[step, pair[0]]).astype(jnp.bfloat16)
         back = add(back, local[chips - step, pair[1]]).astype(jnp.bfloat16)
         sent = (ahead, back)
@@ -263,7 +264,7 @@
         )
 
     tables = []
-    for aux, slot in ((target, slot_of), (other_names // slots, other_names % slots)):
+    for aux, slot in ((n // slots, n % slots) for n in (names, other_names)):
         held = jnp.where(aux % 2 == core, cell_of(aux, slot), held_cells)
         key = held * block_count + series
         rank = jnp.sum(jnp.where(key[None, :] < key[:, None], 1, 0), axis=1)

time: 98.1 us -> 97.3 us (level)
    ppermute x24, waiting for transfers between devices: 25.8 us -> 23 us  [cells_body(): up[pair[0]], down[pair[1]] = (forward(ahead), backward(back))]
    ppermute x2, waiting for transfers between devices: 0.01 us -> 2.46 us  [cells_body(): got = across(others[p])]
    ppermute x2, waiting for transfers between devices: 2.76 us -> 3.91 us  [cells_body(): backward(own[h])]
  transfers between devices with their start and end apart: 35 -> 35, of which waited for: 23 -> 21; matrix products, arithmetic and copies ran while one was open for 3% -> 3% of each run, Pallas kernels for 10% -> 9%
where the time goes in v5:
time: 97.3 us; the launch traced here: 97.1 us
  starting transfers between devices  36.8 us (38%)
  waiting for transfers between devices  36.4 us (37%)
  Pallas kernels  14.5 us (15%)
  local copies, waits for them, and re-layouts  4.9 us (5%)
  other arithmetic  3.64 us (4%)
    ppermute x24, starting transfers between devices, cells_body(): up[pair[0]], down[pair[1]] = (forward(ahead), backward(back))  29 us
    ppermute x24, waiting for transfers between devices, cells_body(): up[pair[0]], down[pair[1]] = (forward(ahead), backward(back))  23 us
    pallas_call x8, Pallas kernels, apply_cells(): pl.pallas_call(functools.partial(apply_cells_kernel, group, takes, turned...  10.3 us
    unnamed x10, local copies, waits for them, and re-layouts  4.39 us
    pallas_call x1, Pallas kernels, sum_cells(): pl.pallas_call(functools.partial(sum_cells_kernel, sends), out_shape=tupl...  4.18 us
    ppermute x2, waiting for transfers between devices, cells_body(): backward(own[h])  3.91 us
    ppermute x2, starting transfers between devices, cells_body(): forward(own[h])  2.89 us
    ppermute x2, waiting for transfers between devices, cells_body(): forward(own[h])  2.56 us
  transfers between devices with their start and end apart: 35, of which 21 were waited for; matrix products, arithmetic and copies ran while one was open for 3% of the time, Pallas kernels for 9%

profile of v5, /device:TPU:0, one launch (start us, length us, event | category | flops | bytes accessed | tf_op | source)
XLA Modules:
  0.0 97.1 jit_solution(18255876792874082006)
XLA Ops:
  0.0 0.7 fusion.22
  0.9 4.2 %sum_cells.1 = (bf16[128,120,256]{2,1,0:T(8,128)(2,1)S(1)}, bf16[8,120,256]{2,1,0:T(8,128)(2,1)S(1)}, bf16[56,120,256]{2,1,0:T(8,128)(2,1)S(1)}, bf16[4,120,256]...) custom-call(s32[64]{0:T(128)S(1)} %get-tuple-element.134.cell, s32[64]{0:T(128)S(1)} %select_reduce_fusion.4.again, ...), custom_call_target="tpu_custom_call" | custom-call | flops 503316480 | bytes 12058624 | tf_op jit(solution)/shard_map/sum_cells/pallas_call | solution.py:80
  5.7 1.4 %collective-permute-done.1 = s32[64]{0:T(128)S(1)} collective-permute-done((s32[64]{0:T(128)S(1)}, s32[64]{0:T(128)S(1)}, u32[]{:S(2)}, u32[]{:S(2)}) %collective-permute-start.1) | collective-permute-done | bytes 288 | tf_op jit(solution)/shard_map/ppermute | solution.py:231
  7.9 2.7 %collective-permute-start.6 = (bf16[4,120,256]{2,1,0:T(8,128)(2,1)S(1)}, bf16[4,120,256]{2,1,0:T(8,128)(2,1)S(1)}, u32[]{:S(2)}, u32[]{:S(2)}) collective-permute-start(bf16[4,120,256]{2,1,0:T(8,128)(2,1)S(1)} %add_convert_fusion.12), channel_id=1, source_target_pairs={{0,4},{2,10},{8,0},{10,18},{16,8},{18,26},{24,16},{26,30},{28,24},... | collective-permute-start | bytes 737288 | tf_op jit(solution)/shard_map/ppermute | solution.py:255
  10.8 2.5 %collective-permute-done.2 = bf16[56,120,256]{2,1,0:T(8,128)(2,1)S(1)} collective-permute-done((bf16[56,120,256]{2,1,0:T(8,128)(2,1)S(1)}, bf16[56,120,256]{2,1,0:T(8,128)(2,1)S(1)}, u32[]{:S(2)}, u32[]{:S(2)}) %collective-permute-start.2) | collective-permute-done | bytes 3440672 | tf_op jit(solution)/shard_map/ppermute | solution.py:229
  13.5 2.9 %collective-permute-start.4 = (bf16[4,120,256]{2,1,0:T(8,128)(2,1)S(1)}, bf16[4,120,256]{2,1,0:T(8,128)(2,1)S(1)}, u32[]{:S(2)}, u32[]{:S(2)}) collective-permute-start(bf16[4,120,256]{2,1,0:T(8,128)(2,1)S(1)} %add_convert_fusion.14), channel_id=1, source_target_pairs={{0,4},{2,10},{8,0},{10,18},{16,8},{18,26},{24,16},{26,30},{28,24},... | collective-permute-start | bytes 737288 | tf_op jit(solution)/shard_map/ppermute | solution.py:255
  16.5 1.6 %collective-permute-start.3 = (bf16[4,120,256]{2,1,0:T(8,128)(2,1)S(1)}, bf16[4,120,256]{2,1,0:T(8,128)(2,1)S(1)}, u32[]{:S(2)}, u32[]{:S(2)}) collective-permute-start(bf16[4,120,256]{2,1,0:T(8,128)(2,1)S(1)} %add_convert_fusion.15), channel_id=1, source_target_pairs={{0,8},{2,6},{8,16},{10,2},{16,24},{18,10},{24,28},{26,18},{28,20},... | collective-permute-start | bytes 737288 | tf_op jit(solution)/shard_map/ppermute | solution.py:255
  18.2 1.0 collective-permute-start.8
  19.2 1.2 %collective-permute-start.7 = (bf16[4,120,256]{2,1,0:T(8,128)(2,1)S(1)}, bf16[4,120,256]{2,1,0:T(8,128)(2,1)S(1)}, u32[]{:S(2)}, u32[]{:S(2)}) collective-permute-start(bf16[4,120,256]{2,1,0:T(8,128)(2,1)S(1)} %add_convert_fusion.11), channel_id=1, source_target_pairs={{0,8},{2,6},{8,16},{10,2},{16,24},{18,10},{24,28},{26,18},{28,20},... | collective-permute-start | bytes 737288 | tf_op jit(solution)/shard_map/ppermute | solution.py:255
  20.4 1.3 %collective-permute-done.4 = bf16[4,120,256]{2,1,0:T(8,128)(2,1)S(1)} collective-permute-done((bf16[4,120,256]{2,1,0:T(8,128)(2,1)S(1)}, bf16[4,120,256]{2,1,0:T(8,128)(2,1)S(1)}, u32[]{:S(2)}, u32[]{:S(2)}) %collective-permute-start.4) | collective-permute-done | bytes 245792 | tf_op jit(solution)/shard_map/ppermute | solution.py:255
  21.7 2.8 %collective-permute-done.3 = bf16[4,120,256]{2,1,0:T(8,128)(2,1)S(1)} collective-permute-done((bf16[4,120,256]{2,1,0:T(8,128)(2,1)S(1)}, bf16[4,120,256]{2,1,0:T(8,128)(2,1)S(1)}, u32[]{:S(2)}, u32[]{:S(2)}) %collective-permute-start.3) | collective-permute-done | bytes 245792 | tf_op jit(solution)/shard_map/ppermute | solution.py:255
  24.6 1.7 %collective-permute-start.12 = (bf16[4,120,256]{2,1,0:T(8,128)(2,1)S(1)}, bf16[4,120,256]{2,1,0:T(8,128)(2,1)S(1)}, u32[]{:S(2)}, u32[]{:S(2)}) collective-permute-start(bf16[4,120,256]{2,1,0:T(8,128)(2,1)S(1)} %add_convert_fusion.8), channel_id=1, source_target_pairs={{0,4},{2,10},{8,0},{10,18},{16,8},{18,26},{24,16},{26,30},{28,24},... | collective-permute-start | bytes 737288 | tf_op jit(solution)/shard_map/ppermute | solution.py:255
  26.4 0.9 collective-permute-start.11
  27.3 1.0 %collective-permute-done.7 = bf16[4,120,256]{2,1,0:T(8,128)(2,1)S(1)} collective-permute-done((bf16[4,120,256]{2,1,0:T(8,128)(2,1)S(1)}, bf16[4,120,256]{2,1,0:T(8,128)(2,1)S(1)}, u32[]{:S(2)}, u32[]{:S(2)}) %collective-permute-start.7) | collective-permute-done | bytes 245792 | tf_op jit(solution)/shard_map/ppermute | solution.py:255
  28.4 1.7 %collective-permute-start.10 = (bf16[4,120,256]{2,1,0:T(8,128)(2,1)S(1)}, bf16[4,120,256]{2,1,0:T(8,128)(2,1)S(1)}, u32[]{:S(2)}, u32[]{:S(2)}) collective-permute-start(bf16[4,120,256]{2,1,0:T(8,128)(2,1)S(1)} %add_convert_fusion.6), channel_id=1, source_target_pairs={{0,4},{2,10},{8,0},{10,18},{16,8},{18,26},{24,16},{26,30},{28,24},... | collective-permute-start | bytes 737288 | tf_op jit(solution)/shard_map/ppermute | solution.py:255
  30.2 0.9 collective-permute-start.9
  31.8 2.2 %collective-permute-done.12 = bf16[4,120,256]{2,1,0:T(8,128)(2,1)S(1)} collective-permute-done((bf16[4,120,256]{2,1,0:T(8,128)(2,1)S(1)}, bf16[4,120,256]{2,1,0:T(8,128)(2,1)S(1)}, u32[]{:S(2)}, u32[]{:S(2)}) %collective-permute-start.12) | collective-permute-done | bytes 245792 | tf_op jit(solution)/shard_map/ppermute | solution.py:255
  34.4 1.7 %collective-permute-start.16 = (bf16[4,120,256]{2,1,0:T(8,128)(2,1)S(1)}, bf16[4,120,256]{2,1,0:T(8,128)(2,1)S(1)}, u32[]{:S(2)}, u32[]{:S(2)}) collective-permute-start(bf16[4,120,256]{2,1,0:T(8,128)(2,1)S(1)} %add_convert_fusion.4), channel_id=1, source_target_pairs={{0,4},{2,10},{8,0},{10,18},{16,8},{18,26},{24,16},{26,30},{28,24},... | collective-permute-start | bytes 737288 | tf_op jit(solution)/shard_map/ppermute | solution.py:255
  36.6 2.6 %collective-permute-done.10 = bf16[4,120,256]{2,1,0:T(8,128)(2,1)S(1)} collective-permute-done((bf16[4,120,256]{2,1,0:T(8,128)(2,1)S(1)}, bf16[4,120,256]{2,1,0:T(8,128)(2,1)S(1)}, u32[]{:S(2)}, u32[]{:S(2)}) %collective-permute-start.10) | collective-permute-done | bytes 245792 | tf_op jit(solution)/shard_map/ppermute | solution.py:255
  39.6 2.0 %collective-permute-start.17 = (bf16[4,120,256]{2,1,0:T(8,128)(2,1)S(1)}, bf16[4,120,256]{2,1,0:T(8,128)(2,1)S(1)}, u32[]{:S(2)}, u32[]{:S(2)}) collective-permute-start(bf16[4,120,256]{2,1,0:T(8,128)(2,1)S(1)} %add_convert_fusion.1), channel_id=1, source_target_pairs={{0,8},{2,6},{8,16},{10,2},{16,24},{18,10},{24,28},{26,18},{28,20},... | collective-permute-start | bytes 737288 | tf_op jit(solution)/shard_map/ppermute | solution.py:255
  41.9 6.6 %collective-permute-done.17 = bf16[4,120,256]{2,1,0:T(8,128)(2,1)S(1)} collective-permute-done((bf16[4,120,256]{2,1,0:T(8,128)(2,1)S(1)}, bf16[4,120,256]{2,1,0:T(8,128)(2,1)S(1)}, u32[]{:S(2)}, u32[]{:S(2)}) %collective-permute-start.17) | collective-permute-done | bytes 245792 | tf_op jit(solution)/shard_map/ppermute | solution.py:255
  48.7 2.5 %collective-permute-start.19 = (bf16[4,120,256]{2,1,0:T(8,128)(2,1)S(1)}, bf16[4,120,256]{2,1,0:T(8,128)(2,1)S(1)}, u32[]{:S(2)}, u32[]{:S(2)}) collective-permute-start(bf16[4,120,256]{2,1,0:T(8,128)(2,1)S(1)} %convolution_convert_fusion.first), channel_id=1, source_target_pairs={{0,8},{2,6},{8,16},{10,2},{16,24},{18,10},{24,28},{26,18},{28,20},... | collective-permute-start | bytes 737288 | tf_op jit(solution)/shard_map/ppermute | solution.py:278
  51.7 1.7 %collective-permute-start.18 = (bf16[4,120,256]{2,1,0:T(8,128)(2,1)S(1)}, bf16[4,120,256]{2,1,0:T(8,128)(2,1)S(1)}, u32[]{:S(2)}, u32[]{:S(2)}) collective-permute-start(bf16[4,120,256]{2,1,0:T(8,128)(2,1)S(1)} %convolution_convert_fusion.first), channel_id=1, source_target_pairs={{0,4},{2,10},{8,0},{10,18},{16,8},{18,26},{24,16},{26,30},{28,24},... | collective-permute-start | bytes 737288 | tf_op jit(solution)/shard_map/ppermute | solution.py:278
  53.9 1.1 %apply_cells.8.before = f32[2,120,128]{2,1,0:T(8,128)S(1)} custom-call(s32[2,9]{1,0:T(2,128)S(1)} %pad_add_fusion.bounds, s32[2,64]{1,0:T(2,128)S(1)} %pad_add_fusion.1.order, s32[2,64]{1,0:T(2,128)S(1)} %pad_add_fusion.2.cell, f32[2,120,128]{2,1,0:T(8,128)S(1)} %broadcast_in_dim.87.before, bf16[64,256,128]{2,1,0:T(8,128)(2,1)S(1)} %copy-done.1, ...), custom_call_target="tpu_custom_call" | custom-call | flops 125829120 | bytes 1540096 | tf_op jit(solution)/shard_map/apply_cells/pallas_call | solution.py:139
  55.0 2.6 %collective-permute-done.19.first = bf16[4,120,256]{2,1,0:T(8,128)(2,1)S(1)} collective-permute-done((bf16[4,120,256]{2,1,0:T(8,128)(2,1)S(1)}, bf16[4,120,256]{2,1,0:T(8,128)(2,1)S(1)}, u32[]{:S(2)}, u32[]{:S(2)}) %collective-permute-start.19) | collective-permute-done | bytes 245792 | tf_op jit(solution)/shard_map/ppermute | solution.py:278
  57.5 2.4 %collective-permute-done.20.second = bf16[4,120,256]{2,1,0:T(8,128)(2,1)S(1)} collective-permute-done((bf16[4,120,256]{2,1,0:T(8,128)(2,1)S(1)}, bf16[4,120,256]{2,1,0:T(8,128)(2,1)S(1)}, u32[]{:S(2)}, u32[]{:S(2)}) %collective-permute-start.20) | collective-permute-done | bytes 245792 | tf_op jit(solution)/shard_map/ppermute | solution.py:278
  60.0 1.1 %collective-permute-start.24 = (bf16[4,120,256]{2,1,0:T(8,128)(2,1)S(1)}, bf16[4,120,256]{2,1,0:T(8,128)(2,1)S(1)}, u32[]{:S(2)}, u32[]{:S(2)}) collective-permute-start(bf16[4,120,256]{2,1,0:T(8,128)(2,1)S(1)} %collective-permute-done.19.first), channel_id=1, source_target_pairs={{0,8},{2,6},{8,16},{10,2},{16,24},{18,10},{24,28},{26,18},{28,20},... | collective-permute-start | bytes 737288 | tf_op jit(solution)/shard_map/ppermute | solution.py:285
  61.1 0.9 collective-permute-start.25
  62.0 1.5 %apply_cells.9.before = f32[2,120,128]{2,1,0:T(8,128)S(1)} custom-call(s32[2,9]{1,0:T(2,128)S(1)} %pad_add_fusion.bounds, s32[2,64]{1,0:T(2,128)S(1)} %pad_add_fusion.1.order, s32[2,64]{1,0:T(2,128)S(1)} %pad_add_fusion.2.cell, f32[2,120,128]{2,1,0:T(8,128)S(1)} %apply_cells.8.before, bf16[64,256,128]{2,1,0:T(8,128)(2,1)S(1)} %copy-done.1, ...), custom_call_target="tpu_custom_call" | custom-call | flops 125829120 | bytes 1540096 | tf_op jit(solution)/shard_map/apply_cells/pallas_call | solution.py:139
  63.5 1.5 %collective-permute-done.18.second = bf16[4,120,256]{2,1,0:T(8,128)(2,1)S(1)} collective-permute-done((bf16[4,120,256]{2,1,0:T(8,128)(2,1)S(1)}, bf16[4,120,256]{2,1,0:T(8,128)(2,1)S(1)}, u32[]{:S(2)}, u32[]{:S(2)}) %collective-permute-start.18) | collective-permute-done | bytes 245792 | tf_op jit(solution)/shard_map/ppermute | solution.py:278
  65.0 1.4 %collective-permute-start.22 = (bf16[4,120,256]{2,1,0:T(8,128)(2,1)S(1)}, bf16[4,120,256]{2,1,0:T(8,128)(2,1)S(1)}, u32[]{:S(2)}, u32[]{:S(2)}) collective-permute-start(bf16[4,120,256]{2,1,0:T(8,128)(2,1)S(1)} %collective-permute-done.15.first), channel_id=1, source_target_pairs={{0,8},{2,6},{8,16},{10,2},{16,24},{18,10},{24,28},{26,18},{28,20},... | collective-permute-start | bytes 737288 | tf_op jit(solution)/shard_map/ppermute | solution.py:285
  67.0 1.3 %apply_cells.10.before = f32[2,120,128]{2,1,0:T(8,128)S(1)} custom-call(s32[2,9]{1,0:T(2,128)S(1)} %pad_add_fusion.bounds, s32[2,64]{1,0:T(2,128)S(1)} %pad_add_fusion.1.order, s32[2,64]{1,0:T(2,128)S(1)} %pad_add_fusion.2.cell, f32[2,120,128]{2,1,0:T(8,128)S(1)} %apply_cells.9.before, bf16[64,256,128]{2,1,0:T(8,128)(2,1)S(1)} %copy-done.1, ...), custom_call_target="tpu_custom_call" | custom-call | flops 125829120 | bytes 1540096 | tf_op jit(solution)/shard_map/apply_cells/pallas_call | solution.py:139
  68.8 1.5 %collective-permute-done.25.second = bf16[4,120,256]{2,1,0:T(8,128)(2,1)S(1)} collective-permute-done((bf16[4,120,256]{2,1,0:T(8,128)(2,1)S(1)}, bf16[4,120,256]{2,1,0:T(8,128)(2,1)S(1)}, u32[]{:S(2)}, u32[]{:S(2)}) %collective-permute-start.25) | collective-permute-done | bytes 245792 | tf_op jit(solution)/shard_map/ppermute | solution.py:285
  70.3 1.4 %collective-permute-start.28 = (bf16[4,120,256]{2,1,0:T(8,128)(2,1)S(1)}, bf16[4,120,256]{2,1,0:T(8,128)(2,1)S(1)}, u32[]{:S(2)}, u32[]{:S(2)}) collective-permute-start(bf16[4,120,256]{2,1,0:T(8,128)(2,1)S(1)} %collective-permute-done.24.first), channel_id=1, source_target_pairs={{0,8},{2,6},{8,16},{10,2},{16,24},{18,10},{24,28},{26,18},{28,20},... | collective-permute-start | bytes 737288 | tf_op jit(solution)/shard_map/ppermute | solution.py:285
  72.3 1.1 %apply_cells.11.before = f32[2,120,128]{2,1,0:T(8,128)S(1)} custom-call(s32[2,9]{1,0:T(2,128)S(1)} %pad_add_fusion.bounds, s32[2,64]{1,0:T(2,128)S(1)} %pad_add_fusion.1.order, s32[2,64]{1,0:T(2,128)S(1)} %pad_add_fusion.2.cell, f32[2,120,128]{2,1,0:T(8,128)S(1)} %apply_cells.10.before, bf16[64,256,128]{2,1,0:T(8,128)(2,1)S(1)} %copy-done.1, ...), custom_call_target="tpu_custom_call" | custom-call | flops 125829120 | bytes 1540096 | tf_op jit(solution)/shard_map/apply_cells/pallas_call | solution.py:139
  74.0 1.5 %collective-permute-done.23.second = bf16[4,120,256]{2,1,0:T(8,128)(2,1)S(1)} collective-permute-done((bf16[4,120,256]{2,1,0:T(8,128)(2,1)S(1)}, bf16[4,120,256]{2,1,0:T(8,128)(2,1)S(1)}, u32[]{:S(2)}, u32[]{:S(2)}) %collective-permute-start.23) | collective-permute-done | bytes 245792 | tf_op jit(solution)/shard_map/ppermute | solution.py:285
  75.4 1.5 %collective-permute-start.26 = (bf16[4,120,256]{2,1,0:T(8,128)(2,1)S(1)}, bf16[4,120,256]{2,1,0:T(8,128)(2,1)S(1)}, u32[]{:S(2)}, u32[]{:S(2)}) collective-permute-start(bf16[4,120,256]{2,1,0:T(8,128)(2,1)S(1)} %collective-permute-done.22.first), channel_id=1, source_target_pairs={{0,8},{2,6},{8,16},{10,2},{16,24},{18,10},{24,28},{26,18},{28,20},... | collective-permute-start | bytes 737288 | tf_op jit(solution)/shard_map/ppermute | solution.py:285
  77.5 1.3 %apply_cells.12.before = f32[2,120,128]{2,1,0:T(8,128)S(1)} custom-call(s32[2,9]{1,0:T(2,128)S(1)} %pad_add_fusion.bounds, s32[2,64]{1,0:T(2,128)S(1)} %pad_add_fusion.1.order, s32[2,64]{1,0:T(2,128)S(1)} %pad_add_fusion.2.cell, f32[2,120,128]{2,1,0:T(8,128)S(1)} %apply_cells.11.before, bf16[64,256,128]{2,1,0:T(8,128)(2,1)S(1)} %copy-done.1, ...), custom_call_target="tpu_custom_call" | custom-call | flops 125829120 | bytes 1540096 | tf_op jit(solution)/shard_map/apply_cells/pallas_call | solution.py:139
  79.2 1.4 %collective-permute-done.29.second = bf16[4,120,256]{2,1,0:T(8,128)(2,1)S(1)} collective-permute-done((bf16[4,120,256]{2,1,0:T(8,128)(2,1)S(1)}, bf16[4,120,256]{2,1,0:T(8,128)(2,1)S(1)}, u32[]{:S(2)}, u32[]{:S(2)}) %collective-permute-start.29) | collective-permute-done | bytes 245792 | tf_op jit(solution)/shard_map/ppermute | solution.py:285
  80.6 1.6 %collective-permute-start.30 = (bf16[4,120,256]{2,1,0:T(8,128)(2,1)S(1)}, bf16[4,120,256]{2,1,0:T(8,128)(2,1)S(1)}, u32[]{:S(2)}, u32[]{:S(2)}) collective-permute-start(bf16[4,120,256]{2,1,0:T(8,128)(2,1)S(1)} %collective-permute-done.28.first), channel_id=1, source_target_pairs={{0,8},{2,6},{8,16},{10,2},{16,24},{18,10},{24,28},{26,18},{28,20},... | collective-permute-start | bytes 737288 | tf_op jit(solution)/shard_map/ppermute | solution.py:285
  82.7 2.2 %copy-done.2 = bf16[64,256,128]{2,1,0:T(8,128)(2,1)S(1)} copy-done((bf16[64,256,128]{2,1,0:T(8,128)(2,1)S(1)}, bf16[64,256,128]{2,1,0:T(8,128)(2,1)}, u32[]{:S(2)}) %copy-start.2) | copy-done | bytes 4194328
  84.9 2.2 %copy-done.4 = bf16[64,256,128]{2,1,0:T(8,128)(2,1)S(1)} copy-done((bf16[64,256,128]{2,1,0:T(8,128)(2,1)S(1)}, bf16[64,256,128]{2,1,0:T(8,128)(2,1)}, u32[]{:S(2)}) %copy-start.4) | copy-done | bytes 4194328
  87.0 1.3 %apply_cells.13.before = f32[2,120,128]{2,1,0:T(8,128)S(1)} custom-call(s32[2,9]{1,0:T(2,128)S(1)} %pad_add_fusion.bounds, s32[2,64]{1,0:T(2,128)S(1)} %pad_add_fusion.1.order, s32[2,64]{1,0:T(2,128)S(1)} %pad_add_fusion.2.cell, f32[2,120,128]{2,1,0:T(8,128)S(1)} %apply_cells.12.before, bf16[64,256,128]{2,1,0:T(8,128)(2,1)S(1)} %copy-done.2, ...), custom_call_target="tpu_custom_call" | custom-call | flops 125829120 | bytes 1540096 | tf_op jit(solution)/shard_map/apply_cells/pallas_call | solution.py:139
  88.4 1.4 %apply_cells.14 = (f32[2,120,128]{2,1,0:T(8,128)S(1)}, bf16[8,256,128]{2,1,0:T(8,128)(2,1)S(1)}, bf16[8,256,128]{2,1,0:T(8,128)(2,1)S(1)}) custom-call(s32[2,9]{1,0:T(2,128)S(1)} %pad_add_fusion.bounds, s32[2,64]{1,0:T(2,128)S(1)} %pad_add_fusion.1.order, s32[2,64]{1,0:T(2,128)S(1)} %pad_add_fusion.2.cell, f32[2,120,128]{2,1,0:T(8,128)S(1)} %apply_cells.13.before, ...), custom_call_target="tpu_custom_call" | custom-call | flops 125829120 | bytes 1540096 | tf_op jit(solution)/shard_map/apply_cells/pallas_call | solution.py:139
  89.8 1.4 %apply_cells.15 = f32[2,128,120]{2,1,0:T(8,128)S(1)} custom-call(s32[2,9]{1,0:T(2,128)S(1)} %pad_add_fusion.bounds, s32[2,64]{1,0:T(2,128)S(1)} %pad_add_fusion.1.order, s32[2,64]{1,0:T(2,128)S(1)} %pad_add_fusion.2.cell, f32[2,120,128]{2,1,0:T(8,128)S(1)} %get-tuple-element.90.before, bf16[8,256,128]{2,1,0:T(8,128)(2,1)S(1)} %get-tuple-element.91.mine, ...), custom_call_target="tpu_custom_call" | custom-call | flops 125829120 | bytes 1540096 | tf_op jit(solution)/shard_map/apply_cells/pallas_call | solution.py:139
  91.2 1.6 %collective-permute-start.33 = (f32[64,120]{1,0:T(8,128)S(1)}, f32[64,120]{1,0:T(8,128)S(1)}, u32[]{:S(2)}, u32[]{:S(2)}) collective-permute-start(f32[64,120]{1,0:T(8,128)S(1)} %get-tuple-element.132), channel_id=1, source_target_pairs={{0,1},{1,0},{2,3},{3,2},{4,5},{5,4},{6,7},{7,6},{8,9},{9,8},{10,11... | collective-permute-start | bytes 92168 | tf_op jit(solution)/shard_map/ppermute | solution.py:169
  93.4 1.8 %collective-permute-done.33 = f32[64,120]{1,0:T(8,128)S(1)} collective-permute-done((f32[64,120]{1,0:T(8,128)S(1)}, f32[64,120]{1,0:T(8,128)S(1)}, u32[]{:S(2)}, u32[]{:S(2)}) %collective-permute-start.33) | collective-permute-done | bytes 30752 | tf_op jit(solution)/shard_map/ppermute | solution.py:169
  95.2 1.3 %collective-permute-done.34 = f32[64,120]{1,0:T(8,128)S(1)} collective-permute-done((f32[64,120]{1,0:T(8,128)S(1)}, f32[64,120]{1,0:T(8,128)S(1)}, u32[]{:S(2)}, u32[]{:S(2)}) %collective-permute-start.34) | collective-permute-done | bytes 30752 | tf_op jit(solution)/shard_map/ppermute | solution.py:170
  (77 shorter events, 11.3 us)
Async XLA Ops:
  0.0 48.5 %copy-start = (bf16[1,256,256]{2,1,0:T(8,128)(2,1)S(1)}, bf16[1,256,256]{2,1,0:T(8,128)(2,1)}, u32[]{:S(2)}) copy-start(bf16[1,256,256]{2,1,0:T(8,128)(2,1)} %param.9) | copy-start | bytes 393220
  5.1 2.0 %collective-permute-start = (bf16[8,120,256]{2,1,0:T(8,128)(2,1)S(1)}, bf16[8,120,256]{2,1,0:T(8,128)(2,1)S(1)}, u32[]{:S(2)}, u32[]{:S(2)}) collective-permute-start(bf16[8,120,256]{2,1,0:T(8,128)(2,1)S(1)} %get-tuple-element.50), channel_id=1, source_target_pairs={{0,2},{2,0},{4,6},{6,4},{8,10},{10,8},{12,14},{14,12},{16,18},{18,... | collective-permute-start | bytes 1474568 | tf_op jit(solution)/shard_map/ppermute | solution.py:229
  5.6 1.5 %collective-permute-start.1 = (s32[64]{0:T(128)S(1)}, s32[64]{0:T(128)S(1)}, u32[]{:S(2)}, u32[]{:S(2)}) collective-permute-start(s32[64]{0:T(128)S(1)} %get-tuple-element.61), channel_id=1, source_target_pairs={{0,2},{2,0},{4,6},{6,4},{8,10},{10,8},{12,14},{14,12},{16,18},{18,... | collective-permute-start | bytes 776 | tf_op jit(solution)/shard_map/ppermute | solution.py:231
  7.1 6.1 %collective-permute-start.2 = (bf16[56,120,256]{2,1,0:T(8,128)(2,1)S(1)}, bf16[56,120,256]{2,1,0:T(8,128)(2,1)S(1)}, u32[]{:S(2)}, u32[]{:S(2)}) collective-permute-start(bf16[56,120,256]{2,1,0:T(8,128)(2,1)S(1)} %get-tuple-element.52), channel_id=1, source_target_pairs={{0,2},{2,0},{4,6},{6,4},{8,10},{10,8},{12,14},{14,12},{16,18},{18,... | collective-permute-start | bytes 10321928 | tf_op jit(solution)/shard_map/ppermute | solution.py:229
  7.8 8.6 %copy-start.1 = (bf16[64,256,128]{2,1,0:T(8,128)(2,1)S(1)}, bf16[64,256,128]{2,1,0:T(8,128)(2,1)}, u32[]{:S(2)}) copy-start(bf16[64,256,128]{2,1,0:T(8,128)(2,1)} %mine.13) | copy-start | bytes 12582916
  7.9 10.2 %collective-permute-start.6 = (bf16[4,120,256]{2,1,0:T(8,128)(2,1)S(1)}, bf16[4,120,256]{2,1,0:T(8,128)(2,1)S(1)}, u32[]{:S(2)}, u32[]{:S(2)}) collective-permute-start(bf16[4,120,256]{2,1,0:T(8,128)(2,1)S(1)} %add_convert_fusion.12), channel_id=1, source_target_pairs={{0,4},{2,10},{8,0},{10,18},{16,8},{18,26},{24,16},{26,30},{28,24},... | collective-permute-start | bytes 737288 | tf_op jit(solution)/shard_map/ppermute | solution.py:255
  10.6 7.5 %collective-permute-start.5 = (bf16[4,120,256]{2,1,0:T(8,128)(2,1)S(1)}, bf16[4,120,256]{2,1,0:T(8,128)(2,1)S(1)}, u32[]{:S(2)}, u32[]{:S(2)}) collective-permute-start(bf16[4,120,256]{2,1,0:T(8,128)(2,1)S(1)} %add_convert_fusion.13), channel_id=1, source_target_pairs={{0,8},{2,6},{8,16},{10,2},{16,24},{18,10},{24,28},{26,18},{28,20},... | collective-permute-start | bytes 737288 | tf_op jit(solution)/shard_map/ppermute | solution.py:255
  13.5 8.1 %collective-permute-start.4 = (bf16[4,120,256]{2,1,0:T(8,128)(2,1)S(1)}, bf16[4,120,256]{2,1,0:T(8,128)(2,1)S(1)}, u32[]{:S(2)}, u32[]{:S(2)}) collective-permute-start(bf16[4,120,256]{2,1,0:T(8,128)(2,1)S(1)} %add_convert_fusion.14), channel_id=1, source_target_pairs={{0,4},{2,10},{8,0},{10,18},{16,8},{18,26},{24,16},{26,30},{28,24},... | collective-permute-start | bytes 737288 | tf_op jit(solution)/shard_map/ppermute | solution.py:255
  16.4 37.4 %collective-permute-start.21 = (bf16[64,256,128]{2,1,0:T(8,128)(2,1)S(1)}, bf16[64,256,128]{2,1,0:T(8,128)(2,1)S(1)}, u32[]{:S(2)}, u32[]{:S(2)}) collective-permute-start(bf16[64,256,128]{2,1,0:T(8,128)(2,1)S(1)} %copy-done.1), channel_id=1, source_target_pairs={{0,2},{2,0},{4,6},{6,4},{8,10},{10,8},{12,14},{14,12},{16,18},{18,... | collective-permute-start | bytes 12582920 | tf_op jit(solution)/shard_map/ppermute | solution.py:235
  16.5 8.0 %collective-permute-start.3 = (bf16[4,120,256]{2,1,0:T(8,128)(2,1)S(1)}, bf16[4,120,256]{2,1,0:T(8,128)(2,1)S(1)}, u32[]{:S(2)}, u32[]{:S(2)}) collective-permute-start(bf16[4,120,256]{2,1,0:T(8,128)(2,1)S(1)} %add_convert_fusion.15), channel_id=1, source_target_pairs={{0,8},{2,6},{8,16},{10,2},{16,24},{18,10},{24,28},{26,18},{28,20},... | collective-permute-start | bytes 737288 | tf_op jit(solution)/shard_map/ppermute | solution.py:255
  18.2 9.1 %collective-permute-start.8 = (bf16[4,120,256]{2,1,0:T(8,128)(2,1)S(1)}, bf16[4,120,256]{2,1,0:T(8,128)(2,1)S(1)}, u32[]{:S(2)}, u32[]{:S(2)}) collective-permute-start(bf16[4,120,256]{2,1,0:T(8,128)(2,1)S(1)} %add_convert_fusion.10), channel_id=1, source_target_pairs={{0,4},{2,10},{8,0},{10,18},{16,8},{18,26},{24,16},{26,30},{28,24},... | collective-permute-start | bytes 737288 | tf_op jit(solution)/shard_map/ppermute | solution.py:255
  19.2 9.1 %collective-permute-start.7 = (bf16[4,120,256]{2,1,0:T(8,128)(2,1)S(1)}, bf16[4,120,256]{2,1,0:T(8,128)(2,1)S(1)}, u32[]{:S(2)}, u32[]{:S(2)}) collective-permute-start(bf16[4,120,256]{2,1,0:T(8,128)(2,1)S(1)} %add_convert_fusion.11), channel_id=1, source_target_pairs={{0,8},{2,6},{8,16},{10,2},{16,24},{18,10},{24,28},{26,18},{28,20},... | collective-permute-start | bytes 737288 | tf_op jit(solution)/shard_map/ppermute | solution.py:255
  24.6 9.3 %collective-permute-start.12 = (bf16[4,120,256]{2,1,0:T(8,128)(2,1)S(1)}, bf16[4,120,256]{2,1,0:T(8,128)(2,1)S(1)}, u32[]{:S(2)}, u32[]{:S(2)}) collective-permute-start(bf16[4,120,256]{2,1,0:T(8,128)(2,1)S(1)} %add_convert_fusion.8), channel_id=1, source_target_pairs={{0,4},{2,10},{8,0},{10,18},{16,8},{18,26},{24,16},{26,30},{28,24},... | collective-permute-start | bytes 737288 | tf_op jit(solution)/shard_map/ppermute | solution.py:255
  26.4 7.8 %collective-permute-start.11 = (bf16[4,120,256]{2,1,0:T(8,128)(2,1)S(1)}, bf16[4,120,256]{2,1,0:T(8,128)(2,1)S(1)}, u32[]{:S(2)}, u32[]{:S(2)}) collective-permute-start(bf16[4,120,256]{2,1,0:T(8,128)(2,1)S(1)} %add_convert_fusion.9), channel_id=1, source_target_pairs={{0,8},{2,6},{8,16},{10,2},{16,24},{18,10},{24,28},{26,18},{28,20},... | collective-permute-start | bytes 737288 | tf_op jit(solution)/shard_map/ppermute | solution.py:255
  28.4 10.8 %collective-permute-start.10 = (bf16[4,120,256]{2,1,0:T(8,128)(2,1)S(1)}, bf16[4,120,256]{2,1,0:T(8,128)(2,1)S(1)}, u32[]{:S(2)}, u32[]{:S(2)}) collective-permute-start(bf16[4,120,256]{2,1,0:T(8,128)(2,1)S(1)} %add_convert_fusion.6), channel_id=1, source_target_pairs={{0,4},{2,10},{8,0},{10,18},{16,8},{18,26},{24,16},{26,30},{28,24},... | collective-permute-start | bytes 737288 | tf_op jit(solution)/shard_map/ppermute | solution.py:255
  30.2 9.3 %collective-permute-start.9 = (bf16[4,120,256]{2,1,0:T(8,128)(2,1)S(1)}, bf16[4,120,256]{2,1,0:T(8,128)(2,1)S(1)}, u32[]{:S(2)}, u32[]{:S(2)}) collective-permute-start(bf16[4,120,256]{2,1,0:T(8,128)(2,1)S(1)} %add_convert_fusion.7), channel_id=1, source_target_pairs={{0,8},{2,6},{8,16},{10,2},{16,24},{18,10},{24,28},{26,18},{28,20},... | collective-permute-start | bytes 737288 | tf_op jit(solution)/shard_map/ppermute | solution.py:255
  34.4 14.1 %collective-permute-start.16 = (bf16[4,120,256]{2,1,0:T(8,128)(2,1)S(1)}, bf16[4,120,256]{2,1,0:T(8,128)(2,1)S(1)}, u32[]{:S(2)}, u32[]{:S(2)}) collective-permute-start(bf16[4,120,256]{2,1,0:T(8,128)(2,1)S(1)} %add_convert_fusion.4), channel_id=1, source_target_pairs={{0,4},{2,10},{8,0},{10,18},{16,8},{18,26},{24,16},{26,30},{28,24},... | collective-permute-start | bytes 737288 | tf_op jit(solution)/shard_map/ppermute | solution.py:255
  36.1 15.1 %collective-permute-start.14 = (bf16[4,120,256]{2,1,0:T(8,128)(2,1)S(1)}, bf16[4,120,256]{2,1,0:T(8,128)(2,1)S(1)}, u32[]{:S(2)}, u32[]{:S(2)}) collective-permute-start(bf16[4,120,256]{2,1,0:T(8,128)(2,1)S(1)} %add_convert_fusion.5), channel_id=1, source_target_pairs={{0,8},{2,6},{8,16},{10,2},{16,24},{18,10},{24,28},{26,18},{28,20},... | collective-permute-start | bytes 737288 | tf_op jit(solution)/shard_map/ppermute | solution.py:255
  39.6 8.8 %collective-permute-start.17 = (bf16[4,120,256]{2,1,0:T(8,128)(2,1)S(1)}, bf16[4,120,256]{2,1,0:T(8,128)(2,1)S(1)}, u32[]{:S(2)}, u32[]{:S(2)}) collective-permute-start(bf16[4,120,256]{2,1,0:T(8,128)(2,1)S(1)} %add_convert_fusion.1), channel_id=1, source_target_pairs={{0,8},{2,6},{8,16},{10,2},{16,24},{18,10},{24,28},{26,18},{28,20},... | collective-permute-start | bytes 737288 | tf_op jit(solution)/shard_map/ppermute | solution.py:255
  41.7 9.5 %collective-permute-start.13 = (bf16[4,120,256]{2,1,0:T(8,128)(2,1)S(1)}, bf16[4,120,256]{2,1,0:T(8,128)(2,1)S(1)}, u32[]{:S(2)}, u32[]{:S(2)}) collective-permute-start(bf16[4,120,256]{2,1,0:T(8,128)(2,1)S(1)} %add_convert_fusion.3), channel_id=1, source_target_pairs={{0,4},{2,10},{8,0},{10,18},{16,8},{18,26},{24,16},{26,30},{28,24},... | collective-permute-start | bytes 737288 | tf_op jit(solution)/shard_map/ppermute | solution.py:255
  48.7 8.8 %collective-permute-start.19 = (bf16[4,120,256]{2,1,0:T(8,128)(2,1)S(1)}, bf16[4,120,256]{2,1,0:T(8,128)(2,1)S(1)}, u32[]{:S(2)}, u32[]{:S(2)}) collective-permute-start(bf16[4,120,256]{2,1,0:T(8,128)(2,1)S(1)} %convolution_convert_fusion.first), channel_id=1, source_target_pairs={{0,8},{2,6},{8,16},{10,2},{16,24},{18,10},{24,28},{26,18},{28,20},... | collective-permute-start | bytes 737288 | tf_op jit(solution)/shard_map/ppermute | solution.py:278
  51.5 8.5 %collective-permute-start.20 = (bf16[4,120,256]{2,1,0:T(8,128)(2,1)S(1)}, bf16[4,120,256]{2,1,0:T(8,128)(2,1)S(1)}, u32[]{:S(2)}, u32[]{:S(2)}) collective-permute-start(bf16[4,120,256]{2,1,0:T(8,128)(2,1)S(1)} %convolution_convert_fusion.1.second), channel_id=1, source_target_pairs={{0,4},{2,10},{8,0},{10,18},{16,8},{18,26},{24,16},{26,30},{28,24},... | collective-permute-start | bytes 737288 | tf_op jit(solution)/shard_map/ppermute | solution.py:278
  51.7 13.3 %collective-permute-start.18 = (bf16[4,120,256]{2,1,0:T(8,128)(2,1)S(1)}, bf16[4,120,256]{2,1,0:T(8,128)(2,1)S(1)}, u32[]{:S(2)}, u32[]{:S(2)}) collective-permute-start(bf16[4,120,256]{2,1,0:T(8,128)(2,1)S(1)} %convolution_convert_fusion.first), channel_id=1, source_target_pairs={{0,4},{2,10},{8,0},{10,18},{16,8},{18,26},{24,16},{26,30},{28,24},... | collective-permute-start | bytes 737288 | tf_op jit(solution)/shard_map/ppermute | solution.py:278
  53.4 11.6 %collective-permute-start.15 = (bf16[4,120,256]{2,1,0:T(8,128)(2,1)S(1)}, bf16[4,120,256]{2,1,0:T(8,128)(2,1)S(1)}, u32[]{:S(2)}, u32[]{:S(2)}) collective-permute-start(bf16[4,120,256]{2,1,0:T(8,128)(2,1)S(1)} %convolution_convert_fusion.1.second), channel_id=1, source_target_pairs={{0,8},{2,6},{8,16},{10,2},{16,24},{18,10},{24,28},{26,18},{28,20},... | collective-permute-start | bytes 737288 | tf_op jit(solution)/shard_map/ppermute | solution.py:278
  53.9 23.6 %copy-start.3 = (bf16[64,256,128]{2,1,0:T(8,128)(2,1)}, bf16[64,256,128]{2,1,0:T(8,128)(2,1)S(1)}, u32[]{:S(2)}) copy-start(bf16[64,256,128]{2,1,0:T(8,128)(2,1)S(1)} %collective-permute-done.21.other) | copy-start | bytes 12582916
  60.0 8.8 %collective-permute-start.24 = (bf16[4,120,256]{2,1,0:T(8,128)(2,1)S(1)}, bf16[4,120,256]{2,1,0:T(8,128)(2,1)S(1)}, u32[]{:S(2)}, u32[]{:S(2)}) collective-permute-start(bf16[4,120,256]{2,1,0:T(8,128)(2,1)S(1)} %collective-permute-done.19.first), channel_id=1, source_target_pairs={{0,8},{2,6},{8,16},{10,2},{16,24},{18,10},{24,28},{26,18},{28,20},... | collective-permute-start | bytes 737288 | tf_op jit(solution)/shard_map/ppermute | solution.py:285
  61.1 9.2 %collective-permute-start.25 = (bf16[4,120,256]{2,1,0:T(8,128)(2,1)S(1)}, bf16[4,120,256]{2,1,0:T(8,128)(2,1)S(1)}, u32[]{:S(2)}, u32[]{:S(2)}) collective-permute-start(bf16[4,120,256]{2,1,0:T(8,128)(2,1)S(1)} %collective-permute-done.20.second), channel_id=1, source_target_pairs={{0,4},{2,10},{8,0},{10,18},{16,8},{18,26},{24,16},{26,30},{28,24},... | collective-permute-start | bytes 737288 | tf_op jit(solution)/shard_map/ppermute | solution.py:285
  65.0 9.0 %collective-permute-start.22 = (bf16[4,120,256]{2,1,0:T(8,128)(2,1)S(1)}, bf16[4,120,256]{2,1,0:T(8,128)(2,1)S(1)}, u32[]{:S(2)}, u32[]{:S(2)}) collective-permute-start(bf16[4,120,256]{2,1,0:T(8,128)(2,1)S(1)} %collective-permute-done.15.first), channel_id=1, source_target_pairs={{0,8},{2,6},{8,16},{10,2},{16,24},{18,10},{24,28},{26,18},{28,20},... | collective-permute-start | bytes 737288 | tf_op jit(solution)/shard_map/ppermute | solution.py:285
  66.4 9.0 %collective-permute-start.23 = (bf16[4,120,256]{2,1,0:T(8,128)(2,1)S(1)}, bf16[4,120,256]{2,1,0:T(8,128)(2,1)S(1)}, u32[]{:S(2)}, u32[]{:S(2)}) collective-permute-start(bf16[4,120,256]{2,1,0:T(8,128)(2,1)S(1)} %collective-permute-done.18.second), channel_id=1, source_target_pairs={{0,4},{2,10},{8,0},{10,18},{16,8},{18,26},{24,16},{26,30},{28,24},... | collective-permute-start | bytes 737288 | tf_op jit(solution)/shard_map/ppermute | solution.py:285
  70.3 9.0 %collective-permute-start.28 = (bf16[4,120,256]{2,1,0:T(8,128)(2,1)S(1)}, bf16[4,120,256]{2,1,0:T(8,128)(2,1)S(1)}, u32[]{:S(2)}, u32[]{:S(2)}) collective-permute-start(bf16[4,120,256]{2,1,0:T(8,128)(2,1)S(1)} %collective-permute-done.24.first), channel_id=1, source_target_pairs={{0,8},{2,6},{8,16},{10,2},{16,24},{18,10},{24,28},{26,18},{28,20},... | collective-permute-start | bytes 737288 | tf_op jit(solution)/shard_map/ppermute | solution.py:285
  71.7 9.0 %collective-permute-start.29 = (bf16[4,120,256]{2,1,0:T(8,128)(2,1)S(1)}, bf16[4,120,256]{2,1,0:T(8,128)(2,1)S(1)}, u32[]{:S(2)}, u32[]{:S(2)}) collective-permute-start(bf16[4,120,256]{2,1,0:T(8,128)(2,1)S(1)} %collective-permute-done.25.second), channel_id=1, source_target_pairs={{0,4},{2,10},{8,0},{10,18},{16,8},{18,26},{24,16},{26,30},{28,24},... | collective-permute-start | bytes 737288 | tf_op jit(solution)/shard_map/ppermute | solution.py:285
  75.4 12.9 %collective-permute-start.26 = (bf16[4,120,256]{2,1,0:T(8,128)(2,1)S(1)}, bf16[4,120,256]{2,1,0:T(8,128)(2,1)S(1)}, u32[]{:S(2)}, u32[]{:S(2)}) collective-permute-start(bf16[4,120,256]{2,1,0:T(8,128)(2,1)S(1)} %collective-permute-done.22.first), channel_id=1, source_target_pairs={{0,8},{2,6},{8,16},{10,2},{16,24},{18,10},{24,28},{26,18},{28,20},... | collective-permute-start | bytes 737288 | tf_op jit(solution)/shard_map/ppermute | solution.py:285
  76.9 11.4 %collective-permute-start.27 = (bf16[4,120,256]{2,1,0:T(8,128)(2,1)S(1)}, bf16[4,120,256]{2,1,0:T(8,128)(2,1)S(1)}, u32[]{:S(2)}, u32[]{:S(2)}) collective-permute-start(bf16[4,120,256]{2,1,0:T(8,128)(2,1)S(1)} %collective-permute-done.23.second), channel_id=1, source_target_pairs={{0,4},{2,10},{8,0},{10,18},{16,8},{18,26},{24,16},{26,30},{28,24},... | collective-permute-start | bytes 737288 | tf_op jit(solution)/shard_map/ppermute | solution.py:285
  80.6 9.1 %collective-permute-start.30 = (bf16[4,120,256]{2,1,0:T(8,128)(2,1)S(1)}, bf16[4,120,256]{2,1,0:T(8,128)(2,1)S(1)}, u32[]{:S(2)}, u32[]{:S(2)}) collective-permute-start(bf16[4,120,256]{2,1,0:T(8,128)(2,1)S(1)} %collective-permute-done.28.first), channel_id=1, source_target_pairs={{0,8},{2,6},{8,16},{10,2},{16,24},{18,10},{24,28},{26,18},{28,20},... | collective-permute-start | bytes 737288 | tf_op jit(solution)/shard_map/ppermute | solution.py:285
  82.2 7.6 %collective-permute-start.31 = (bf16[4,120,256]{2,1,0:T(8,128)(2,1)S(1)}, bf16[4,120,256]{2,1,0:T(8,128)(2,1)S(1)}, u32[]{:S(2)}, u32[]{:S(2)}) collective-permute-start(bf16[4,120,256]{2,1,0:T(8,128)(2,1)S(1)} %collective-permute-done.29.second), channel_id=1, source_target_pairs={{0,4},{2,10},{8,0},{10,18},{16,8},{18,26},{24,16},{26,30},{28,24},... | collective-permute-start | bytes 737288 | tf_op jit(solution)/shard_map/ppermute | solution.py:285
  82.7 2.2 %copy-start.2 = (bf16[64,256,128]{2,1,0:T(8,128)(2,1)S(1)}, bf16[64,256,128]{2,1,0:T(8,128)(2,1)}, u32[]{:S(2)}) copy-start(bf16[64,256,128]{2,1,0:T(8,128)(2,1)} %mine.13) | copy-start | bytes 12582916
  84.9 2.2 %copy-start.4 = (bf16[64,256,128]{2,1,0:T(8,128)(2,1)S(1)}, bf16[64,256,128]{2,1,0:T(8,128)(2,1)}, u32[]{:S(2)}) copy-start(bf16[64,256,128]{2,1,0:T(8,128)(2,1)} %copy-done.3) | copy-start | bytes 12582916
  91.2 4.0 %collective-permute-start.33 = (f32[64,120]{1,0:T(8,128)S(1)}, f32[64,120]{1,0:T(8,128)S(1)}, u32[]{:S(2)}, u32[]{:S(2)}) collective-permute-start(f32[64,120]{1,0:T(8,128)S(1)} %get-tuple-element.132), channel_id=1, source_target_pairs={{0,1},{1,0},{2,3},{3,2},{4,5},{5,4},{6,7},{7,6},{8,9},{9,8},{10,11... | collective-permute-start | bytes 92168 | tf_op jit(solution)/shard_map/ppermute | solution.py:169
  92.8 3.7 %collective-permute-start.34 = (f32[64,120]{1,0:T(8,128)S(1)}, f32[64,120]{1,0:T(8,128)S(1)}, u32[]{:S(2)}, u32[]{:S(2)}) collective-permute-start(f32[64,120]{1,0:T(8,128)S(1)} %get-tuple-element.131), channel_id=1, source_target_pairs={{0,3},{1,2},{2,1},{3,0},{4,7},{5,6},{6,5},{7,4},{8,11},{9,10},{10,... | collective-permute-start | bytes 92168 | tf_op jit(solution)/shard_map/ppermute | solution.py:170
  92.8 3.7 %collective-permute-start.32 = (f32[64,120]{1,0:T(8,128)S(1)}, f32[64,120]{1,0:T(8,128)S(1)}, u32[]{:S(2)}, u32[]{:S(2)}) collective-permute-start(f32[64,120]{1,0:T(8,128)S(1)} %slice_bitcast_fusion.2), channel_id=1, source_target_pairs={{0,2},{2,0},{4,6},{6,4},{8,10},{10,8},{12,14},{14,12},{16,18},{18,... | collective-permute-start | bytes 92168 | tf_op jit(solution)/shard_map/ppermute | solution.py:171

commit v6 on v5

--- a/solution.py
+++ b/solution.py
@@ -161,16 +161,11 @@
     if lax.axis_size("ctr") != 2:
         return sum_over_ctr((total[0] + lax.ppermute(total[1], "wide", cores)).T)
     width = total.shape[1] // 2
-    low, high = total[:, :width], total[:, width:]
+    whole_sum = total[0] + lax.ppermute(total[1], "wide", cores)
+    low, high = whole_sum[:width], whole_sum[width:]
     lower = lax.axis_index("ctr") == 0
     mine, other = jnp.where(lower, low, high), jnp.where(lower, high, low)
-    diagonal = [(2 * a + y, 2 * b + 1 - y) for a, b in cores for y in range(2)]
-    parts = (
-        lax.ppermute(other[0], "ctr", [(0, 1), (1, 0)]),
-        lax.ppermute(other[1], ("wide", "ctr"), diagonal),
-        lax.ppermute(mine[1], "wide", cores),
-    )
-    return ((mine[0] + parts[2]) + (parts[0] + parts[1])).T
+    return (mine + lax.ppermute(other, "ctr", [(0, 1), (1, 0)])).T
 
 
 def cells_body(tens, coef, aux_of, slot_of, metric):

time: 97.3 us -> 97.3 us (level)
  waiting for transfers between devices: 36.4 us -> 41.9 us
  local copies, waits for them, and re-layouts: 4.9 us -> 0.52 us
    ppermute x24, waiting for transfers between devices: 23 us -> 28.1 us  [cells_body(): up[pair[0]], down[pair[1]] = (forward(ahead), backward(back))]
    unnamed x10 -> x4, local copies, waits for them, and re-layouts: 4.39 us -> 0.01 us
    ppermute x3 -> x2, waiting for transfers between devices: 3.09 us -> 3.49 us  [the longest x1 2.34 us: sum_over_cores_and_ctr(): return (mine + lax.ppermute(other, 'ctr', [(0, 1), (1, 0)])).T]
    ppermute x3 -> x2, starting transfers between devices: 2.21 us -> 1.81 us  [the longest x1 1.64 us: sum_over_cores_and_ctr(): return (mine + lax.ppermute(other, 'ctr', [(0, 1), (1, 0)])).T]
  transfers between devices with their start and end apart: 35 -> 34, of which waited for: 21 -> 24; matrix products, arithmetic and copies ran while one was open for 3% -> 3% of each run, Pallas kernels for 9% -> 9%
where the time goes in v6:
time: 97.3 us; the launch traced here: 97.1 us
  waiting for transfers between devices  41.9 us (43%)
  starting transfers between devices  36.4 us (37%)
  Pallas kernels  13.8 us (14%)
  other arithmetic  3.64 us (4%)
    ppermute x24, starting transfers between devices, cells_body(): up[pair[0]], down[pair[1]] = (forward(ahead), backward(back))  29 us
    ppermute x24, waiting for transfers between devices, cells_body(): up[pair[0]], down[pair[1]] = (forward(ahead), backward(back))  28.1 us
    pallas_call x8, Pallas kernels, apply_cells(): pl.pallas_call(functools.partial(apply_cells_kernel, group, takes, turned...  9.66 us
    pallas_call x1, Pallas kernels, sum_cells(): pl.pallas_call(functools.partial(sum_cells_kernel, sends), out_shape=tupl...  4.18 us
    ppermute x2, waiting for transfers between devices, cells_body(): backward(own[h])  3.9 us
    ppermute x2, starting transfers between devices, cells_body(): forward(own[h])  2.87 us
    ppermute x2, waiting for transfers between devices, cells_body(): forward(own[h])  2.56 us
    ppermute x2, waiting for transfers between devices, cells_body(): got = across(others[p])  2.45 us
  transfers between devices with their start and end apart: 34, of which 24 were waited for; matrix products, arithmetic and copies ran while one was open for 3% of the time, Pallas kernels for 9%

profile of v6, /device:TPU:0, one launch (start us, length us, event | category | flops | bytes accessed | tf_op | source)
XLA Modules:
  0.0 97.1 jit_solution(3347312773513332478)
XLA Ops:
  0.0 0.7 fusion.20
  0.9 4.2 %sum_cells.1 = (bf16[128,120,256]{2,1,0:T(8,128)(2,1)S(1)}, bf16[8,120,256]{2,1,0:T(8,128)(2,1)S(1)}, bf16[56,120,256]{2,1,0:T(8,128)(2,1)S(1)}, bf16[4,120,256]...) custom-call(s32[64]{0:T(128)S(1)} %get-tuple-element.130.cell, s32[64]{0:T(128)S(1)} %select_reduce_fusion.4.again, ...), custom_call_target="tpu_custom_call" | custom-call | flops 503316480 | bytes 12058624 | tf_op jit(solution)/shard_map/sum_cells/pallas_call | solution.py:80
  5.7 1.4 %collective-permute-done.1 = s32[64]{0:T(128)S(1)} collective-permute-done((s32[64]{0:T(128)S(1)}, s32[64]{0:T(128)S(1)}, u32[]{:S(2)}, u32[]{:S(2)}) %collective-permute-start.1) | collective-permute-done | bytes 288 | tf_op jit(solution)/shard_map/ppermute | solution.py:226
  7.9 2.7 %collective-permute-start.6 = (bf16[4,120,256]{2,1,0:T(8,128)(2,1)S(1)}, bf16[4,120,256]{2,1,0:T(8,128)(2,1)S(1)}, u32[]{:S(2)}, u32[]{:S(2)}) collective-permute-start(bf16[4,120,256]{2,1,0:T(8,128)(2,1)S(1)} %add_convert_fusion.12), channel_id=1, source_target_pairs={{0,4},{2,10},{8,0},{10,18},{16,8},{18,26},{24,16},{26,30},{28,24},... | collective-permute-start | bytes 737288 | tf_op jit(solution)/shard_map/ppermute | solution.py:250
  10.8 2.4 %collective-permute-done.2 = bf16[56,120,256]{2,1,0:T(8,128)(2,1)S(1)} collective-permute-done((bf16[56,120,256]{2,1,0:T(8,128)(2,1)S(1)}, bf16[56,120,256]{2,1,0:T(8,128)(2,1)S(1)}, u32[]{:S(2)}, u32[]{:S(2)}) %collective-permute-start.2) | collective-permute-done | bytes 3440672 | tf_op jit(solution)/shard_map/ppermute | solution.py:224
  13.5 2.9 %collective-permute-start.4 = (bf16[4,120,256]{2,1,0:T(8,128)(2,1)S(1)}, bf16[4,120,256]{2,1,0:T(8,128)(2,1)S(1)}, u32[]{:S(2)}, u32[]{:S(2)}) collective-permute-start(bf16[4,120,256]{2,1,0:T(8,128)(2,1)S(1)} %add_convert_fusion.14), channel_id=1, source_target_pairs={{0,4},{2,10},{8,0},{10,18},{16,8},{18,26},{24,16},{26,30},{28,24},... | collective-permute-start | bytes 737288 | tf_op jit(solution)/shard_map/ppermute | solution.py:250
  16.5 1.6 %collective-permute-start.3 = (bf16[4,120,256]{2,1,0:T(8,128)(2,1)S(1)}, bf16[4,120,256]{2,1,0:T(8,128)(2,1)S(1)}, u32[]{:S(2)}, u32[]{:S(2)}) collective-permute-start(bf16[4,120,256]{2,1,0:T(8,128)(2,1)S(1)} %add_convert_fusion.15), channel_id=1, source_target_pairs={{0,8},{2,6},{8,16},{10,2},{16,24},{18,10},{24,28},{26,18},{28,20},... | collective-permute-start | bytes 737288 | tf_op jit(solution)/shard_map/ppermute | solution.py:250
  18.2 1.0 %collective-permute-start.8 = (bf16[4,120,256]{2,1,0:T(8,128)(2,1)S(1)}, bf16[4,120,256]{2,1,0:T(8,128)(2,1)S(1)}, u32[]{:S(2)}, u32[]{:S(2)}) collective-permute-start(bf16[4,120,256]{2,1,0:T(8,128)(2,1)S(1)} %add_convert_fusion.10), channel_id=1, source_target_pairs={{0,4},{2,10},{8,0},{10,18},{16,8},{18,26},{24,16},{26,30},{28,24},... | collective-permute-start | bytes 737288 | tf_op jit(solution)/shard_map/ppermute | solution.py:250
  19.3 1.2 %collective-permute-start.7 = (bf16[4,120,256]{2,1,0:T(8,128)(2,1)S(1)}, bf16[4,120,256]{2,1,0:T(8,128)(2,1)S(1)}, u32[]{:S(2)}, u32[]{:S(2)}) collective-permute-start(bf16[4,120,256]{2,1,0:T(8,128)(2,1)S(1)} %add_convert_fusion.11), channel_id=1, source_target_pairs={{0,8},{2,6},{8,16},{10,2},{16,24},{18,10},{24,28},{26,18},{28,20},... | collective-permute-start | bytes 737288 | tf_op jit(solution)/shard_map/ppermute | solution.py:250
  20.4 1.2 %collective-permute-done.4 = bf16[4,120,256]{2,1,0:T(8,128)(2,1)S(1)} collective-permute-done((bf16[4,120,256]{2,1,0:T(8,128)(2,1)S(1)}, bf16[4,120,256]{2,1,0:T(8,128)(2,1)S(1)}, u32[]{:S(2)}, u32[]{:S(2)}) %collective-permute-start.4) | collective-permute-done | bytes 245792 | tf_op jit(solution)/shard_map/ppermute | solution.py:250
  21.7 2.8 %collective-permute-done.3 = bf16[4,120,256]{2,1,0:T(8,128)(2,1)S(1)} collective-permute-done((bf16[4,120,256]{2,1,0:T(8,128)(2,1)S(1)}, bf16[4,120,256]{2,1,0:T(8,128)(2,1)S(1)}, u32[]{:S(2)}, u32[]{:S(2)}) %collective-permute-start.3) | collective-permute-done | bytes 245792 | tf_op jit(solution)/shard_map/ppermute | solution.py:250
  24.6 1.7 %collective-permute-start.12 = (bf16[4,120,256]{2,1,0:T(8,128)(2,1)S(1)}, bf16[4,120,256]{2,1,0:T(8,128)(2,1)S(1)}, u32[]{:S(2)}, u32[]{:S(2)}) collective-permute-start(bf16[4,120,256]{2,1,0:T(8,128)(2,1)S(1)} %add_convert_fusion.8), channel_id=1, source_target_pairs={{0,4},{2,10},{8,0},{10,18},{16,8},{18,26},{24,16},{26,30},{28,24},... | collective-permute-start | bytes 737288 | tf_op jit(solution)/shard_map/ppermute | solution.py:250
  26.4 0.9 collective-permute-start.11
  27.3 1.0 %collective-permute-done.7 = bf16[4,120,256]{2,1,0:T(8,128)(2,1)S(1)} collective-permute-done((bf16[4,120,256]{2,1,0:T(8,128)(2,1)S(1)}, bf16[4,120,256]{2,1,0:T(8,128)(2,1)S(1)}, u32[]{:S(2)}, u32[]{:S(2)}) %collective-permute-start.7) | collective-permute-done | bytes 245792 | tf_op jit(solution)/shard_map/ppermute | solution.py:250
  28.4 1.7 %collective-permute-start.10 = (bf16[4,120,256]{2,1,0:T(8,128)(2,1)S(1)}, bf16[4,120,256]{2,1,0:T(8,128)(2,1)S(1)}, u32[]{:S(2)}, u32[]{:S(2)}) collective-permute-start(bf16[4,120,256]{2,1,0:T(8,128)(2,1)S(1)} %add_convert_fusion.6), channel_id=1, source_target_pairs={{0,4},{2,10},{8,0},{10,18},{16,8},{18,26},{24,16},{26,30},{28,24},... | collective-permute-start | bytes 737288 | tf_op jit(solution)/shard_map/ppermute | solution.py:250
  30.2 0.9 collective-permute-start.9
  31.7 2.2 %collective-permute-done.12 = bf16[4,120,256]{2,1,0:T(8,128)(2,1)S(1)} collective-permute-done((bf16[4,120,256]{2,1,0:T(8,128)(2,1)S(1)}, bf16[4,120,256]{2,1,0:T(8,128)(2,1)S(1)}, u32[]{:S(2)}, u32[]{:S(2)}) %collective-permute-start.12) | collective-permute-done | bytes 245792 | tf_op jit(solution)/shard_map/ppermute | solution.py:250
  34.4 1.7 %collective-permute-start.16 = (bf16[4,120,256]{2,1,0:T(8,128)(2,1)S(1)}, bf16[4,120,256]{2,1,0:T(8,128)(2,1)S(1)}, u32[]{:S(2)}, u32[]{:S(2)}) collective-permute-start(bf16[4,120,256]{2,1,0:T(8,128)(2,1)S(1)} %add_convert_fusion.4), channel_id=1, source_target_pairs={{0,4},{2,10},{8,0},{10,18},{16,8},{18,26},{24,16},{26,30},{28,24},... | collective-permute-start | bytes 737288 | tf_op jit(solution)/shard_map/ppermute | solution.py:250
  36.6 2.6 %collective-permute-done.10 = bf16[4,120,256]{2,1,0:T(8,128)(2,1)S(1)} collective-permute-done((bf16[4,120,256]{2,1,0:T(8,128)(2,1)S(1)}, bf16[4,120,256]{2,1,0:T(8,128)(2,1)S(1)}, u32[]{:S(2)}, u32[]{:S(2)}) %collective-permute-start.10) | collective-permute-done | bytes 245792 | tf_op jit(solution)/shard_map/ppermute | solution.py:250
  39.6 2.0 %collective-permute-start.17 = (bf16[4,120,256]{2,1,0:T(8,128)(2,1)S(1)}, bf16[4,120,256]{2,1,0:T(8,128)(2,1)S(1)}, u32[]{:S(2)}, u32[]{:S(2)}) collective-permute-start(bf16[4,120,256]{2,1,0:T(8,128)(2,1)S(1)} %add_convert_fusion.1), channel_id=1, source_target_pairs={{0,8},{2,6},{8,16},{10,2},{16,24},{18,10},{24,28},{26,18},{28,20},... | collective-permute-start | bytes 737288 | tf_op jit(solution)/shard_map/ppermute | solution.py:250
  41.9 6.6 %collective-permute-done.17 = bf16[4,120,256]{2,1,0:T(8,128)(2,1)S(1)} collective-permute-done((bf16[4,120,256]{2,1,0:T(8,128)(2,1)S(1)}, bf16[4,120,256]{2,1,0:T(8,128)(2,1)S(1)}, u32[]{:S(2)}, u32[]{:S(2)}) %collective-permute-start.17) | collective-permute-done | bytes 245792 | tf_op jit(solution)/shard_map/ppermute | solution.py:250
  48.7 2.4 %collective-permute-start.19 = (bf16[4,120,256]{2,1,0:T(8,128)(2,1)S(1)}, bf16[4,120,256]{2,1,0:T(8,128)(2,1)S(1)}, u32[]{:S(2)}, u32[]{:S(2)}) collective-permute-start(bf16[4,120,256]{2,1,0:T(8,128)(2,1)S(1)} %convolution_convert_fusion.first), channel_id=1, source_target_pairs={{0,8},{2,6},{8,16},{10,2},{16,24},{18,10},{24,28},{26,18},{28,20},... | collective-permute-start | bytes 737288 | tf_op jit(solution)/shard_map/ppermute | solution.py:273
  51.8 1.7 %collective-permute-start.18 = (bf16[4,120,256]{2,1,0:T(8,128)(2,1)S(1)}, bf16[4,120,256]{2,1,0:T(8,128)(2,1)S(1)}, u32[]{:S(2)}, u32[]{:S(2)}) collective-permute-start(bf16[4,120,256]{2,1,0:T(8,128)(2,1)S(1)} %convolution_convert_fusion.first), channel_id=1, source_target_pairs={{0,4},{2,10},{8,0},{10,18},{16,8},{18,26},{24,16},{26,30},{28,24},... | collective-permute-start | bytes 737288 | tf_op jit(solution)/shard_map/ppermute | solution.py:273
  53.9 1.1 %apply_cells.8.before = f32[2,120,128]{2,1,0:T(8,128)S(1)} custom-call(s32[2,9]{1,0:T(2,128)S(1)} %pad_add_fusion.bounds, s32[2,64]{1,0:T(2,128)S(1)} %pad_add_fusion.1.order, s32[2,64]{1,0:T(2,128)S(1)} %pad_add_fusion.2.cell, f32[2,120,128]{2,1,0:T(8,128)S(1)} %broadcast_in_dim.87.before, bf16[64,256,128]{2,1,0:T(8,128)(2,1)S(1)} %copy-done.1, ...), custom_call_target="tpu_custom_call" | custom-call | flops 125829120 | bytes 1540096 | tf_op jit(solution)/shard_map/apply_cells/pallas_call | solution.py:139
  55.0 2.6 %collective-permute-done.19.first = bf16[4,120,256]{2,1,0:T(8,128)(2,1)S(1)} collective-permute-done((bf16[4,120,256]{2,1,0:T(8,128)(2,1)S(1)}, bf16[4,120,256]{2,1,0:T(8,128)(2,1)S(1)}, u32[]{:S(2)}, u32[]{:S(2)}) %collective-permute-start.19) | collective-permute-done | bytes 245792 | tf_op jit(solution)/shard_map/ppermute | solution.py:273
  57.5 2.4 %collective-permute-done.20.second = bf16[4,120,256]{2,1,0:T(8,128)(2,1)S(1)} collective-permute-done((bf16[4,120,256]{2,1,0:T(8,128)(2,1)S(1)}, bf16[4,120,256]{2,1,0:T(8,128)(2,1)S(1)}, u32[]{:S(2)}, u32[]{:S(2)}) %collective-permute-start.20) | collective-permute-done | bytes 245792 | tf_op jit(solution)/shard_map/ppermute | solution.py:273
  60.0 1.2 %collective-permute-start.24 = (bf16[4,120,256]{2,1,0:T(8,128)(2,1)S(1)}, bf16[4,120,256]{2,1,0:T(8,128)(2,1)S(1)}, u32[]{:S(2)}, u32[]{:S(2)}) collective-permute-start(bf16[4,120,256]{2,1,0:T(8,128)(2,1)S(1)} %collective-permute-done.19.first), channel_id=1, source_target_pairs={{0,8},{2,6},{8,16},{10,2},{16,24},{18,10},{24,28},{26,18},{28,20},... | collective-permute-start | bytes 737288 | tf_op jit(solution)/shard_map/ppermute | solution.py:280
  61.1 0.9 collective-permute-start.25
  62.0 1.5 %apply_cells.9.before = f32[2,120,128]{2,1,0:T(8,128)S(1)} custom-call(s32[2,9]{1,0:T(2,128)S(1)} %pad_add_fusion.bounds, s32[2,64]{1,0:T(2,128)S(1)} %pad_add_fusion.1.order, s32[2,64]{1,0:T(2,128)S(1)} %pad_add_fusion.2.cell, f32[2,120,128]{2,1,0:T(8,128)S(1)} %apply_cells.8.before, bf16[64,256,128]{2,1,0:T(8,128)(2,1)S(1)} %copy-done.1, ...), custom_call_target="tpu_custom_call" | custom-call | flops 125829120 | bytes 1540096 | tf_op jit(solution)/shard_map/apply_cells/pallas_call | solution.py:139
  63.5 1.5 %collective-permute-done.18.second = bf16[4,120,256]{2,1,0:T(8,128)(2,1)S(1)} collective-permute-done((bf16[4,120,256]{2,1,0:T(8,128)(2,1)S(1)}, bf16[4,120,256]{2,1,0:T(8,128)(2,1)S(1)}, u32[]{:S(2)}, u32[]{:S(2)}) %collective-permute-start.18) | collective-permute-done | bytes 245792 | tf_op jit(solution)/shard_map/ppermute | solution.py:273
  65.0 1.4 %collective-permute-start.22 = (bf16[4,120,256]{2,1,0:T(8,128)(2,1)S(1)}, bf16[4,120,256]{2,1,0:T(8,128)(2,1)S(1)}, u32[]{:S(2)}, u32[]{:S(2)}) collective-permute-start(bf16[4,120,256]{2,1,0:T(8,128)(2,1)S(1)} %collective-permute-done.15.first), channel_id=1, source_target_pairs={{0,8},{2,6},{8,16},{10,2},{16,24},{18,10},{24,28},{26,18},{28,20},... | collective-permute-start | bytes 737288 | tf_op jit(solution)/shard_map/ppermute | solution.py:280
  67.0 1.1 %apply_cells.10.before = f32[2,120,128]{2,1,0:T(8,128)S(1)} custom-call(s32[2,9]{1,0:T(2,128)S(1)} %pad_add_fusion.bounds, s32[2,64]{1,0:T(2,128)S(1)} %pad_add_fusion.1.order, s32[2,64]{1,0:T(2,128)S(1)} %pad_add_fusion.2.cell, f32[2,120,128]{2,1,0:T(8,128)S(1)} %apply_cells.9.before, bf16[64,256,128]{2,1,0:T(8,128)(2,1)S(1)} %copy-done.1, ...), custom_call_target="tpu_custom_call" | custom-call | flops 125829120 | bytes 1540096 | tf_op jit(solution)/shard_map/apply_cells/pallas_call | solution.py:139
  68.8 1.5 %collective-permute-done.25.second = bf16[4,120,256]{2,1,0:T(8,128)(2,1)S(1)} collective-permute-done((bf16[4,120,256]{2,1,0:T(8,128)(2,1)S(1)}, bf16[4,120,256]{2,1,0:T(8,128)(2,1)S(1)}, u32[]{:S(2)}, u32[]{:S(2)}) %collective-permute-start.25) | collective-permute-done | bytes 245792 | tf_op jit(solution)/shard_map/ppermute | solution.py:280
  70.3 1.4 %collective-permute-start.28 = (bf16[4,120,256]{2,1,0:T(8,128)(2,1)S(1)}, bf16[4,120,256]{2,1,0:T(8,128)(2,1)S(1)}, u32[]{:S(2)}, u32[]{:S(2)}) collective-permute-start(bf16[4,120,256]{2,1,0:T(8,128)(2,1)S(1)} %collective-permute-done.24.first), channel_id=1, source_target_pairs={{0,8},{2,6},{8,16},{10,2},{16,24},{18,10},{24,28},{26,18},{28,20},... | collective-permute-start | bytes 737288 | tf_op jit(solution)/shard_map/ppermute | solution.py:280
  72.3 1.1 %apply_cells.11.before = f32[2,120,128]{2,1,0:T(8,128)S(1)} custom-call(s32[2,9]{1,0:T(2,128)S(1)} %pad_add_fusion.bounds, s32[2,64]{1,0:T(2,128)S(1)} %pad_add_fusion.1.order, s32[2,64]{1,0:T(2,128)S(1)} %pad_add_fusion.2.cell, f32[2,120,128]{2,1,0:T(8,128)S(1)} %apply_cells.10.before, bf16[64,256,128]{2,1,0:T(8,128)(2,1)S(1)} %copy-done.1, ...), custom_call_target="tpu_custom_call" | custom-call | flops 125829120 | bytes 1540096 | tf_op jit(solution)/shard_map/apply_cells/pallas_call | solution.py:139
  74.0 1.5 %collective-permute-done.23.second = bf16[4,120,256]{2,1,0:T(8,128)(2,1)S(1)} collective-permute-done((bf16[4,120,256]{2,1,0:T(8,128)(2,1)S(1)}, bf16[4,120,256]{2,1,0:T(8,128)(2,1)S(1)}, u32[]{:S(2)}, u32[]{:S(2)}) %collective-permute-start.23) | collective-permute-done | bytes 245792 | tf_op jit(solution)/shard_map/ppermute | solution.py:280
  75.4 1.5 %collective-permute-start.26 = (bf16[4,120,256]{2,1,0:T(8,128)(2,1)S(1)}, bf16[4,120,256]{2,1,0:T(8,128)(2,1)S(1)}, u32[]{:S(2)}, u32[]{:S(2)}) collective-permute-start(bf16[4,120,256]{2,1,0:T(8,128)(2,1)S(1)} %collective-permute-done.22.first), channel_id=1, source_target_pairs={{0,8},{2,6},{8,16},{10,2},{16,24},{18,10},{24,28},{26,18},{28,20},... | collective-permute-start | bytes 737288 | tf_op jit(solution)/shard_map/ppermute | solution.py:280
  77.5 1.1 %apply_cells.12.before = f32[2,120,128]{2,1,0:T(8,128)S(1)} custom-call(s32[2,9]{1,0:T(2,128)S(1)} %pad_add_fusion.bounds, s32[2,64]{1,0:T(2,128)S(1)} %pad_add_fusion.1.order, s32[2,64]{1,0:T(2,128)S(1)} %pad_add_fusion.2.cell, f32[2,120,128]{2,1,0:T(8,128)S(1)} %apply_cells.11.before, bf16[64,256,128]{2,1,0:T(8,128)(2,1)S(1)} %copy-done.1, ...), custom_call_target="tpu_custom_call" | custom-call | flops 125829120 | bytes 1540096 | tf_op jit(solution)/shard_map/apply_cells/pallas_call | solution.py:139
  79.2 1.4 %collective-permute-done.29.second = bf16[4,120,256]{2,1,0:T(8,128)(2,1)S(1)} collective-permute-done((bf16[4,120,256]{2,1,0:T(8,128)(2,1)S(1)}, bf16[4,120,256]{2,1,0:T(8,128)(2,1)S(1)}, u32[]{:S(2)}, u32[]{:S(2)}) %collective-permute-start.29) | collective-permute-done | bytes 245792 | tf_op jit(solution)/shard_map/ppermute | solution.py:280
  80.6 1.6 %collective-permute-start.30 = (bf16[4,120,256]{2,1,0:T(8,128)(2,1)S(1)}, bf16[4,120,256]{2,1,0:T(8,128)(2,1)S(1)}, u32[]{:S(2)}, u32[]{:S(2)}) collective-permute-start(bf16[4,120,256]{2,1,0:T(8,128)(2,1)S(1)} %collective-permute-done.28.first), channel_id=1, source_target_pairs={{0,8},{2,6},{8,16},{10,2},{16,24},{18,10},{24,28},{26,18},{28,20},... | collective-permute-start | bytes 737288 | tf_op jit(solution)/shard_map/ppermute | solution.py:280
  82.7 1.3 %apply_cells.13.before = f32[2,120,128]{2,1,0:T(8,128)S(1)} custom-call(s32[2,9]{1,0:T(2,128)S(1)} %pad_add_fusion.bounds, s32[2,64]{1,0:T(2,128)S(1)} %pad_add_fusion.1.order, s32[2,64]{1,0:T(2,128)S(1)} %pad_add_fusion.2.cell, f32[2,120,128]{2,1,0:T(8,128)S(1)} %apply_cells.12.before, bf16[64,256,128]{2,1,0:T(8,128)(2,1)S(1)} %copy-done.1, ...), custom_call_target="tpu_custom_call" | custom-call | flops 125829120 | bytes 1540096 | tf_op jit(solution)/shard_map/apply_cells/pallas_call | solution.py:139
  84.5 1.4 %collective-permute-done.27.second = bf16[4,120,256]{2,1,0:T(8,128)(2,1)S(1)} collective-permute-done((bf16[4,120,256]{2,1,0:T(8,128)(2,1)S(1)}, bf16[4,120,256]{2,1,0:T(8,128)(2,1)S(1)}, u32[]{:S(2)}, u32[]{:S(2)}) %collective-permute-start.27) | collective-permute-done | bytes 245792 | tf_op jit(solution)/shard_map/ppermute | solution.py:280
  85.9 1.1 %apply_cells.14 = (f32[2,120,128]{2,1,0:T(8,128)S(1)}, bf16[8,256,128]{2,1,0:T(8,128)(2,1)S(1)}, bf16[8,256,128]{2,1,0:T(8,128)(2,1)S(1)}) custom-call(s32[2,9]{1,0:T(2,128)S(1)} %pad_add_fusion.bounds, s32[2,64]{1,0:T(2,128)S(1)} %pad_add_fusion.1.order, s32[2,64]{1,0:T(2,128)S(1)} %pad_add_fusion.2.cell, f32[2,120,128]{2,1,0:T(8,128)S(1)} %apply_cells.13.before, ...), custom_call_target="tpu_custom_call" | custom-call | flops 125829120 | bytes 1540096 | tf_op jit(solution)/shard_map/apply_cells/pallas_call | solution.py:139
  87.0 2.7 %collective-permute-done.30.first = bf16[4,120,256]{2,1,0:T(8,128)(2,1)S(1)} collective-permute-done((bf16[4,120,256]{2,1,0:T(8,128)(2,1)S(1)}, bf16[4,120,256]{2,1,0:T(8,128)(2,1)S(1)}, u32[]{:S(2)}, u32[]{:S(2)}) %collective-permute-start.30) | collective-permute-done | bytes 245792 | tf_op jit(solution)/shard_map/ppermute | solution.py:280
  89.8 1.4 %apply_cells.15 = f32[2,128,120]{2,1,0:T(8,128)S(1)} custom-call(s32[2,9]{1,0:T(2,128)S(1)} %pad_add_fusion.bounds, s32[2,64]{1,0:T(2,128)S(1)} %pad_add_fusion.1.order, s32[2,64]{1,0:T(2,128)S(1)} %pad_add_fusion.2.cell, f32[2,120,128]{2,1,0:T(8,128)S(1)} %get-tuple-element.90.before, bf16[8,256,128]{2,1,0:T(8,128)(2,1)S(1)} %get-tuple-element.91.mine, ...), custom_call_target="tpu_custom_call" | custom-call | flops 125829120 | bytes 1540096 | tf_op jit(solution)/shard_map/apply_cells/pallas_call | solution.py:139
  91.4 1.1 %collective-permute-done.32 = f32[128,120]{1,0:T(8,128)S(1)} collective-permute-done((f32[128,120]{1,0:T(8,128)S(1)}, f32[128,120]{1,0:T(8,128)S(1)}, u32[]{:S(2)}, u32[]{:S(2)}) %collective-permute-start.32) | collective-permute-done | bytes 61472 | tf_op jit(solution)/shard_map/ppermute | solution.py:164
  92.5 1.6 %collective-permute-start.33 = (f32[64,120]{1,0:T(8,128)S(1)}, f32[64,120]{1,0:T(8,128)S(1)}, u32[]{:S(2)}, u32[]{:S(2)}) collective-permute-start(f32[64,120]{1,0:T(8,128)S(1)} %slice_select_fusion), channel_id=1, source_target_pairs={{0,1},{1,0},{2,3},{3,2},{4,5},{5,4},{6,7},{7,6},{8,9},{9,8},{10,11... | collective-permute-start | bytes 92168 | tf_op jit(solution)/shard_map/ppermute | solution.py:168
  94.2 2.3 %collective-permute-done.33 = f32[64,120]{1,0:T(8,128)S(1)} collective-permute-done((f32[64,120]{1,0:T(8,128)S(1)}, f32[64,120]{1,0:T(8,128)S(1)}, u32[]{:S(2)}, u32[]{:S(2)}) %collective-permute-start.33) | collective-permute-done | bytes 30752 | tf_op jit(solution)/shard_map/ppermute | solution.py:168
  (69 shorter events, 11.8 us)
Async XLA Ops:
  0.0 48.5 %copy-start = (bf16[1,256,256]{2,1,0:T(8,128)(2,1)S(1)}, bf16[1,256,256]{2,1,0:T(8,128)(2,1)}, u32[]{:S(2)}) copy-start(bf16[1,256,256]{2,1,0:T(8,128)(2,1)} %param.9) | copy-start | bytes 393220
  5.1 2.0 %collective-permute-start = (bf16[8,120,256]{2,1,0:T(8,128)(2,1)S(1)}, bf16[8,120,256]{2,1,0:T(8,128)(2,1)S(1)}, u32[]{:S(2)}, u32[]{:S(2)}) collective-permute-start(bf16[8,120,256]{2,1,0:T(8,128)(2,1)S(1)} %get-tuple-element.50), channel_id=1, source_target_pairs={{0,2},{2,0},{4,6},{6,4},{8,10},{10,8},{12,14},{14,12},{16,18},{18,... | collective-permute-start | bytes 1474568 | tf_op jit(solution)/shard_map/ppermute | solution.py:224
  5.6 1.5 %collective-permute-start.1 = (s32[64]{0:T(128)S(1)}, s32[64]{0:T(128)S(1)}, u32[]{:S(2)}, u32[]{:S(2)}) collective-permute-start(s32[64]{0:T(128)S(1)} %get-tuple-element.61), channel_id=1, source_target_pairs={{0,2},{2,0},{4,6},{6,4},{8,10},{10,8},{12,14},{14,12},{16,18},{18,... | collective-permute-start | bytes 776 | tf_op jit(solution)/shard_map/ppermute | solution.py:226
  7.1 6.1 %collective-permute-start.2 = (bf16[56,120,256]{2,1,0:T(8,128)(2,1)S(1)}, bf16[56,120,256]{2,1,0:T(8,128)(2,1)S(1)}, u32[]{:S(2)}, u32[]{:S(2)}) collective-permute-start(bf16[56,120,256]{2,1,0:T(8,128)(2,1)S(1)} %get-tuple-element.52), channel_id=1, source_target_pairs={{0,2},{2,0},{4,6},{6,4},{8,10},{10,8},{12,14},{14,12},{16,18},{18,... | collective-permute-start | bytes 10321928 | tf_op jit(solution)/shard_map/ppermute | solution.py:224
  7.9 8.6 %copy-start.1 = (bf16[64,256,128]{2,1,0:T(8,128)(2,1)S(1)}, bf16[64,256,128]{2,1,0:T(8,128)(2,1)}, u32[]{:S(2)}) copy-start(bf16[64,256,128]{2,1,0:T(8,128)(2,1)} %mine.13) | copy-start | bytes 12582916
  7.9 10.2 %collective-permute-start.6 = (bf16[4,120,256]{2,1,0:T(8,128)(2,1)S(1)}, bf16[4,120,256]{2,1,0:T(8,128)(2,1)S(1)}, u32[]{:S(2)}, u32[]{:S(2)}) collective-permute-start(bf16[4,120,256]{2,1,0:T(8,128)(2,1)S(1)} %add_convert_fusion.12), channel_id=1, source_target_pairs={{0,4},{2,10},{8,0},{10,18},{16,8},{18,26},{24,16},{26,30},{28,24},... | collective-permute-start | bytes 737288 | tf_op jit(solution)/shard_map/ppermute | solution.py:250
  10.6 7.5 %collective-permute-start.5 = (bf16[4,120,256]{2,1,0:T(8,128)(2,1)S(1)}, bf16[4,120,256]{2,1,0:T(8,128)(2,1)S(1)}, u32[]{:S(2)}, u32[]{:S(2)}) collective-permute-start(bf16[4,120,256]{2,1,0:T(8,128)(2,1)S(1)} %add_convert_fusion.13), channel_id=1, source_target_pairs={{0,8},{2,6},{8,16},{10,2},{16,24},{18,10},{24,28},{26,18},{28,20},... | collective-permute-start | bytes 737288 | tf_op jit(solution)/shard_map/ppermute | solution.py:250
  13.5 8.1 %collective-permute-start.4 = (bf16[4,120,256]{2,1,0:T(8,128)(2,1)S(1)}, bf16[4,120,256]{2,1,0:T(8,128)(2,1)S(1)}, u32[]{:S(2)}, u32[]{:S(2)}) collective-permute-start(bf16[4,120,256]{2,1,0:T(8,128)(2,1)S(1)} %add_convert_fusion.14), channel_id=1, source_target_pairs={{0,4},{2,10},{8,0},{10,18},{16,8},{18,26},{24,16},{26,30},{28,24},... | collective-permute-start | bytes 737288 | tf_op jit(solution)/shard_map/ppermute | solution.py:250
  16.4 37.4 %collective-permute-start.21 = (bf16[64,256,128]{2,1,0:T(8,128)(2,1)S(1)}, bf16[64,256,128]{2,1,0:T(8,128)(2,1)S(1)}, u32[]{:S(2)}, u32[]{:S(2)}) collective-permute-start(bf16[64,256,128]{2,1,0:T(8,128)(2,1)S(1)} %copy-done.1), channel_id=1, source_target_pairs={{0,2},{2,0},{4,6},{6,4},{8,10},{10,8},{12,14},{14,12},{16,18},{18,... | collective-permute-start | bytes 12582920 | tf_op jit(solution)/shard_map/ppermute | solution.py:230
  16.5 8.0 %collective-permute-start.3 = (bf16[4,120,256]{2,1,0:T(8,128)(2,1)S(1)}, bf16[4,120,256]{2,1,0:T(8,128)(2,1)S(1)}, u32[]{:S(2)}, u32[]{:S(2)}) collective-permute-start(bf16[4,120,256]{2,1,0:T(8,128)(2,1)S(1)} %add_convert_fusion.15), channel_id=1, source_target_pairs={{0,8},{2,6},{8,16},{10,2},{16,24},{18,10},{24,28},{26,18},{28,20},... | collective-permute-start | bytes 737288 | tf_op jit(solution)/shard_map/ppermute | solution.py:250
  18.2 9.1 %collective-permute-start.8 = (bf16[4,120,256]{2,1,0:T(8,128)(2,1)S(1)}, bf16[4,120,256]{2,1,0:T(8,128)(2,1)S(1)}, u32[]{:S(2)}, u32[]{:S(2)}) collective-permute-start(bf16[4,120,256]{2,1,0:T(8,128)(2,1)S(1)} %add_convert_fusion.10), channel_id=1, source_target_pairs={{0,4},{2,10},{8,0},{10,18},{16,8},{18,26},{24,16},{26,30},{28,24},... | collective-permute-start | bytes 737288 | tf_op jit(solution)/shard_map/ppermute | solution.py:250
  19.3 9.1 %collective-permute-start.7 = (bf16[4,120,256]{2,1,0:T(8,128)(2,1)S(1)}, bf16[4,120,256]{2,1,0:T(8,128)(2,1)S(1)}, u32[]{:S(2)}, u32[]{:S(2)}) collective-permute-start(bf16[4,120,256]{2,1,0:T(8,128)(2,1)S(1)} %add_convert_fusion.11), channel_id=1, source_target_pairs={{0,8},{2,6},{8,16},{10,2},{16,24},{18,10},{24,28},{26,18},{28,20},... | collective-permute-start | bytes 737288 | tf_op jit(solution)/shard_map/ppermute | solution.py:250
  24.6 9.3 %collective-permute-start.12 = (bf16[4,120,256]{2,1,0:T(8,128)(2,1)S(1)}, bf16[4,120,256]{2,1,0:T(8,128)(2,1)S(1)}, u32[]{:S(2)}, u32[]{:S(2)}) collective-permute-start(bf16[4,120,256]{2,1,0:T(8,128)(2,1)S(1)} %add_convert_fusion.8), channel_id=1, source_target_pairs={{0,4},{2,10},{8,0},{10,18},{16,8},{18,26},{24,16},{26,30},{28,24},... | collective-permute-start | bytes 737288 | tf_op jit(solution)/shard_map/ppermute | solution.py:250
  26.4 7.9 %collective-permute-start.11 = (bf16[4,120,256]{2,1,0:T(8,128)(2,1)S(1)}, bf16[4,120,256]{2,1,0:T(8,128)(2,1)S(1)}, u32[]{:S(2)}, u32[]{:S(2)}) collective-permute-start(bf16[4,120,256]{2,1,0:T(8,128)(2,1)S(1)} %add_convert_fusion.9), channel_id=1, source_target_pairs={{0,8},{2,6},{8,16},{10,2},{16,24},{18,10},{24,28},{26,18},{28,20},... | collective-permute-start | bytes 737288 | tf_op jit(solution)/shard_map/ppermute | solution.py:250
  28.4 10.8 %collective-permute-start.10 = (bf16[4,120,256]{2,1,0:T(8,128)(2,1)S(1)}, bf16[4,120,256]{2,1,0:T(8,128)(2,1)S(1)}, u32[]{:S(2)}, u32[]{:S(2)}) collective-permute-start(bf16[4,120,256]{2,1,0:T(8,128)(2,1)S(1)} %add_convert_fusion.6), channel_id=1, source_target_pairs={{0,4},{2,10},{8,0},{10,18},{16,8},{18,26},{24,16},{26,30},{28,24},... | collective-permute-start | bytes 737288 | tf_op jit(solution)/shard_map/ppermute | solution.py:250
  30.2 9.4 %collective-permute-start.9 = (bf16[4,120,256]{2,1,0:T(8,128)(2,1)S(1)}, bf16[4,120,256]{2,1,0:T(8,128)(2,1)S(1)}, u32[]{:S(2)}, u32[]{:S(2)}) collective-permute-start(bf16[4,120,256]{2,1,0:T(8,128)(2,1)S(1)} %add_convert_fusion.7), channel_id=1, source_target_pairs={{0,8},{2,6},{8,16},{10,2},{16,24},{18,10},{24,28},{26,18},{28,20},... | collective-permute-start | bytes 737288 | tf_op jit(solution)/shard_map/ppermute | solution.py:250
  34.4 14.1 %collective-permute-start.16 = (bf16[4,120,256]{2,1,0:T(8,128)(2,1)S(1)}, bf16[4,120,256]{2,1,0:T(8,128)(2,1)S(1)}, u32[]{:S(2)}, u32[]{:S(2)}) collective-permute-start(bf16[4,120,256]{2,1,0:T(8,128)(2,1)S(1)} %add_convert_fusion.4), channel_id=1, source_target_pairs={{0,4},{2,10},{8,0},{10,18},{16,8},{18,26},{24,16},{26,30},{28,24},... | collective-permute-start | bytes 737288 | tf_op jit(solution)/shard_map/ppermute | solution.py:250
  36.1 15.0 %collective-permute-start.14 = (bf16[4,120,256]{2,1,0:T(8,128)(2,1)S(1)}, bf16[4,120,256]{2,1,0:T(8,128)(2,1)S(1)}, u32[]{:S(2)}, u32[]{:S(2)}) collective-permute-start(bf16[4,120,256]{2,1,0:T(8,128)(2,1)S(1)} %add_convert_fusion.5), channel_id=1, source_target_pairs={{0,8},{2,6},{8,16},{10,2},{16,24},{18,10},{24,28},{26,18},{28,20},... | collective-permute-start | bytes 737288 | tf_op jit(solution)/shard_map/ppermute | solution.py:250
  39.6 8.8 %collective-permute-start.17 = (bf16[4,120,256]{2,1,0:T(8,128)(2,1)S(1)}, bf16[4,120,256]{2,1,0:T(8,128)(2,1)S(1)}, u32[]{:S(2)}, u32[]{:S(2)}) collective-permute-start(bf16[4,120,256]{2,1,0:T(8,128)(2,1)S(1)} %add_convert_fusion.1), channel_id=1, source_target_pairs={{0,8},{2,6},{8,16},{10,2},{16,24},{18,10},{24,28},{26,18},{28,20},... | collective-permute-start | bytes 737288 | tf_op jit(solution)/shard_map/ppermute | solution.py:250
  41.7 9.5 %collective-permute-start.13 = (bf16[4,120,256]{2,1,0:T(8,128)(2,1)S(1)}, bf16[4,120,256]{2,1,0:T(8,128)(2,1)S(1)}, u32[]{:S(2)}, u32[]{:S(2)}) collective-permute-start(bf16[4,120,256]{2,1,0:T(8,128)(2,1)S(1)} %add_convert_fusion.3), channel_id=1, source_target_pairs={{0,4},{2,10},{8,0},{10,18},{16,8},{18,26},{24,16},{26,30},{28,24},... | collective-permute-start | bytes 737288 | tf_op jit(solution)/shard_map/ppermute | solution.py:250
  48.7 8.8 %collective-permute-start.19 = (bf16[4,120,256]{2,1,0:T(8,128)(2,1)S(1)}, bf16[4,120,256]{2,1,0:T(8,128)(2,1)S(1)}, u32[]{:S(2)}, u32[]{:S(2)}) collective-permute-start(bf16[4,120,256]{2,1,0:T(8,128)(2,1)S(1)} %convolution_convert_fusion.first), channel_id=1, source_target_pairs={{0,8},{2,6},{8,16},{10,2},{16,24},{18,10},{24,28},{26,18},{28,20},... | collective-permute-start | bytes 737288 | tf_op jit(solution)/shard_map/ppermute | solution.py:273
  51.5 8.5 %collective-permute-start.20 = (bf16[4,120,256]{2,1,0:T(8,128)(2,1)S(1)}, bf16[4,120,256]{2,1,0:T(8,128)(2,1)S(1)}, u32[]{:S(2)}, u32[]{:S(2)}) collective-permute-start(bf16[4,120,256]{2,1,0:T(8,128)(2,1)S(1)} %convolution_convert_fusion.1.second), channel_id=1, source_target_pairs={{0,4},{2,10},{8,0},{10,18},{16,8},{18,26},{24,16},{26,30},{28,24},... | collective-permute-start | bytes 737288 | tf_op jit(solution)/shard_map/ppermute | solution.py:273
  51.8 13.2 %collective-permute-start.18 = (bf16[4,120,256]{2,1,0:T(8,128)(2,1)S(1)}, bf16[4,120,256]{2,1,0:T(8,128)(2,1)S(1)}, u32[]{:S(2)}, u32[]{:S(2)}) collective-permute-start(bf16[4,120,256]{2,1,0:T(8,128)(2,1)S(1)} %convolution_convert_fusion.first), channel_id=1, source_target_pairs={{0,4},{2,10},{8,0},{10,18},{16,8},{18,26},{24,16},{26,30},{28,24},... | collective-permute-start | bytes 737288 | tf_op jit(solution)/shard_map/ppermute | solution.py:273
  53.4 11.6 %collective-permute-start.15 = (bf16[4,120,256]{2,1,0:T(8,128)(2,1)S(1)}, bf16[4,120,256]{2,1,0:T(8,128)(2,1)S(1)}, u32[]{:S(2)}, u32[]{:S(2)}) collective-permute-start(bf16[4,120,256]{2,1,0:T(8,128)(2,1)S(1)} %convolution_convert_fusion.1.second), channel_id=1, source_target_pairs={{0,8},{2,6},{8,16},{10,2},{16,24},{18,10},{24,28},{26,18},{28,20},... | collective-permute-start | bytes 737288 | tf_op jit(solution)/shard_map/ppermute | solution.py:273
  60.0 8.8 %collective-permute-start.24 = (bf16[4,120,256]{2,1,0:T(8,128)(2,1)S(1)}, bf16[4,120,256]{2,1,0:T(8,128)(2,1)S(1)}, u32[]{:S(2)}, u32[]{:S(2)}) collective-permute-start(bf16[4,120,256]{2,1,0:T(8,128)(2,1)S(1)} %collective-permute-done.19.first), channel_id=1, source_target_pairs={{0,8},{2,6},{8,16},{10,2},{16,24},{18,10},{24,28},{26,18},{28,20},... | collective-permute-start | bytes 737288 | tf_op jit(solution)/shard_map/ppermute | solution.py:280
  61.1 9.1 %collective-permute-start.25 = (bf16[4,120,256]{2,1,0:T(8,128)(2,1)S(1)}, bf16[4,120,256]{2,1,0:T(8,128)(2,1)S(1)}, u32[]{:S(2)}, u32[]{:S(2)}) collective-permute-start(bf16[4,120,256]{2,1,0:T(8,128)(2,1)S(1)} %collective-permute-done.20.second), channel_id=1, source_target_pairs={{0,4},{2,10},{8,0},{10,18},{16,8},{18,26},{24,16},{26,30},{28,24},... | collective-permute-start | bytes 737288 | tf_op jit(solution)/shard_map/ppermute | solution.py:280
  65.0 9.0 %collective-permute-start.22 = (bf16[4,120,256]{2,1,0:T(8,128)(2,1)S(1)}, bf16[4,120,256]{2,1,0:T(8,128)(2,1)S(1)}, u32[]{:S(2)}, u32[]{:S(2)}) collective-permute-start(bf16[4,120,256]{2,1,0:T(8,128)(2,1)S(1)} %collective-permute-done.15.first), channel_id=1, source_target_pairs={{0,8},{2,6},{8,16},{10,2},{16,24},{18,10},{24,28},{26,18},{28,20},... | collective-permute-start | bytes 737288 | tf_op jit(solution)/shard_map/ppermute | solution.py:280
  66.4 9.0 %collective-permute-start.23 = (bf16[4,120,256]{2,1,0:T(8,128)(2,1)S(1)}, bf16[4,120,256]{2,1,0:T(8,128)(2,1)S(1)}, u32[]{:S(2)}, u32[]{:S(2)}) collective-permute-start(bf16[4,120,256]{2,1,0:T(8,128)(2,1)S(1)} %collective-permute-done.18.second), channel_id=1, source_target_pairs={{0,4},{2,10},{8,0},{10,18},{16,8},{18,26},{24,16},{26,30},{28,24},... | collective-permute-start | bytes 737288 | tf_op jit(solution)/shard_map/ppermute | solution.py:280
  70.3 9.0 %collective-permute-start.28 = (bf16[4,120,256]{2,1,0:T(8,128)(2,1)S(1)}, bf16[4,120,256]{2,1,0:T(8,128)(2,1)S(1)}, u32[]{:S(2)}, u32[]{:S(2)}) collective-permute-start(bf16[4,120,256]{2,1,0:T(8,128)(2,1)S(1)} %collective-permute-done.24.first), channel_id=1, source_target_pairs={{0,8},{2,6},{8,16},{10,2},{16,24},{18,10},{24,28},{26,18},{28,20},... | collective-permute-start | bytes 737288 | tf_op jit(solution)/shard_map/ppermute | solution.py:280
  71.7 9.0 %collective-permute-start.29 = (bf16[4,120,256]{2,1,0:T(8,128)(2,1)S(1)}, bf16[4,120,256]{2,1,0:T(8,128)(2,1)S(1)}, u32[]{:S(2)}, u32[]{:S(2)}) collective-permute-start(bf16[4,120,256]{2,1,0:T(8,128)(2,1)S(1)} %collective-permute-done.25.second), channel_id=1, source_target_pairs={{0,4},{2,10},{8,0},{10,18},{16,8},{18,26},{24,16},{26,30},{28,24},... | collective-permute-start | bytes 737288 | tf_op jit(solution)/shard_map/ppermute | solution.py:280
  75.4 9.1 %collective-permute-start.26 = (bf16[4,120,256]{2,1,0:T(8,128)(2,1)S(1)}, bf16[4,120,256]{2,1,0:T(8,128)(2,1)S(1)}, u32[]{:S(2)}, u32[]{:S(2)}) collective-permute-start(bf16[4,120,256]{2,1,0:T(8,128)(2,1)S(1)} %collective-permute-done.22.first), channel_id=1, source_target_pairs={{0,8},{2,6},{8,16},{10,2},{16,24},{18,10},{24,28},{26,18},{28,20},... | collective-permute-start | bytes 737288 | tf_op jit(solution)/shard_map/ppermute | solution.py:280
  76.9 9.0 %collective-permute-start.27 = (bf16[4,120,256]{2,1,0:T(8,128)(2,1)S(1)}, bf16[4,120,256]{2,1,0:T(8,128)(2,1)S(1)}, u32[]{:S(2)}, u32[]{:S(2)}) collective-permute-start(bf16[4,120,256]{2,1,0:T(8,128)(2,1)S(1)} %collective-permute-done.23.second), channel_id=1, source_target_pairs={{0,4},{2,10},{8,0},{10,18},{16,8},{18,26},{24,16},{26,30},{28,24},... | collective-permute-start | bytes 737288 | tf_op jit(solution)/shard_map/ppermute | solution.py:280
  80.6 9.1 %collective-permute-start.30 = (bf16[4,120,256]{2,1,0:T(8,128)(2,1)S(1)}, bf16[4,120,256]{2,1,0:T(8,128)(2,1)S(1)}, u32[]{:S(2)}, u32[]{:S(2)}) collective-permute-start(bf16[4,120,256]{2,1,0:T(8,128)(2,1)S(1)} %collective-permute-done.28.first), channel_id=1, source_target_pairs={{0,8},{2,6},{8,16},{10,2},{16,24},{18,10},{24,28},{26,18},{28,20},... | collective-permute-start | bytes 737288 | tf_op jit(solution)/shard_map/ppermute | solution.py:280
  82.2 7.6 %collective-permute-start.31 = (bf16[4,120,256]{2,1,0:T(8,128)(2,1)S(1)}, bf16[4,120,256]{2,1,0:T(8,128)(2,1)S(1)}, u32[]{:S(2)}, u32[]{:S(2)}) collective-permute-start(bf16[4,120,256]{2,1,0:T(8,128)(2,1)S(1)} %collective-permute-done.29.second), channel_id=1, source_target_pairs={{0,4},{2,10},{8,0},{10,18},{16,8},{18,26},{24,16},{26,30},{28,24},... | collective-permute-start | bytes 737288 | tf_op jit(solution)/shard_map/ppermute | solution.py:280
  91.2 1.3 %collective-permute-start.32 = (f32[128,120]{1,0:T(8,128)S(1)}, f32[128,120]{1,0:T(8,128)S(1)}, u32[]{:S(2)}, u32[]{:S(2)}) collective-permute-start(f32[128,120]{1,0:T(8,128)S(1)} %slice_bitcast_fusion), channel_id=1, source_target_pairs={{0,2},{2,0},{4,6},{6,4},{8,10},{10,8},{12,14},{14,12},{16,18},{18,... | collective-permute-start | bytes 184328 | tf_op jit(solution)/shard_map/ppermute | solution.py:164
  92.5 4.0 %collective-permute-start.33 = (f32[64,120]{1,0:T(8,128)S(1)}, f32[64,120]{1,0:T(8,128)S(1)}, u32[]{:S(2)}, u32[]{:S(2)}) collective-permute-start(f32[64,120]{1,0:T(8,128)S(1)} %slice_select_fusion), channel_id=1, source_target_pairs={{0,1},{1,0},{2,3},{3,2},{4,5},{5,4},{6,7},{7,6},{8,9},{9,8},{10,11... | collective-permute-start | bytes 92168 | tf_op jit(solution)/shard_map/ppermute | solution.py:168
